TPU v7x, 32 devices: a whole 2x2x4 slice. The times are simulated.
32 devices in a mesh: vv: 4 (over y, core), oo: 8 (over z, x).
Axes of the slice: x: 2, y: 2, z: 4, core: 2. Of those that a mesh axis runs over, the one named last changes fastest.
Arguments:
- integrals: bfloat16 [1024, 256], P('vv', 'oo'), may hold values from -0.375 to 0.375
- amplitudes: bfloat16 [256, 4096], P('vv', 'oo'), may hold values from -6 to 6
- occ_energy: float32 [64], replicated, may hold values from -2 to -0.3
- vir_energy: float32 [32], replicated, may hold values from 0.1 to 3
Outputs:
- update: bfloat16 [1024, 4096], P('vv', 'oo')
All inputs are finite; a program needn't handle non-finite values.
Results may differ from a plain program's by a relative error of at most 0.0085.
Values may be sent and summed in bfloat16 or wider, within the bound.
No kernel may reach another device: no remote copies, remote signals or barrier semaphores. Data moves between devices by JAX's collectives and lax.ppermute only.
A program may use at most 64 MiB of HBM per device.

v0:
```python
import jax
import jax.numpy as jnp
from jax import lax
from jax.sharding import PartitionSpec as P


def on_device(integrals, amplitudes, occ_energy, vir_energy):
    vir_all = vir_energy.shape[0]
    occ_all = occ_energy.shape[0]
    vir_local = vir_all // lax.axis_size("vv")
    occ_local = occ_all // lax.axis_size("oo")
    row_count = vir_local * vir_all
    col_count = occ_local * occ_all
    amp_full = lax.all_gather(amplitudes, "vv", axis=0, tiled=True)
    int_full = lax.all_gather(integrals, "oo", axis=1, tiled=True)
    summed = jnp.dot(int_full, amp_full, preferred_element_type=jnp.float32)
    ladder = summed.astype(jnp.bfloat16).reshape(vir_local, vir_all, occ_local, occ_all)
    moved = lax.all_to_all(
        lax.all_to_all(ladder, "vv", split_axis=1, concat_axis=0, tiled=True),
        "oo",
        split_axis=3,
        concat_axis=2,
        tiled=True,
    )
    mirrored = jnp.transpose(moved, (1, 0, 3, 2))
    vir_mine = lax.dynamic_slice_in_dim(vir_energy, lax.axis_index("vv") * vir_local, vir_local, 0)
    occ_mine = lax.dynamic_slice_in_dim(occ_energy, lax.axis_index("oo") * occ_local, occ_local, 0)
    denom = (
        occ_mine[None, None, :, None]
        + occ_energy[None, None, None, :]
        - vir_mine[:, None, None, None]
        - vir_energy[None, :, None, None]
    )
    total = ladder.astype(jnp.float32) + mirrored.astype(jnp.float32)
    return (total / denom).astype(jnp.bfloat16).reshape(row_count, col_count)


def solution(mesh):
    placed = (P("vv", "oo"), P("vv", "oo"), P(), P())
    return jax.shard_map(
        on_device, mesh=mesh, in_specs=placed, out_specs=P("vv", "oo"), check_vma=False
    )
```

profile of v0, /device:TPU:0, one launch (start us, length us, event | category | flops | bytes accessed | tf_op | source)
XLA Modules:
  0.0 71.6 jit_solution(15824396406727908297)
XLA Ops:
  0.0 32.5 %all_gather.6 = bf16[256,256]{0,1:T(8,128)(2,1)S(1)} all-gather(bf16[256,32]{0,1:T(8,128)(2,1)} %param.4), channel_id=1, replica_groups=mesh['vv'=4,'oo'=8] {'oo'}, dimensions={1}, use_global_device_ids=true | all-gather | bytes 147456 | tf_op jit(solution)/shard_map/all_gather | solution.py:15
  32.5 6.0 %all_gather.7 = bf16[256,512]{1,0:T(8,128)(2,1)S(1)} all-gather(bf16[64,512]{1,0:T(8,128)(2,1)} %param.5), channel_id=1, replica_groups=mesh['vv'=4,'oo'=8] {'vv'}, dimensions={0}, use_global_device_ids=true | all-gather | bytes 327680 | tf_op jit(solution)/shard_map/all_gather | solution.py:14
  38.5 0.2 convolution_convert_fusion
  38.8 0.3 reshape.50
  39.0 0.1 copy.38
  39.2 0.4 reshape.54
  39.6 8.6 %all_to_all.27 = bf16[4,2,16384]{2,1,0:T(2,128)(2,1)S(1)} all-to-all(bf16[4,2,16384]{2,1,0:T(2,128)(2,1)S(1)} %reshape.54), channel_id=1, replica_groups=mesh['vv'=4,'oo'=8] {'vv'}, dimensions={0} | all-to-all | bytes 524288 | tf_op jit(solution)/shard_map/all_to_all | solution.py:19
  48.2 0.3 reshape.55
  48.5 0.0 copy-start
  48.6 0.1 copy.30
  48.7 1.7 %copy.31 = bf16[32,8,8,64]{0,2,1,3:T(8,128)(2,1)S(1)} copy(bf16[32,8,8,64]{3,2,1,0:T(8,128)(2,1)S(1)} %bitcast.29) | data formatting | bytes 524288 | tf_op jit(solution)/shard_map/all_to_all | solution.py:19
  50.4 1.7 %reshape.56 = bf16[8,2,8192]{2,1,0:T(2,128)(2,1)} reshape(bf16[64,8,8,32]{3,2,1,0:T(8,128)(2,1)S(1)} %bitcast.28) | data formatting | bytes 524288
  52.1 5.5 %all-to-all-start.1 = ((bf16[8,2,8192]{2,1,0:T(2,128)(2,1)}), bf16[8,2,8192]{2,1,0:T(2,128)(2,1)S(1)}, u32[]{:S(2)}, u32[]{:S(2)}) async-start(bf16[8,2,8192]{2,1,0:T(2,128)(2,1)} %reshape.56), calls=%async_computation.1 | async-start | bytes 524288 | tf_op jit(solution)/shard_map/all_to_all | solution.py:18
  57.5 0.1 dynamic_slice.7
  57.6 0.1 dynamic_slice.6
  57.7 0.1 broadcast_add_fusion
  57.8 0.1 broadcast_subtract_fusion
  57.9 8.2 %all-to-all-done.1 = bf16[8,2,8192]{2,1,0:T(2,128)(2,1)S(1)} async-done(((bf16[8,2,8192]{2,1,0:T(2,128)(2,1)}), bf16[8,2,8192]{2,1,0:T(2,128)(2,1)S(1)}, u32[]{:S(2)}, u32[]{:S(2)}) %all-to-all-start.1) | async-done | bytes 262176 | tf_op jit(solution)/shard_map/all_to_all | solution.py:18
  66.1 0.5 reshape.57
  66.6 0.6 convert_bitcast_fusion
  67.2 0.3 copy.33
  67.5 1.6 %copy.34 = f32[32,8,64,8]{2,3,0,1:T(8,128)} copy(f32[32,8,64,8]{0,3,2,1:T(8,128)S(1)} %bitcast.26) | data formatting | bytes 1048576 | tf_op jit(solution)/shard_map/convert_element_type | solution.py:34
  69.1 1.5 %fusion.1 = bf16[8,32,8,64]{3,2,1,0:T(8,128)(2,1)S(1)} fusion(f32[32,8,64,8]{2,3,0,1:T(8,128)} %copy.34, bf16[8,32,8,64]{3,2,1,0:T(8,128)(2,1)S(1)} %reshape.50, f32[32]{0:T(128)S(1)} %copy-done, f32[8,8,64]{2,1,0:T(8,128)S(1)} %broadcast_subtract_fusion), kind=kLoop, calls=%fused_computation.4 | loop fusion | flops 655360 | bytes 1065088 | tf_op jit(solution)/shard_map/convert_element_type | solution.py:35
  70.6 1.0 %reshape.51 = bf16[256,512]{1,0:T(8,128)(2,1)} reshape(bf16[8,32,8,64]{3,2,1,0:T(8,128)(2,1)S(1)} %fusion.1) | data formatting | bytes 524288 | tf_op jit(solution)/shard_map/reshape | solution.py:35
  (3 shorter events, 0.0 us)
Async XLA Ops:
  48.5 9.0 %copy-start = (f32[32]{0:T(128)S(1)}, f32[32]{0:T(128)}, u32[]{:S(2)}) copy-start(f32[32]{0:T(128)} %param.7) | copy-start | bytes 388
  48.6 9.1 %copy-start.1 = (f32[64]{0:T(128)S(1)}, f32[64]{0:T(128)}, u32[]{:S(2)}) copy-start(f32[64]{0:T(128)} %param.6) | copy-start | bytes 772
  52.1 14.0 %all-to-all-start.1 = ((bf16[8,2,8192]{2,1,0:T(2,128)(2,1)}), bf16[8,2,8192]{2,1,0:T(2,128)(2,1)S(1)}, u32[]{:S(2)}, u32[]{:S(2)}) async-start(bf16[8,2,8192]{2,1,0:T(2,128)(2,1)} %reshape.56), calls=%async_computation.1 | async-start | bytes 524288 | tf_op jit(solution)/shard_map/all_to_all | solution.py:18
where the time goes:
time: 71.9 us; the launch traced here: 71.6 us
  blocking collectives  47.1 us (66%)
  local copies, waits for them, and re-layouts  8.24 us (11%)
  waiting for transfers between devices  8.24 us (11%)
  starting transfers between devices  5.46 us (8%)
  other arithmetic  2.24 us (3%)
    all_gather x1, blocking collectives, on_device(): int_full = lax.all_gather(integrals, 'oo', axis=1, tiled=True)  32.5 us
    all_to_all x1, blocking collectives, on_device(): lax.all_to_all(ladder, 'vv', split_axis=1, concat_axis=0, tiled=True)  8.59 us
    all_to_all x1, waiting for transfers between devices, on_device(): lax.all_to_all(lax.all_to_all(ladder, 'vv', split_axis=1, concat_axis=0,...  8.24 us
    all_gather x1, blocking collectives, on_device(): amp_full = lax.all_gather(amplitudes, 'vv', axis=0, tiled=True)  5.98 us
    all_to_all x1, starting transfers between devices, on_device(): lax.all_to_all(lax.all_to_all(ladder, 'vv', split_axis=1, concat_axis=0,...  5.46 us
    unnamed x8, local copies, waits for them, and re-layouts  2.91 us
    convert_element_type x2, local copies, waits for them, and re-layouts, on_device(): total = ladder.astype(jnp.float32) + mirrored.astype(jnp.float32)  1.89 us
    all_to_all x2, local copies, waits for them, and re-layouts, on_device(): lax.all_to_all(ladder, 'vv', split_axis=1, concat_axis=0, tiled=True)  1.84 us
  transfers between devices with their start and end apart: 1, of which 1 were waited for; matrix products, arithmetic and copies ran while one was open for 0% of the time, Pallas kernels for 0%

commit v1 on v0

v1 whole, which is shorter than its diff:
```python
import functools

import jax
import jax.numpy as jnp
from jax import lax
from jax.experimental import pallas as pl
from jax.experimental.pallas import tpu as pltpu
from jax.sharding import PartitionSpec as P

LANES = 128
F32 = jnp.float32
BF16 = jnp.bfloat16
VMEM = pltpu.MemorySpace.VMEM


def one_hot(rows, source):
    n = source.shape[1]
    pick = lax.broadcasted_iota(jnp.int32, (rows, n), 0) == source
    return jnp.where(pick, 1.0, 0.0).astype(BF16)


def columns(n):
    return lax.broadcasted_iota(jnp.int32, (1, n), 1)


def pack_kernel(occ_all, t_ref, v_ref, out_ref):
    parts, rows, lanes = out_ref.shape
    depth, cols = t_ref.shape
    own = cols // occ_all
    square = own * own
    col = columns(cols)
    source = (col % square // own) * occ_all + (col // square) * own + col % own
    moved = jnp.dot(t_ref[...], one_hot(cols, source), preferred_element_type=F32)
    fold = lanes // square
    high = depth // fold
    for part in range(parts):
        piece = [
            moved[h * high : (h + 1) * high, part * square : (part + 1) * square]
            for h in range(fold)
        ]
        out_ref[part, :high, :] = jnp.concatenate(piece, axis=1).astype(BF16)
    deep = v_ref.shape[0]
    for chunk in range((rows - high) // deep):
        block = v_ref[:, chunk * lanes : (chunk + 1) * lanes]
        for part in range(parts):
            out_ref[part, high + chunk * deep : high + (chunk + 1) * deep, :] = block


def integral_columns(got_ref, high, deep):
    parts, rows, lanes = got_ref.shape
    return jnp.concatenate(
        [
            got_ref[:, high + c * deep : high + (c + 1) * deep, :].reshape(parts * deep, lanes)
            for c in range((rows - high) // deep)
        ],
        axis=1,
    )


def split_kernel(sizes, got_ref, send_ref, keep_ref):
    vir_parts, vir_own, occ_own, high, deep, kept = sizes
    parts, _, lanes = got_ref.shape
    square = occ_own * occ_own
    fold = lanes // square
    cols = parts * square
    occ_all = parts * occ_own
    packed = got_ref[:, :high, :].astype(F32)
    halves = [
        jnp.concatenate(
            [packed[part, :, h * square : (h + 1) * square] for part in range(parts)], axis=1
        )
        for h in range(fold)
    ]
    amps = jnp.concatenate(halves, axis=0).astype(BF16)
    col = columns(cols)
    source = (col % occ_all // occ_own) * square + (col % occ_own) * occ_own + col // occ_all
    amps = jnp.dot(amps, one_hot(cols, source), preferred_element_type=F32).astype(BF16)
    depth = amps.shape[0]
    chunks = cols // lanes
    for c in range(chunks):
        block = amps[:, c * lanes : (c + 1) * lanes]
        send_ref[c * depth : (c + 1) * depth, :] = block
        keep_ref[c * depth : (c + 1) * depth, :] = block
    me = lax.axis_index("vv")
    ints = integral_columns(got_ref, high, deep)
    total, rows = ints.shape
    area = vir_own * vir_own
    col = columns(rows)
    owner = jnp.bitwise_xor(col // area, me)
    source = (col % vir_own) * (vir_parts * vir_own) + owner * vir_own + col % area // vir_own
    ints = jnp.dot(ints, one_hot(rows, source), preferred_element_type=F32).astype(BF16)
    base = chunks * depth
    for c in range(kept):
        keep_ref[base + c * total : base + (c + 1) * total, :] = ints[:, c * lanes : (c + 1) * lanes]
    first = rows // lanes - (send_ref.shape[0] - base) // total
    for c in range(first, rows // lanes):
        at = base + (c - first) * total
        send_ref[at : at + total, :] = ints[:, c * lanes : (c + 1) * lanes]


def direct_kernel(sizes, *refs):
    vir_parts, vir_own, occ_own, high, deep, width = sizes
    got_ref, occ_ref, row_ref, *amp_refs, lad_ref, den_ref, sel_ref, all_ref = refs
    me = lax.axis_index("vv")
    depth = amp_refs[0].shape[0]
    for rel, ref in enumerate(amp_refs):
        at = pl.multiple_of(jnp.bitwise_xor(me, rel) * depth, depth)
        all_ref[pl.ds(at, depth), :] = ref[...]
    ints = integral_columns(got_ref, high, deep)
    lad_ref[...] = lax.dot_general(
        ints, all_ref[...], (((0,), (0,)), ((), ())), preferred_element_type=F32
    ).astype(BF16)
    den_ref[...] = occ_ref[...] - row_ref[:, :1] - row_ref[:, 1:]
    rows, n = sel_ref.shape
    area = vir_own * vir_own
    vir_all = vir_parts * vir_own
    row = lax.broadcasted_iota(jnp.int32, (rows, 1), 0)
    rel = jnp.bitwise_xor(row % vir_all // vir_own, me)
    source = rel * width + (rel % (width // area)) * area + row // vir_all * vir_own + row % vir_own
    pick = lax.broadcasted_iota(jnp.int32, (rows, n), 1) == source
    sel_ref[...] = jnp.where(pick, 1.0, 0.0).astype(BF16)


def mirror_kernel(sizes, *refs):
    depth, total, width = sizes
    lad_ref, den_ref, sel_ref, *got_refs, out_ref, all_ref = refs
    me = lax.axis_index("vv")
    rows, cols = out_ref.shape
    chunks = cols // LANES
    for rel, ref in enumerate(got_refs):
        at = pl.multiple_of(jnp.bitwise_xor(me, rel) * depth, depth)
        for c in range(chunks):
            all_ref[pl.ds(at, depth), c * LANES : (c + 1) * LANES] = ref[c * depth : (c + 1) * depth, :]
    base = chunks * depth
    ints = jnp.concatenate(
        [
            ref[base + c * total : base + (c + 1) * total, :]
            for ref in got_refs
            for c in range(width // LANES)
        ],
        axis=1,
    )
    rows_mirrored = lax.dot_general(
        sel_ref[...], ints, (((1,), (1,)), ((), ())), preferred_element_type=F32
    ).astype(BF16)
    mirrored = jnp.dot(rows_mirrored, all_ref[...], preferred_element_type=F32).astype(BF16)
    total_sum = lad_ref[...].astype(F32) + mirrored.astype(F32)
    out_ref[...] = (total_sum / den_ref[...]).astype(BF16)


def call(kernel, outs, args, scratch=(), flops=0):
    outs = tuple(outs)
    moved = sum(x.size * x.dtype.itemsize for x in (*args, *outs))
    result = pl.pallas_call(
        kernel,
        out_shape=outs,
        in_specs=[pl.BlockSpec(memory_space=VMEM)] * len(args),
        out_specs=tuple(pl.BlockSpec(memory_space=VMEM) for _ in outs),
        scratch_shapes=list(scratch),
        cost_estimate=pl.CostEstimate(flops=flops, bytes_accessed=moved, transcendentals=0),
    )(*args)
    return result


def on_device(integrals, amplitudes, occ_energy, vir_energy):
    vir_parts, occ_parts = lax.axis_size("vv"), lax.axis_size("oo")
    vir_all, occ_all = vir_energy.shape[0], occ_energy.shape[0]
    vir_own, occ_own = vir_all // vir_parts, occ_all // occ_parts
    depth, cols = amplitudes.shape
    rows, deep = integrals.shape
    total = deep * occ_parts
    high = depth * occ_own * occ_own // LANES
    area = vir_own * vir_own

    def swap(x, step):
        return lax.ppermute(x, "vv", [(k, k ^ step) for k in range(vir_parts)])

    shape = (occ_parts, high + rows // LANES * deep, LANES)
    (packed,) = call(
        functools.partial(pack_kernel, occ_all),
        [jax.ShapeDtypeStruct(shape, BF16)],
        (amplitudes, integrals.T),
        flops=2 * depth * cols * cols,
    )
    got = lax.all_to_all(packed, "oo", 0, 0, tiled=True)

    step = vir_parts // 2
    lanes = rows
    halves = step * area % LANES == 0
    send_lanes = lanes // 2 if halves else lanes
    amp_rows = cols // LANES * depth
    send, keep = call(
        functools.partial(
            split_kernel, (vir_parts, vir_own, occ_own, high, deep, send_lanes // LANES)
        ),
        [jax.ShapeDtypeStruct((amp_rows + send_lanes // LANES * total, LANES), BF16)] * 2,
        (got,),
        flops=2 * depth * cols * cols + 2 * total * rows * rows,
    )
    held = {0: (send, keep)}
    direct = {0: amplitudes}
    lanes = send_lanes
    while step:
        direct |= {k ^ step: swap(x, step) for k, x in direct.items()}
        arrived = {k: x for k, (_, x) in held.items()}
        arrived |= {k ^ step: swap(x, step) for k, (x, _) in held.items()}
        step //= 2
        if step and step * area % LANES == 0:
            lanes //= 2
            cut = amp_rows + lanes // LANES * total
            held = {
                k: (jnp.concatenate([x[:amp_rows], x[cut:]]), x[:cut]) for k, x in arrived.items()
            }
        else:
            held = {k: (x, x) for k, x in arrived.items()}
    order = range(vir_parts)

    vir_mine = lax.dynamic_slice_in_dim(vir_energy, lax.axis_index("vv") * vir_own, vir_own, 0)
    occ_mine = lax.dynamic_slice_in_dim(occ_energy, lax.axis_index("oo") * occ_own, occ_own, 0)
    occ_pair = (occ_mine[:, None] + occ_energy[None, :]).reshape(1, cols)
    vir_pair = jnp.stack(
        [
            jnp.broadcast_to(vir_mine[:, None], (vir_own, vir_all)),
            jnp.broadcast_to(vir_energy[None, :], (vir_own, vir_all)),
        ],
        axis=-1,
    ).reshape(rows, 2)
    ladder, denom, select = call(
        functools.partial(direct_kernel, (vir_parts, vir_own, occ_own, high, deep, lanes)),
        [
            jax.ShapeDtypeStruct((rows, cols), BF16),
            jax.ShapeDtypeStruct((rows, cols), F32),
            jax.ShapeDtypeStruct((rows, vir_parts * lanes), BF16),
        ],
        (got, occ_pair, vir_pair, *(direct[k] for k in order)),
        scratch=[pltpu.VMEM((total, cols), BF16)],
        flops=2 * rows * total * cols,
    )
    (update,) = call(
        functools.partial(mirror_kernel, (depth, total, lanes)),
        [jax.ShapeDtypeStruct((rows, cols), BF16)],
        (ladder, denom, select, *(arrived[k] for k in order)),
        scratch=[pltpu.VMEM((total, cols), BF16)],
        flops=2 * rows * total * cols * 2,
    )
    return update


def solution(mesh):
    placed = (P("vv", "oo"), P("vv", "oo"), P(), P())
    return jax.shard_map(
        on_device, mesh=mesh, in_specs=placed, out_specs=P("vv", "oo"), check_vma=False
    )
```

time: 71.9 us -> 33.8 us (0.47)
  blocking collectives: 47.1 us -> 15.3 us
  Pallas kernels: 0 us -> 8.66 us
  waiting for transfers between devices: 8.24 us -> 1.92 us
  local copies, waits for them, and re-layouts: 8.24 us -> 4.3 us
  starting transfers between devices: 5.46 us -> 3.05 us
  other arithmetic: 2.24 us -> 0.08 us
    all_gather x2 -> x0, blocking collectives: 38.5 us -> none  [the longest x1 32.5 us: on_device(): int_full = lax.all_gather(integrals, 'oo', axis=1, tiled=True)]
    pallas_call x0 -> x4, Pallas kernels: none -> 8.66 us  [call(): pl.pallas_call(kernel, out_shape=outs, in_specs=[pl.BlockSpec(memory_spac...]
    all_to_all x1 -> x0, waiting for transfers between devices: 8.24 us -> none  [on_device(): lax.all_to_all(lax.all_to_all(ladder, 'vv', split_axis=1, concat_axis=0,...]
    all_to_all x1, blocking collectives: 8.59 us -> 15.3 us  [on_device(): got = lax.all_to_all(packed, 'oo', 0, 0, tiled=True)]
    all_to_all x1 -> x0, starting transfers between devices: 5.46 us -> none  [on_device(): lax.all_to_all(lax.all_to_all(ladder, 'vv', split_axis=1, concat_axis=0,...]
    ppermute x0 -> x6, starting transfers between devices: none -> 3.05 us  [swap(): return lax.ppermute(x, 'vv', [(k, k ^ step) for k in range(vir_parts)])]
    convert_element_type x2 -> x0, other arithmetic: 2.09 us -> none  [the longest x1 1.48 us: on_device(): return (total / denom).astype(jnp.bfloat16).reshape(row_count, col_count)]
    ppermute x0 -> x6, waiting for transfers between devices: none -> 1.92 us  [swap(): return lax.ppermute(x, 'vv', [(k, k ^ step) for k in range(vir_parts)])]
  transfers between devices with their start and end apart: 1 -> 6, of which waited for: 1 -> 1; matrix products, arithmetic and copies ran while one was open for 0% -> 5% of each run, Pallas kernels for 0% -> 7%
where the time goes in v1:
time: 33.8 us; the launch traced here: 33.4 us
  blocking collectives  15.3 us (45%)
  Pallas kernels  8.66 us (26%)
  local copies, waits for them, and re-layouts  4.3 us (13%)
  starting transfers between devices  3.05 us (9%)
  waiting for transfers between devices  1.92 us (6%)
    all_to_all x1, blocking collectives, on_device(): got = lax.all_to_all(packed, 'oo', 0, 0, tiled=True)  15.3 us
    pallas_call x4, Pallas kernels, call(): pl.pallas_call(kernel, out_shape=outs, in_specs=[pl.BlockSpec(memory_spac...  8.66 us
    ppermute x6, starting transfers between devices, swap(): return lax.ppermute(x, 'vv', [(k, k ^ step) for k in range(vir_parts)])  3.05 us
    unnamed x18, local copies, waits for them, and re-layouts  2.64 us
    ppermute x6, waiting for transfers between devices, swap(): return lax.ppermute(x, 'vv', [(k, k ^ step) for k in range(vir_parts)])  1.92 us
    another operation x3, local copies, waits for them, and re-layouts, on_device(): jnp.stack([jnp.broadcast_to(vir_mine[:, None], (vir_own, vir_all)), jnp.b...  0.86 us
  transfers between devices with their start and end apart: 6, of which 1 were waited for; matrix products, arithmetic and copies ran while one was open for 5% of the time, Pallas kernels for 7%

profile of v1, /device:TPU:0, one launch (start us, length us, event | category | flops | bytes accessed | tf_op | source)
XLA Modules:
  0.0 33.4 jit_solution(6336684273187545497)
XLA Ops:
  0.0 1.8 %shard_map.46 = bf16[8,96,128]{2,1,0:T(8,128)(2,1)} custom-call(bf16[64,512]{1,0:T(8,128)(2,1)} %refs_3_.1, bf16[32,256]{1,0:T(8,128)(2,1)} %bitcast.3), custom_call_target="tpu_custom_call" | custom-call | flops 33554432 | bytes 278528 | tf_op jit(solution)/shard_map/pallas_call | solution.py:154
  1.8 15.3 %all_to_all.5.refs_0_.got_ref = bf16[8,96,128]{2,1,0:T(8,128)(2,1)} all-to-all(bf16[8,96,128]{2,1,0:T(8,128)(2,1)} %shard_map.46), channel_id=1, replica_groups=mesh['vv'=4,'oo'=8] {'oo'}, dimensions={0} | all-to-all | bytes 393216 | tf_op jit(solution)/shard_map/all_to_all | solution.py:185
  17.2 2.0 %shard_map.48 = (bf16[512,128]{1,0:T(8,128)(2,1)}, bf16[512,128]{1,0:T(8,128)(2,1)}) custom-call(bf16[8,96,128]{2,1,0:T(8,128)(2,1)} %all_to_all.5.refs_0_.got_ref), custom_call_target="tpu_custom_call" | custom-call | flops 67108864 | bytes 458752 | tf_op jit(solution)/shard_map/pallas_call | solution.py:154
  19.2 1.5 %collective-permute-start.4 = (bf16[512,128]{1,0:T(8,128)(2,1)}, bf16[512,128]{1,0:T(8,128)(2,1)S(1)}, u32[]{:S(2)}, u32[]{:S(2)}) collective-permute-start(bf16[512,128]{1,0:T(8,128)(2,1)} %get-tuple-element.14), channel_id=1, source_target_pairs={{0,16},{8,24},{16,0},{24,8},{1,17},{9,25},{17,1},{25,9},{2,18},{10... | collective-permute-start | bytes 393224 | tf_op jit(solution)/shard_map/ppermute | solution.py:176
  20.7 0.5 %collective-permute-start.1 = (bf16[64,512]{1,0:T(8,128)(2,1)S(1)}, bf16[64,512]{1,0:T(8,128)(2,1)S(1)}, u32[]{:S(2)}, u32[]{:S(2)}) collective-permute-start(bf16[64,512]{1,0:T(8,128)(2,1)S(1)} %copy-done), channel_id=1, source_target_pairs={{0,16},{8,24},{16,0},{24,8},{1,17},{9,25},{17,1},{25,9},{2,18},{10... | collective-permute-start | bytes 196616 | tf_op jit(solution)/shard_map/ppermute | solution.py:176
  21.2 0.7 %copy-done.7 = f32[64]{0:T(128)S(1)} copy-done((f32[64]{0:T(128)S(1)}, f32[64]{0:T(128)}, u32[]{:S(2)}) %copy-start.7) | copy-done | bytes 280
  21.9 0.1 dynamic_slice.6
  21.9 0.5 %collective-permute-start.3 = (bf16[512,128]{1,0:T(8,128)(2,1)}, bf16[512,128]{1,0:T(8,128)(2,1)S(1)}, u32[]{:S(2)}, u32[]{:S(2)}) collective-permute-start(bf16[512,128]{1,0:T(8,128)(2,1)} %get-tuple-element.13.refs_3_), channel_id=1, source_target_pairs={{0,8},{8,0},{16,24},{24,16},{1,9},{9,1},{17,25},{25,17},{2,10},{10... | collective-permute-start | bytes 393224 | tf_op jit(solution)/shard_map/ppermute | solution.py:176
  22.5 1.9 %collective-permute-done.4.refs_5_ = bf16[512,128]{1,0:T(8,128)(2,1)S(1)} collective-permute-done((bf16[512,128]{1,0:T(8,128)(2,1)}, bf16[512,128]{1,0:T(8,128)(2,1)S(1)}, u32[]{:S(2)}, u32[]{:S(2)}) %collective-permute-start.4) | collective-permute-done | bytes 131104 | tf_op jit(solution)/shard_map/ppermute | solution.py:176
  24.4 0.0 collective-permute-start.5
  24.4 0.1 broadcast_add_fusion
  24.4 0.7 %copy-done.8 = f32[32]{0:T(128)S(1)} copy-done((f32[32]{0:T(128)S(1)}, f32[32]{0:T(128)}, u32[]{:S(2)}) %copy-start.8) | copy-done | bytes 152
  25.1 0.1 dynamic_slice.7
  25.2 0.0 collective-permute-done.1.refs_5_
  25.2 0.5 %collective-permute-start.2 = (bf16[64,512]{1,0:T(8,128)(2,1)S(1)}, bf16[64,512]{1,0:T(8,128)(2,1)S(1)}, u32[]{:S(2)}, u32[]{:S(2)}) collective-permute-start(bf16[64,512]{1,0:T(8,128)(2,1)S(1)} %collective-permute-done.1.refs_5_), channel_id=1, source_target_pairs={{0,8},{8,0},{16,24},{24,16},{1,9},{9,1},{17,25},{25,17},{2,10},{10... | collective-permute-start | bytes 196616 | tf_op jit(solution)/shard_map/ppermute | solution.py:176
  25.7 0.1 stack_broadcast_in_dim.4
  25.8 0.8 %copy.5 = f32[8,32,2]{2,1,0:T(8,128)} copy(f32[8,32,2]{1,0,2:T(8,128)S(1)} %pad_maximum_fusion) | data formatting | bytes 4096 | tf_op jit(solution)/shard_map/stack | solution.py:221
  26.6 0.6 %add.33.refs_1_ = f32[1,512]{1,0:T(1,128)} reshape(f32[8,64]{1,0:T(8,128)S(1)} %broadcast_add_fusion) | data formatting | bytes 4096 | tf_op jit(solution)/shard_map/add | solution.py:220
  27.2 0.6 %copy-done.5 = bf16[64,512]{1,0:T(8,128)(2,1)} copy-done((bf16[64,512]{1,0:T(8,128)(2,1)}, bf16[64,512]{1,0:T(8,128)(2,1)S(1)}, u32[]{:S(2)}) %copy-start.5) | copy-done | bytes 65560
  27.8 0.0 copy-done.6
  27.9 2.3 %shard_map.47 = (bf16[256,512]{1,0:T(8,128)(2,1)}, f32[256,512]{1,0:T(8,128)}, bf16[256,512]{1,0:T(8,128)(2,1)}) custom-call(bf16[8,96,128]{2,1,0:T(8,128)(2,1)} %all_to_all.5.refs_0_.got_ref, f32[1,512]{1,0:T(1,128)} %add.33.refs_1_, f32[256,2]{1,0:T(8,128)} %bitcast.2, bf16[64,512]{1,0:T(8,128)(2,1)} %refs_3_.1, bf16[64,512]{1,0:T(8,128)(2,1)} %copy-done.5, ...), custom_call_target="tpu_custom_call" | custom-call | flops 67108864 | bytes 1511424 | tf_op jit(solution)/shard_map/pallas_call | solution.py:154
  30.2 0.6 %copy-done.2 = bf16[512,128]{1,0:T(8,128)(2,1)} copy-done((bf16[512,128]{1,0:T(8,128)(2,1)}, bf16[512,128]{1,0:T(8,128)(2,1)S(1)}, u32[]{:S(2)}) %copy-start.2) | copy-done | bytes 131096
  30.8 0.1 copy-done.3
  30.9 2.5 %shard_map.49 = bf16[256,512]{1,0:T(8,128)(2,1)} custom-call(bf16[256,512]{1,0:T(8,128)(2,1)} %get-tuple-element.10.refs_0_, f32[256,512]{1,0:T(8,128)} %get-tuple-element.11.refs_1_, bf16[256,512]{1,0:T(8,128)(2,1)} %get-tuple-element.12.refs_2_, bf16[512,128]{1,0:T(8,128)(2,1)} %get-tuple-element.13.refs_3_, bf16[512,128]{1,0:T(8,128)(2,1)} %copy-done.2, ...), custom_call_target="tpu_custom_call" | custom-call | flops 134217728 | bytes 1835008 | tf_op jit(solution)/shard_map/pallas_call | solution.py:154
  (19 shorter events, 0.0 us)
Async XLA Ops:
  17.2 3.5 %copy-start = (bf16[64,512]{1,0:T(8,128)(2,1)S(1)}, bf16[64,512]{1,0:T(8,128)(2,1)}, u32[]{:S(2)}) copy-start(bf16[64,512]{1,0:T(8,128)(2,1)} %refs_3_.1) | copy-start | bytes 196612
  19.2 5.2 %collective-permute-start.4 = (bf16[512,128]{1,0:T(8,128)(2,1)}, bf16[512,128]{1,0:T(8,128)(2,1)S(1)}, u32[]{:S(2)}, u32[]{:S(2)}) collective-permute-start(bf16[512,128]{1,0:T(8,128)(2,1)} %get-tuple-element.14), channel_id=1, source_target_pairs={{0,16},{8,24},{16,0},{24,8},{1,17},{9,25},{17,1},{25,9},{2,18},{10... | collective-permute-start | bytes 393224 | tf_op jit(solution)/shard_map/ppermute | solution.py:176
  20.7 4.5 %collective-permute-start.1 = (bf16[64,512]{1,0:T(8,128)(2,1)S(1)}, bf16[64,512]{1,0:T(8,128)(2,1)S(1)}, u32[]{:S(2)}, u32[]{:S(2)}) collective-permute-start(bf16[64,512]{1,0:T(8,128)(2,1)S(1)} %copy-done), channel_id=1, source_target_pairs={{0,16},{8,24},{16,0},{24,8},{1,17},{9,25},{17,1},{25,9},{2,18},{10... | collective-permute-start | bytes 196616 | tf_op jit(solution)/shard_map/ppermute | solution.py:176
  21.2 6.0 %collective-permute-start = (bf16[64,512]{1,0:T(8,128)(2,1)S(1)}, bf16[64,512]{1,0:T(8,128)(2,1)S(1)}, u32[]{:S(2)}, u32[]{:S(2)}) collective-permute-start(bf16[64,512]{1,0:T(8,128)(2,1)S(1)} %copy-done), channel_id=1, source_target_pairs={{0,8},{8,0},{16,24},{24,16},{1,9},{9,1},{17,25},{25,17},{2,10},{10... | collective-permute-start | bytes 196616 | tf_op jit(solution)/shard_map/ppermute | solution.py:176
  21.2 0.7 %copy-start.7 = (f32[64]{0:T(128)S(1)}, f32[64]{0:T(128)}, u32[]{:S(2)}) copy-start(f32[64]{0:T(128)} %param.6) | copy-start | bytes 772
  21.9 8.2 %collective-permute-start.3 = (bf16[512,128]{1,0:T(8,128)(2,1)}, bf16[512,128]{1,0:T(8,128)(2,1)S(1)}, u32[]{:S(2)}, u32[]{:S(2)}) collective-permute-start(bf16[512,128]{1,0:T(8,128)(2,1)} %get-tuple-element.13.refs_3_), channel_id=1, source_target_pairs={{0,8},{8,0},{16,24},{24,16},{1,9},{9,1},{17,25},{25,17},{2,10},{10... | collective-permute-start | bytes 393224 | tf_op jit(solution)/shard_map/ppermute | solution.py:176
  24.4 5.8 %copy-start.1 = (bf16[512,128]{1,0:T(8,128)(2,1)}, bf16[512,128]{1,0:T(8,128)(2,1)S(1)}, u32[]{:S(2)}) copy-start(bf16[512,128]{1,0:T(8,128)(2,1)S(1)} %collective-permute-done.4.refs_5_) | copy-start | bytes 393220
  24.4 5.8 %collective-permute-start.5 = (bf16[512,128]{1,0:T(8,128)(2,1)S(1)}, bf16[512,128]{1,0:T(8,128)(2,1)S(1)}, u32[]{:S(2)}, u32[]{:S(2)}) collective-permute-start(bf16[512,128]{1,0:T(8,128)(2,1)S(1)} %collective-permute-done.4.refs_5_), channel_id=1, source_target_pairs={{0,8},{8,0},{16,24},{24,16},{1,9},{9,1},{17,25},{25,17},{2,10},{10... | collective-permute-start | bytes 393224 | tf_op jit(solution)/shard_map/ppermute | solution.py:176
  24.4 0.7 %copy-start.8 = (f32[32]{0:T(128)S(1)}, f32[32]{0:T(128)}, u32[]{:S(2)}) copy-start(f32[32]{0:T(128)} %param.7) | copy-start | bytes 388
  25.2 2.1 %copy-start.4 = (bf16[64,512]{1,0:T(8,128)(2,1)}, bf16[64,512]{1,0:T(8,128)(2,1)S(1)}, u32[]{:S(2)}) copy-start(bf16[64,512]{1,0:T(8,128)(2,1)S(1)} %collective-permute-done.1.refs_5_) | copy-start | bytes 196612
  25.2 2.0 %collective-permute-start.2 = (bf16[64,512]{1,0:T(8,128)(2,1)S(1)}, bf16[64,512]{1,0:T(8,128)(2,1)S(1)}, u32[]{:S(2)}, u32[]{:S(2)}) collective-permute-start(bf16[64,512]{1,0:T(8,128)(2,1)S(1)} %collective-permute-done.1.refs_5_), channel_id=1, source_target_pairs={{0,8},{8,0},{16,24},{24,16},{1,9},{9,1},{17,25},{25,17},{2,10},{10... | collective-permute-start | bytes 196616 | tf_op jit(solution)/shard_map/ppermute | solution.py:176
  27.2 0.6 %copy-start.5 = (bf16[64,512]{1,0:T(8,128)(2,1)}, bf16[64,512]{1,0:T(8,128)(2,1)S(1)}, u32[]{:S(2)}) copy-start(bf16[64,512]{1,0:T(8,128)(2,1)S(1)} %collective-permute-done.refs_4_) | copy-start | bytes 196612
  27.2 0.7 %copy-start.6 = (bf16[64,512]{1,0:T(8,128)(2,1)}, bf16[64,512]{1,0:T(8,128)(2,1)S(1)}, u32[]{:S(2)}) copy-start(bf16[64,512]{1,0:T(8,128)(2,1)S(1)} %collective-permute-done.2.refs_6_) | copy-start | bytes 196612
  30.1 0.7 %copy-start.2 = (bf16[512,128]{1,0:T(8,128)(2,1)}, bf16[512,128]{1,0:T(8,128)(2,1)S(1)}, u32[]{:S(2)}) copy-start(bf16[512,128]{1,0:T(8,128)(2,1)S(1)} %collective-permute-done.3.refs_4_) | copy-start | bytes 393220
  30.2 0.7 %copy-start.3 = (bf16[512,128]{1,0:T(8,128)(2,1)}, bf16[512,128]{1,0:T(8,128)(2,1)S(1)}, u32[]{:S(2)}) copy-start(bf16[512,128]{1,0:T(8,128)(2,1)S(1)} %collective-permute-done.5.refs_6_) | copy-start | bytes 393220

commit v2 on v1

--- a/solution.py
+++ b/solution.py
@@ -8,6 +8,7 @@
 from jax.sharding import PartitionSpec as P
 
 LANES = 128
+LEAST, MOST = 8 << 20, 60 << 20
 F32 = jnp.float32
 BF16 = jnp.bfloat16
 VMEM = pltpu.MemorySpace.VMEM
@@ -21,6 +22,14 @@
 
 def columns(n):
     return lax.broadcasted_iota(jnp.int32, (1, n), 1)
+
+
+def square_eye(n):
+    return lax.broadcasted_iota(jnp.int32, (n, n), 0) == lax.broadcasted_iota(jnp.int32, (n, n), 1)
+
+
+def pick_sum(values, where, axis):
+    return jnp.sum(jnp.where(where, values, 0.0), axis=axis, keepdims=True)
 
 
 def pack_kernel(occ_all, t_ref, v_ref, out_ref):
@@ -100,7 +109,7 @@
 
 def direct_kernel(sizes, *refs):
     vir_parts, vir_own, occ_own, high, deep, width = sizes
-    got_ref, occ_ref, row_ref, *amp_refs, lad_ref, den_ref, sel_ref, all_ref = refs
+    got_ref, occ_ref, vir_ref, *amp_refs, lad_ref, den_ref, sel_ref, all_ref = refs
     me = lax.axis_index("vv")
     depth = amp_refs[0].shape[0]
     for rel, ref in enumerate(amp_refs):
@@ -110,11 +119,21 @@
     lad_ref[...] = lax.dot_general(
         ints, all_ref[...], (((0,), (0,)), ((), ())), preferred_element_type=F32
     ).astype(BF16)
-    den_ref[...] = occ_ref[...] - row_ref[:, :1] - row_ref[:, 1:]
-    rows, n = sel_ref.shape
+    rows, cols = den_ref.shape
+    vir_all, occ_all = vir_parts * vir_own, occ_ref.shape[1]
+    occ = occ_ref[...]
+    occ_column = pick_sum(occ, square_eye(occ_all), 1)
+    mine = lax.axis_index("oo") * occ_own + columns(cols) // occ_all
+    occ_mine = pick_sum(occ_column, lax.broadcasted_iota(jnp.int32, (occ_all, cols), 0) == mine, 0)
+    occ_pair = occ_mine + jnp.concatenate([occ] * occ_own, axis=1)
+    lane = lax.broadcasted_iota(jnp.int32, (rows, vir_all), 1)
+    row = lax.broadcasted_iota(jnp.int32, (rows, 1), 0)
+    vir = vir_ref[...]
+    vir_mine = pick_sum(vir, lane == me * vir_own + row // vir_all, 1)
+    vir_other = pick_sum(vir, lane == row % vir_all, 1)
+    den_ref[...] = occ_pair - vir_mine - vir_other
+    n = sel_ref.shape[1]
     area = vir_own * vir_own
-    vir_all = vir_parts * vir_own
-    row = lax.broadcasted_iota(jnp.int32, (rows, 1), 0)
     rel = jnp.bitwise_xor(row % vir_all // vir_own, me)
     source = rel * width + (rel % (width // area)) * area + row // vir_all * vir_own + row % vir_own
     pick = lax.broadcasted_iota(jnp.int32, (rows, n), 1) == source
@@ -157,6 +176,7 @@
         in_specs=[pl.BlockSpec(memory_space=VMEM)] * len(args),
         out_specs=tuple(pl.BlockSpec(memory_space=VMEM) for _ in outs),
         scratch_shapes=list(scratch),
+        compiler_params=pltpu.CompilerParams(vmem_limit_bytes=min(MOST, LEAST + 3 * moved)),
         cost_estimate=pl.CostEstimate(flops=flops, bytes_accessed=moved, transcendentals=0),
     )(*args)
     return result
@@ -215,16 +235,6 @@
             held = {k: (x, x) for k, x in arrived.items()}
     order = range(vir_parts)
 
-    vir_mine = lax.dynamic_slice_in_dim(vir_energy, lax.axis_index("vv") * vir_own, vir_own, 0)
-    occ_mine = lax.dynamic_slice_in_dim(occ_energy, lax.axis_index("oo") * occ_own, occ_own, 0)
-    occ_pair = (occ_mine[:, None] + occ_energy[None, :]).reshape(1, cols)
-    vir_pair = jnp.stack(
-        [
-            jnp.broadcast_to(vir_mine[:, None], (vir_own, vir_all)),
-            jnp.broadcast_to(vir_energy[None, :], (vir_own, vir_all)),
-        ],
-        axis=-1,
-    ).reshape(rows, 2)
     ladder, denom, select = call(
         functools.partial(direct_kernel, (vir_parts, vir_own, occ_own, high, deep, lanes)),
         [
@@ -232,7 +242,7 @@
             jax.ShapeDtypeStruct((rows, cols), F32),
             jax.ShapeDtypeStruct((rows, vir_parts * lanes), BF16),
         ],
-        (got, occ_pair, vir_pair, *(direct[k] for k in order)),
+        (got, occ_energy.reshape(1, occ_all), vir_energy.reshape(1, vir_all), *(direct[k] for k in order)),
         scratch=[pltpu.VMEM((total, cols), BF16)],
         flops=2 * rows * total * cols,
     )

time: 33.8 us -> 26.9 us (0.80)
  Pallas kernels: 8.66 us -> 2.23 us
  waiting for transfers between devices: 1.92 us -> 4.5 us
  local copies, waits for them, and re-layouts: 4.3 us -> 2.23 us
  starting transfers between devices: 3.05 us -> 2.61 us
    pallas_call x4, Pallas kernels: 8.66 us -> 2.23 us  [call(): pl.pallas_call(kernel, out_shape=outs, in_specs=[pl.BlockSpec(memory_spac...]
    ppermute x6, waiting for transfers between devices: 1.92 us -> 4.5 us  [swap(): return lax.ppermute(x, 'vv', [(k, k ^ step) for k in range(vir_parts)])]
    another operation x3 -> x0, local copies, waits for them, and re-layouts: 0.86 us -> none  [on_device(): jnp.stack([jnp.broadcast_to(vir_mine[:, None], (vir_own, vir_all)), jnp.b...]
    add x1 -> x0, local copies, waits for them, and re-layouts: 0.65 us -> none  [on_device(): occ_pair = (occ_mine[:, None] + occ_energy[None, :]).reshape(1, cols)]
    ppermute x6, starting transfers between devices: 3.05 us -> 2.61 us  [swap(): return lax.ppermute(x, 'vv', [(k, k ^ step) for k in range(vir_parts)])]
    unnamed x18 -> x10, local copies, waits for them, and re-layouts: 2.64 us -> 2.23 us
  transfers between devices with their start and end apart: 6 -> 6, of which waited for: 1 -> 4; matrix products, arithmetic and copies ran while one was open for 5% -> 0% of each run, Pallas kernels for 7% -> 1%
where the time goes in v2:
time: 26.9 us; the launch traced here: 26.6 us
  blocking collectives  15 us (56%)
  waiting for transfers between devices  4.5 us (17%)
  starting transfers between devices  2.61 us (10%)
  local copies, waits for them, and re-layouts  2.23 us (8%)
  Pallas kernels  2.23 us (8%)
    all_to_all x1, blocking collectives, on_device(): got = lax.all_to_all(packed, 'oo', 0, 0, tiled=True)  15 us
    ppermute x6, waiting for transfers between devices, swap(): return lax.ppermute(x, 'vv', [(k, k ^ step) for k in range(vir_parts)])  4.5 us
    ppermute x6, starting transfers between devices, swap(): return lax.ppermute(x, 'vv', [(k, k ^ step) for k in range(vir_parts)])  2.61 us
    pallas_call x4, Pallas kernels, call(): pl.pallas_call(kernel, out_shape=outs, in_specs=[pl.BlockSpec(memory_spac...  2.23 us
    unnamed x10, local copies, waits for them, and re-layouts  2.23 us
  transfers between devices with their start and end apart: 6, of which 4 were waited for; matrix products, arithmetic and copies ran while one was open for 0% of the time, Pallas kernels for 1%

profile of v2, /device:TPU:0, one launch (start us, length us, event | category | flops | bytes accessed | tf_op | source)
XLA Modules:
  0.0 26.6 jit_solution(12815973891050128685)
XLA Ops:
  0.0 0.0 copy-start
  0.0 0.8 %copy-done = bf16[64,512]{1,0:T(8,128)(2,1)S(1)} copy-done((bf16[64,512]{1,0:T(8,128)(2,1)S(1)}, bf16[64,512]{1,0:T(8,128)(2,1)}, u32[]{:S(2)}) %copy-start) | copy-done | bytes 65560
  0.8 0.0 copy-start.2
  0.8 0.7 %copy-done.2 = bf16[256,32]{0,1:T(8,128)(2,1)S(1)} copy-done((bf16[256,32]{0,1:T(8,128)(2,1)S(1)}, bf16[256,32]{0,1:T(8,128)(2,1)}, u32[]{:S(2)}) %copy-start.2) | copy-done | bytes 16408
  1.6 0.3 %shard_map.46 = bf16[8,96,128]{2,1,0:T(8,128)(2,1)S(1)} custom-call(bf16[64,512]{1,0:T(8,128)(2,1)S(1)} %copy-done, bf16[32,256]{1,0:T(8,128)(2,1)S(1)} %bitcast.3), custom_call_target="tpu_custom_call" | custom-call | flops 33554432 | bytes 278528 | tf_op jit(solution)/shard_map/pallas_call | solution.py:173
  1.9 15.0 %all_to_all.5.refs_0_.got_ref = bf16[8,96,128]{2,1,0:T(8,128)(2,1)S(1)} all-to-all(bf16[8,96,128]{2,1,0:T(8,128)(2,1)S(1)} %shard_map.46), channel_id=1, replica_groups=mesh['vv'=4,'oo'=8] {'oo'}, dimensions={0} | all-to-all | bytes 393216 | tf_op jit(solution)/shard_map/all_to_all | solution.py:205
  16.9 0.4 %shard_map.48 = (bf16[512,128]{1,0:T(8,128)(2,1)S(1)}, bf16[512,128]{1,0:T(8,128)(2,1)S(1)}) custom-call(bf16[8,96,128]{2,1,0:T(8,128)(2,1)S(1)} %all_to_all.5.refs_0_.got_ref), custom_call_target="tpu_custom_call" | custom-call | flops 67108864 | bytes 458752 | tf_op jit(solution)/shard_map/pallas_call | solution.py:173
  17.3 1.6 %collective-permute-start.4 = (bf16[512,128]{1,0:T(8,128)(2,1)S(1)}, bf16[512,128]{1,0:T(8,128)(2,1)S(1)}, u32[]{:S(2)}, u32[]{:S(2)}) collective-permute-start(bf16[512,128]{1,0:T(8,128)(2,1)S(1)} %get-tuple-element.14), channel_id=1, source_target_pairs={{0,16},{8,24},{16,0},{24,8},{1,17},{9,25},{17,1},{25,9},{2,18},{10... | collective-permute-start | bytes 393224 | tf_op jit(solution)/shard_map/ppermute | solution.py:196
  18.9 0.0 copy-done.1
  18.9 0.5 %collective-permute-start.1 = (bf16[64,512]{1,0:T(8,128)(2,1)S(1)}, bf16[64,512]{1,0:T(8,128)(2,1)S(1)}, u32[]{:S(2)}, u32[]{:S(2)}) collective-permute-start(bf16[64,512]{1,0:T(8,128)(2,1)S(1)} %copy-done.1), channel_id=1, source_target_pairs={{0,16},{8,24},{16,0},{24,8},{1,17},{9,25},{17,1},{25,9},{2,18},{10... | collective-permute-start | bytes 196616 | tf_op jit(solution)/shard_map/ppermute | solution.py:196
  19.4 0.0 collective-permute-start.3
  19.4 2.9 %collective-permute-done.4.refs_5_ = bf16[512,128]{1,0:T(8,128)(2,1)S(1)} collective-permute-done((bf16[512,128]{1,0:T(8,128)(2,1)S(1)}, bf16[512,128]{1,0:T(8,128)(2,1)S(1)}, u32[]{:S(2)}, u32[]{:S(2)}) %collective-permute-start.4) | collective-permute-done | bytes 131104 | tf_op jit(solution)/shard_map/ppermute | solution.py:196
  22.3 0.0 collective-permute-start.5
  22.3 0.5 %collective-permute-start = (bf16[64,512]{1,0:T(8,128)(2,1)S(1)}, bf16[64,512]{1,0:T(8,128)(2,1)S(1)}, u32[]{:S(2)}, u32[]{:S(2)}) collective-permute-start(bf16[64,512]{1,0:T(8,128)(2,1)S(1)} %copy-done.1), channel_id=1, source_target_pairs={{0,8},{8,0},{16,24},{24,16},{1,9},{9,1},{17,25},{25,17},{2,10},{10... | collective-permute-start | bytes 196616 | tf_op jit(solution)/shard_map/ppermute | solution.py:196
  22.8 0.3 %collective-permute-done.1.refs_5_ = bf16[64,512]{1,0:T(8,128)(2,1)S(1)} collective-permute-done((bf16[64,512]{1,0:T(8,128)(2,1)S(1)}, bf16[64,512]{1,0:T(8,128)(2,1)S(1)}, u32[]{:S(2)}, u32[]{:S(2)}) %collective-permute-start.1) | collective-permute-done | bytes 65568 | tf_op jit(solution)/shard_map/ppermute | solution.py:196
  23.1 0.0 collective-permute-start.2
  23.1 0.6 %collective-permute-done.refs_4_ = bf16[64,512]{1,0:T(8,128)(2,1)S(1)} collective-permute-done((bf16[64,512]{1,0:T(8,128)(2,1)S(1)}, bf16[64,512]{1,0:T(8,128)(2,1)S(1)}, u32[]{:S(2)}, u32[]{:S(2)}) %collective-permute-start) | collective-permute-done | bytes 65568 | tf_op jit(solution)/shard_map/ppermute | solution.py:196
  23.8 0.6 %collective-permute-done.2.refs_6_ = bf16[64,512]{1,0:T(8,128)(2,1)S(1)} collective-permute-done((bf16[64,512]{1,0:T(8,128)(2,1)S(1)}, bf16[64,512]{1,0:T(8,128)(2,1)S(1)}, u32[]{:S(2)}, u32[]{:S(2)}) %collective-permute-start.2) | collective-permute-done | bytes 65568 | tf_op jit(solution)/shard_map/ppermute | solution.py:196
  24.4 0.7 %copy-done.3 = f32[64]{0:T(128)S(1)} copy-done((f32[64]{0:T(128)S(1)}, f32[64]{0:T(128)}, u32[]{:S(2)}) %copy-start.3) | copy-done | bytes 280
  25.0 0.0 copy-done.4
  25.1 0.3 %shard_map.47 = (bf16[256,512]{1,0:T(8,128)(2,1)S(1)}, f32[256,512]{1,0:T(8,128)S(1)}, bf16[256,512]{1,0:T(8,128)(2,1)S(1)}) custom-call(bf16[8,96,128]{2,1,0:T(8,128)(2,1)S(1)} %all_to_all.5.refs_0_.got_ref, f32[1,64]{1,0:T(1,128)S(1)} %bitcast.4, f32[1,32]{1,0:T(1,128)S(1)} %bitcast.5, bf16[64,512]{1,0:T(8,128)(2,1)S(1)} %copy-done.1, ...), custom_call_target="tpu_custom_call" | custom-call | flops 67108864 | bytes 1507712 | tf_op jit(solution)/shard_map/pallas_call | solution.py:173
  25.4 0.0 collective-permute-done.3.refs_4_
  25.4 0.0 collective-permute-done.5.refs_6_
  25.4 1.2 %shard_map.49 = bf16[256,512]{1,0:T(8,128)(2,1)} custom-call(bf16[256,512]{1,0:T(8,128)(2,1)S(1)} %get-tuple-element.10.refs_0_, f32[256,512]{1,0:T(8,128)S(1)} %get-tuple-element.11.refs_1_, bf16[256,512]{1,0:T(8,128)(2,1)S(1)} %get-tuple-element.12.refs_2_, bf16[512,128]{1,0:T(8,128)(2,1)S(1)} %get-tuple-element.13.refs_3_, ...), custom_call_target="tpu_custom_call" | custom-call | flops 134217728 | bytes 1835008 | tf_op jit(solution)/shard_map/pallas_call | solution.py:173
  (3 shorter events, 0.0 us)
Async XLA Ops:
  0.0 0.8 %copy-start = (bf16[64,512]{1,0:T(8,128)(2,1)S(1)}, bf16[64,512]{1,0:T(8,128)(2,1)}, u32[]{:S(2)}) copy-start(bf16[64,512]{1,0:T(8,128)(2,1)} %refs_3_.1) | copy-start | bytes 196612
  0.8 0.7 %copy-start.2 = (bf16[256,32]{0,1:T(8,128)(2,1)S(1)}, bf16[256,32]{0,1:T(8,128)(2,1)}, u32[]{:S(2)}) copy-start(bf16[256,32]{0,1:T(8,128)(2,1)} %param.4) | copy-start | bytes 49156
  16.9 2.0 %copy-start.1 = (bf16[64,512]{1,0:T(8,128)(2,1)S(1)}, bf16[64,512]{1,0:T(8,128)(2,1)}, u32[]{:S(2)}) copy-start(bf16[64,512]{1,0:T(8,128)(2,1)} %refs_3_.1) | copy-start | bytes 196612
  17.3 5.0 %collective-permute-start.4 = (bf16[512,128]{1,0:T(8,128)(2,1)S(1)}, bf16[512,128]{1,0:T(8,128)(2,1)S(1)}, u32[]{:S(2)}, u32[]{:S(2)}) collective-permute-start(bf16[512,128]{1,0:T(8,128)(2,1)S(1)} %get-tuple-element.14), channel_id=1, source_target_pairs={{0,16},{8,24},{16,0},{24,8},{1,17},{9,25},{17,1},{25,9},{2,18},{10... | collective-permute-start | bytes 393224 | tf_op jit(solution)/shard_map/ppermute | solution.py:196
  18.9 4.3 %collective-permute-start.1 = (bf16[64,512]{1,0:T(8,128)(2,1)S(1)}, bf16[64,512]{1,0:T(8,128)(2,1)S(1)}, u32[]{:S(2)}, u32[]{:S(2)}) collective-permute-start(bf16[64,512]{1,0:T(8,128)(2,1)S(1)} %copy-done.1), channel_id=1, source_target_pairs={{0,16},{8,24},{16,0},{24,8},{1,17},{9,25},{17,1},{25,9},{2,18},{10... | collective-permute-start | bytes 196616 | tf_op jit(solution)/shard_map/ppermute | solution.py:196
  19.4 6.0 %collective-permute-start.3 = (bf16[512,128]{1,0:T(8,128)(2,1)S(1)}, bf16[512,128]{1,0:T(8,128)(2,1)S(1)}, u32[]{:S(2)}, u32[]{:S(2)}) collective-permute-start(bf16[512,128]{1,0:T(8,128)(2,1)S(1)} %get-tuple-element.13.refs_3_), channel_id=1, source_target_pairs={{0,8},{8,0},{16,24},{24,16},{1,9},{9,1},{17,25},{25,17},{2,10},{10... | collective-permute-start | bytes 393224 | tf_op jit(solution)/shard_map/ppermute | solution.py:196
  22.3 3.1 %collective-permute-start.5 = (bf16[512,128]{1,0:T(8,128)(2,1)S(1)}, bf16[512,128]{1,0:T(8,128)(2,1)S(1)}, u32[]{:S(2)}, u32[]{:S(2)}) collective-permute-start(bf16[512,128]{1,0:T(8,128)(2,1)S(1)} %collective-permute-done.4.refs_5_), channel_id=1, source_target_pairs={{0,8},{8,0},{16,24},{24,16},{1,9},{9,1},{17,25},{25,17},{2,10},{10... | collective-permute-start | bytes 393224 | tf_op jit(solution)/shard_map/ppermute | solution.py:196
  22.3 1.4 %collective-permute-start = (bf16[64,512]{1,0:T(8,128)(2,1)S(1)}, bf16[64,512]{1,0:T(8,128)(2,1)S(1)}, u32[]{:S(2)}, u32[]{:S(2)}) collective-permute-start(bf16[64,512]{1,0:T(8,128)(2,1)S(1)} %copy-done.1), channel_id=1, source_target_pairs={{0,8},{8,0},{16,24},{24,16},{1,9},{9,1},{17,25},{25,17},{2,10},{10... | collective-permute-start | bytes 196616 | tf_op jit(solution)/shard_map/ppermute | solution.py:196
  23.1 1.3 %collective-permute-start.2 = (bf16[64,512]{1,0:T(8,128)(2,1)S(1)}, bf16[64,512]{1,0:T(8,128)(2,1)S(1)}, u32[]{:S(2)}, u32[]{:S(2)}) collective-permute-start(bf16[64,512]{1,0:T(8,128)(2,1)S(1)} %collective-permute-done.1.refs_5_), channel_id=1, source_target_pairs={{0,8},{8,0},{16,24},{24,16},{1,9},{9,1},{17,25},{25,17},{2,10},{10... | collective-permute-start | bytes 196616 | tf_op jit(solution)/shard_map/ppermute | solution.py:196
  24.4 0.7 %copy-start.3 = (f32[64]{0:T(128)S(1)}, f32[64]{0:T(128)}, u32[]{:S(2)}) copy-start(f32[64]{0:T(128)} %param.6) | copy-start | bytes 772
  24.4 0.7 %copy-start.4 = (f32[32]{0:T(128)S(1)}, f32[32]{0:T(128)}, u32[]{:S(2)}) copy-start(f32[32]{0:T(128)} %param.7) | copy-start | bytes 388

commit v3 on v2

--- a/solution.py
+++ b/solution.py
@@ -7,8 +7,10 @@
 from jax.experimental.pallas import tpu as pltpu
 from jax.sharding import PartitionSpec as P
 
+
 LANES = 128
 LEAST, MOST = 8 << 20, 60 << 20
+CHOOSE_FLOPS = 10**9
 F32 = jnp.float32
 BF16 = jnp.bfloat16
 VMEM = pltpu.MemorySpace.VMEM
@@ -32,14 +34,11 @@
     return jnp.sum(jnp.where(where, values, 0.0), axis=axis, keepdims=True)
 
 
-def pack_kernel(occ_all, t_ref, v_ref, out_ref):
+def pack_kernel(own, t_ref, v_ref, source_ref, out_ref):
     parts, rows, lanes = out_ref.shape
     depth, cols = t_ref.shape
-    own = cols // occ_all
     square = own * own
-    col = columns(cols)
-    source = (col % square // own) * occ_all + (col // square) * own + col % own
-    moved = jnp.dot(t_ref[...], one_hot(cols, source), preferred_element_type=F32)
+    moved = jnp.dot(t_ref[...], one_hot(cols, source_ref[...]), preferred_element_type=F32)
     fold = lanes // square
     high = depth // fold
     for part in range(parts):
@@ -72,7 +71,6 @@
     square = occ_own * occ_own
     fold = lanes // square
     cols = parts * square
-    occ_all = parts * occ_own
     packed = got_ref[:, :high, :].astype(F32)
     halves = [
         jnp.concatenate(
@@ -81,7 +79,7 @@
         for h in range(fold)
     ]
     amps = jnp.concatenate(halves, axis=0).astype(BF16)
-    col = columns(cols)
+    col, occ_all = columns(cols), parts * occ_own
     source = (col % occ_all // occ_own) * square + (col % occ_own) * occ_own + col // occ_all
     amps = jnp.dot(amps, one_hot(cols, source), preferred_element_type=F32).astype(BF16)
     depth = amps.shape[0]
@@ -90,12 +88,10 @@
         block = amps[:, c * lanes : (c + 1) * lanes]
         send_ref[c * depth : (c + 1) * depth, :] = block
         keep_ref[c * depth : (c + 1) * depth, :] = block
-    me = lax.axis_index("vv")
     ints = integral_columns(got_ref, high, deep)
     total, rows = ints.shape
-    area = vir_own * vir_own
-    col = columns(rows)
-    owner = jnp.bitwise_xor(col // area, me)
+    col, area = columns(rows), vir_own * vir_own
+    owner = jnp.bitwise_xor(col // area, lax.axis_index("vv"))
     source = (col % vir_own) * (vir_parts * vir_own) + owner * vir_own + col % area // vir_own
     ints = jnp.dot(ints, one_hot(rows, source), preferred_element_type=F32).astype(BF16)
     base = chunks * depth
@@ -132,19 +128,25 @@
     vir_mine = pick_sum(vir, lane == me * vir_own + row // vir_all, 1)
     vir_other = pick_sum(vir, lane == row % vir_all, 1)
     den_ref[...] = occ_pair - vir_mine - vir_other
-    n = sel_ref.shape[1]
-    area = vir_own * vir_own
+    n, area = sel_ref.shape[1], vir_own * vir_own
     rel = jnp.bitwise_xor(row % vir_all // vir_own, me)
     source = rel * width + (rel % (width // area)) * area + row // vir_all * vir_own + row % vir_own
     pick = lax.broadcasted_iota(jnp.int32, (rows, n), 1) == source
     sel_ref[...] = jnp.where(pick, 1.0, 0.0).astype(BF16)
 
 
+def choose_kernel(own, source_ref):
+    cols = source_ref.shape[1]
+    square, occ_all = own * own, cols // own
+    col = columns(cols)
+    source_ref[...] = (col % square // own) * occ_all + (col // square) * own + col % own
+
+
 def mirror_kernel(sizes, *refs):
     depth, total, width = sizes
     lad_ref, den_ref, sel_ref, *got_refs, out_ref, all_ref = refs
     me = lax.axis_index("vv")
-    rows, cols = out_ref.shape
+    _, cols = out_ref.shape
     chunks = cols // LANES
     for rel, ref in enumerate(got_refs):
         at = pl.multiple_of(jnp.bitwise_xor(me, rel) * depth, depth)
@@ -167,13 +169,13 @@
     out_ref[...] = (total_sum / den_ref[...]).astype(BF16)
 
 
-def call(kernel, outs, args, scratch=(), flops=0):
+def call(kernel, outs, args, scratch=(), flops=0, space=VMEM):
     outs = tuple(outs)
     moved = sum(x.size * x.dtype.itemsize for x in (*args, *outs))
     result = pl.pallas_call(
         kernel,
         out_shape=outs,
-        in_specs=[pl.BlockSpec(memory_space=VMEM)] * len(args),
+        in_specs=[pl.BlockSpec(memory_space=space)] * len(args),
         out_specs=tuple(pl.BlockSpec(memory_space=VMEM) for _ in outs),
         scratch_shapes=list(scratch),
         compiler_params=pltpu.CompilerParams(vmem_limit_bytes=min(MOST, LEAST + 3 * moved)),
@@ -195,39 +197,44 @@
     def swap(x, step):
         return lax.ppermute(x, "vv", [(k, k ^ step) for k in range(vir_parts)])
 
+    steps = [1 << bit for bit in reversed(range((vir_parts - 1).bit_length()))]
+    widths = [s * area for s in steps if s * area % LANES == 0] or [rows]
+    width = widths[-1]
+
+    (source,) = call(
+        functools.partial(choose_kernel, occ_own),
+        [jax.ShapeDtypeStruct((1, cols), jnp.int32)],
+        (),
+        flops=CHOOSE_FLOPS,
+    )
+
     shape = (occ_parts, high + rows // LANES * deep, LANES)
     (packed,) = call(
-        functools.partial(pack_kernel, occ_all),
+        functools.partial(pack_kernel, occ_own),
         [jax.ShapeDtypeStruct(shape, BF16)],
-        (amplitudes, integrals.T),
+        (amplitudes, integrals.T, source),
         flops=2 * depth * cols * cols,
     )
     got = lax.all_to_all(packed, "oo", 0, 0, tiled=True)
 
-    step = vir_parts // 2
-    lanes = rows
-    halves = step * area % LANES == 0
-    send_lanes = lanes // 2 if halves else lanes
     amp_rows = cols // LANES * depth
+    send_shape = jax.ShapeDtypeStruct((amp_rows + widths[0] // LANES * total, LANES), BF16)
     send, keep = call(
         functools.partial(
-            split_kernel, (vir_parts, vir_own, occ_own, high, deep, send_lanes // LANES)
+            split_kernel, (vir_parts, vir_own, occ_own, high, deep, widths[0] // LANES)
         ),
-        [jax.ShapeDtypeStruct((amp_rows + send_lanes // LANES * total, LANES), BF16)] * 2,
+        [send_shape] * 2,
         (got,),
         flops=2 * depth * cols * cols + 2 * total * rows * rows,
     )
     held = {0: (send, keep)}
     direct = {0: amplitudes}
-    lanes = send_lanes
-    while step:
+    for at, step in enumerate(steps):
         direct |= {k ^ step: swap(x, step) for k, x in direct.items()}
         arrived = {k: x for k, (_, x) in held.items()}
         arrived |= {k ^ step: swap(x, step) for k, (x, _) in held.items()}
-        step //= 2
-        if step and step * area % LANES == 0:
-            lanes //= 2
-            cut = amp_rows + lanes // LANES * total
+        if at + 1 < len(widths):
+            cut = amp_rows + widths[at + 1] // LANES * total
             held = {
                 k: (jnp.concatenate([x[:amp_rows], x[cut:]]), x[:cut]) for k, x in arrived.items()
             }
@@ -235,21 +242,26 @@
             held = {k: (x, x) for k, x in arrived.items()}
     order = range(vir_parts)
 
-    ladder, denom, select = call(
-        functools.partial(direct_kernel, (vir_parts, vir_own, occ_own, high, deep, lanes)),
+    ladder, denom, to_rows = call(
+        functools.partial(direct_kernel, (vir_parts, vir_own, occ_own, high, deep, width)),
         [
             jax.ShapeDtypeStruct((rows, cols), BF16),
             jax.ShapeDtypeStruct((rows, cols), F32),
-            jax.ShapeDtypeStruct((rows, vir_parts * lanes), BF16),
+            jax.ShapeDtypeStruct((rows, vir_parts * width), BF16),
         ],
-        (got, occ_energy.reshape(1, occ_all), vir_energy.reshape(1, vir_all), *(direct[k] for k in order)),
+        (
+            got,
+            occ_energy.reshape(1, occ_all),
+            vir_energy.reshape(1, vir_all),
+            *(direct[k] for k in order),
+        ),
         scratch=[pltpu.VMEM((total, cols), BF16)],
         flops=2 * rows * total * cols,
     )
     (update,) = call(
-        functools.partial(mirror_kernel, (depth, total, lanes)),
+        functools.partial(mirror_kernel, (depth, total, width)),
         [jax.ShapeDtypeStruct((rows, cols), BF16)],
-        (ladder, denom, select, *(arrived[k] for k in order)),
+        (ladder, denom, to_rows, *(arrived[k] for k in order)),
         scratch=[pltpu.VMEM((total, cols), BF16)],
         flops=2 * rows * total * cols * 2,
     )

time: 26.9 us -> 26.2 us (0.974)
  local copies, waits for them, and re-layouts: 2.23 us -> 1.51 us
    unnamed x10 -> x8, local copies, waits for them, and re-layouts: 2.23 us -> 1.51 us
    pallas_call x4 -> x5, Pallas kernels: 2.23 us -> 2.24 us  [call(): pl.pallas_call(kernel, out_shape=outs, in_specs=[pl.BlockSpec(memory_spac...]
where the time goes in v3:
time: 26.2 us; the launch traced here: 25.9 us
  blocking collectives  15 us (57%)
  waiting for transfers between devices  4.49 us (17%)
  starting transfers between devices  2.61 us (10%)
  Pallas kernels  2.24 us (9%)
  local copies, waits for them, and re-layouts  1.51 us (6%)
    all_to_all x1, blocking collectives, on_device(): got = lax.all_to_all(packed, 'oo', 0, 0, tiled=True)  15 us
    ppermute x6, waiting for transfers between devices, swap(): return lax.ppermute(x, 'vv', [(k, k ^ step) for k in range(vir_parts)])  4.49 us
    ppermute x6, starting transfers between devices, swap(): return lax.ppermute(x, 'vv', [(k, k ^ step) for k in range(vir_parts)])  2.61 us
    pallas_call x5, Pallas kernels, call(): pl.pallas_call(kernel, out_shape=outs, in_specs=[pl.BlockSpec(memory_spac...  2.24 us
    unnamed x8, local copies, waits for them, and re-layouts  1.51 us
  transfers between devices with their start and end apart: 6, of which 4 were waited for; matrix products, arithmetic and copies ran while one was open for 0% of the time, Pallas kernels for 1%

profile of v3, /device:TPU:0, one launch (start us, length us, event | category | flops | bytes accessed | tf_op | source)
XLA Modules:
  0.0 25.9 jit_solution(7115516449698461462)
XLA Ops:
  0.0 0.0 copy-start.1
  0.0 0.0 copy-start
  0.0 0.7 %copy-done.1 = bf16[256,32]{0,1:T(8,128)(2,1)S(1)} copy-done((bf16[256,32]{0,1:T(8,128)(2,1)S(1)}, bf16[256,32]{0,1:T(8,128)(2,1)}, u32[]{:S(2)}) %copy-start.1) | copy-done | bytes 16408
  0.7 0.1 copy-done
  0.9 0.3 %shard_map.47 = bf16[8,96,128]{2,1,0:T(8,128)(2,1)S(1)} custom-call(bf16[64,512]{1,0:T(8,128)(2,1)S(1)} %copy-done, bf16[32,256]{1,0:T(8,128)(2,1)S(1)} %bitcast.3, s32[1,512]{1,0:T(1,128)S(1)} %shard_map.46.source_ref), custom_call_target="tpu_custom_call" | custom-call | flops 33554432 | bytes 280576 | tf_op jit(solution)/shard_map/pallas_call | solution.py:175
  1.1 15.0 %all_to_all.5.refs_0_.got_ref = bf16[8,96,128]{2,1,0:T(8,128)(2,1)S(1)} all-to-all(bf16[8,96,128]{2,1,0:T(8,128)(2,1)S(1)} %shard_map.47), channel_id=1, replica_groups=mesh['vv'=4,'oo'=8] {'oo'}, dimensions={0} | all-to-all | bytes 393216 | tf_op jit(solution)/shard_map/all_to_all | solution.py:218
  16.2 0.4 %shard_map.49 = (bf16[512,128]{1,0:T(8,128)(2,1)S(1)}, bf16[512,128]{1,0:T(8,128)(2,1)S(1)}) custom-call(bf16[8,96,128]{2,1,0:T(8,128)(2,1)S(1)} %all_to_all.5.refs_0_.got_ref), custom_call_target="tpu_custom_call" | custom-call | flops 67108864 | bytes 458752 | tf_op jit(solution)/shard_map/pallas_call | solution.py:175
  16.6 1.6 %collective-permute-start.4 = (bf16[512,128]{1,0:T(8,128)(2,1)S(1)}, bf16[512,128]{1,0:T(8,128)(2,1)S(1)}, u32[]{:S(2)}, u32[]{:S(2)}) collective-permute-start(bf16[512,128]{1,0:T(8,128)(2,1)S(1)} %get-tuple-element.14), channel_id=1, source_target_pairs={{0,16},{8,24},{16,0},{24,8},{1,17},{9,25},{17,1},{25,9},{2,18},{10... | collective-permute-start | bytes 393224 | tf_op jit(solution)/shard_map/ppermute | solution.py:198
  18.1 0.5 %collective-permute-start.1 = (bf16[64,512]{1,0:T(8,128)(2,1)S(1)}, bf16[64,512]{1,0:T(8,128)(2,1)S(1)}, u32[]{:S(2)}, u32[]{:S(2)}) collective-permute-start(bf16[64,512]{1,0:T(8,128)(2,1)S(1)} %copy-done), channel_id=1, source_target_pairs={{0,16},{8,24},{16,0},{24,8},{1,17},{9,25},{17,1},{25,9},{2,18},{10... | collective-permute-start | bytes 196616 | tf_op jit(solution)/shard_map/ppermute | solution.py:198
  18.7 0.0 collective-permute-start.3
  18.7 2.9 %collective-permute-done.4.refs_5_ = bf16[512,128]{1,0:T(8,128)(2,1)S(1)} collective-permute-done((bf16[512,128]{1,0:T(8,128)(2,1)S(1)}, bf16[512,128]{1,0:T(8,128)(2,1)S(1)}, u32[]{:S(2)}, u32[]{:S(2)}) %collective-permute-start.4) | collective-permute-done | bytes 131104 | tf_op jit(solution)/shard_map/ppermute | solution.py:198
  21.6 0.0 collective-permute-start.5
  21.6 0.5 %collective-permute-start = (bf16[64,512]{1,0:T(8,128)(2,1)S(1)}, bf16[64,512]{1,0:T(8,128)(2,1)S(1)}, u32[]{:S(2)}, u32[]{:S(2)}) collective-permute-start(bf16[64,512]{1,0:T(8,128)(2,1)S(1)} %copy-done), channel_id=1, source_target_pairs={{0,8},{8,0},{16,24},{24,16},{1,9},{9,1},{17,25},{25,17},{2,10},{10... | collective-permute-start | bytes 196616 | tf_op jit(solution)/shard_map/ppermute | solution.py:198
  22.1 0.3 %collective-permute-done.1.refs_5_ = bf16[64,512]{1,0:T(8,128)(2,1)S(1)} collective-permute-done((bf16[64,512]{1,0:T(8,128)(2,1)S(1)}, bf16[64,512]{1,0:T(8,128)(2,1)S(1)}, u32[]{:S(2)}, u32[]{:S(2)}) %collective-permute-start.1) | collective-permute-done | bytes 65568 | tf_op jit(solution)/shard_map/ppermute | solution.py:198
  22.4 0.0 collective-permute-start.2
  22.4 0.6 %collective-permute-done.refs_4_ = bf16[64,512]{1,0:T(8,128)(2,1)S(1)} collective-permute-done((bf16[64,512]{1,0:T(8,128)(2,1)S(1)}, bf16[64,512]{1,0:T(8,128)(2,1)S(1)}, u32[]{:S(2)}, u32[]{:S(2)}) %collective-permute-start) | collective-permute-done | bytes 65568 | tf_op jit(solution)/shard_map/ppermute | solution.py:198
  23.0 0.6 %collective-permute-done.2.refs_6_ = bf16[64,512]{1,0:T(8,128)(2,1)S(1)} collective-permute-done((bf16[64,512]{1,0:T(8,128)(2,1)S(1)}, bf16[64,512]{1,0:T(8,128)(2,1)S(1)}, u32[]{:S(2)}, u32[]{:S(2)}) %collective-permute-start.2) | collective-permute-done | bytes 65568 | tf_op jit(solution)/shard_map/ppermute | solution.py:198
  23.7 0.0 copy-start.2
  23.7 0.7 %copy-done.2 = f32[64]{0:T(128)S(1)} copy-done((f32[64]{0:T(128)S(1)}, f32[64]{0:T(128)}, u32[]{:S(2)}) %copy-start.2) | copy-done | bytes 280
  24.3 0.0 copy-done.3
  24.3 0.3 %shard_map.48 = (bf16[256,512]{1,0:T(8,128)(2,1)S(1)}, f32[256,512]{1,0:T(8,128)S(1)}, bf16[256,512]{1,0:T(8,128)(2,1)S(1)}) custom-call(bf16[8,96,128]{2,1,0:T(8,128)(2,1)S(1)} %all_to_all.5.refs_0_.got_ref, f32[1,64]{1,0:T(1,128)S(1)} %bitcast.4, f32[1,32]{1,0:T(1,128)S(1)} %bitcast.5, bf16[64,512]{1,0:T(8,128)(2,1)S(1)} %copy-done, ...), custom_call_target="tpu_custom_call" | custom-call | flops 67108864 | bytes 1507712 | tf_op jit(solution)/shard_map/pallas_call | solution.py:175
  24.7 0.0 collective-permute-done.3.refs_4_
  24.7 0.0 collective-permute-done.5.refs_6_
  24.7 1.2 %shard_map.50 = bf16[256,512]{1,0:T(8,128)(2,1)} custom-call(bf16[256,512]{1,0:T(8,128)(2,1)S(1)} %get-tuple-element.10.refs_0_, f32[256,512]{1,0:T(8,128)S(1)} %get-tuple-element.11.refs_1_, bf16[256,512]{1,0:T(8,128)(2,1)S(1)} %get-tuple-element.12.refs_2_, bf16[512,128]{1,0:T(8,128)(2,1)S(1)} %get-tuple-element.13.refs_3_, ...), custom_call_target="tpu_custom_call" | custom-call | flops 134217728 | bytes 1835008 | tf_op jit(solution)/shard_map/pallas_call | solution.py:175
  (2 shorter events, 0.0 us)
Async XLA Ops:
  0.0 0.7 %copy-start.1 = (bf16[256,32]{0,1:T(8,128)(2,1)S(1)}, bf16[256,32]{0,1:T(8,128)(2,1)}, u32[]{:S(2)}) copy-start(bf16[256,32]{0,1:T(8,128)(2,1)} %param.4) | copy-start | bytes 49156
  0.0 0.9 %copy-start = (bf16[64,512]{1,0:T(8,128)(2,1)S(1)}, bf16[64,512]{1,0:T(8,128)(2,1)}, u32[]{:S(2)}) copy-start(bf16[64,512]{1,0:T(8,128)(2,1)} %refs_3_.1) | copy-start | bytes 196612
  16.6 5.0 %collective-permute-start.4 = (bf16[512,128]{1,0:T(8,128)(2,1)S(1)}, bf16[512,128]{1,0:T(8,128)(2,1)S(1)}, u32[]{:S(2)}, u32[]{:S(2)}) collective-permute-start(bf16[512,128]{1,0:T(8,128)(2,1)S(1)} %get-tuple-element.14), channel_id=1, source_target_pairs={{0,16},{8,24},{16,0},{24,8},{1,17},{9,25},{17,1},{25,9},{2,18},{10... | collective-permute-start | bytes 393224 | tf_op jit(solution)/shard_map/ppermute | solution.py:198
  18.1 4.3 %collective-permute-start.1 = (bf16[64,512]{1,0:T(8,128)(2,1)S(1)}, bf16[64,512]{1,0:T(8,128)(2,1)S(1)}, u32[]{:S(2)}, u32[]{:S(2)}) collective-permute-start(bf16[64,512]{1,0:T(8,128)(2,1)S(1)} %copy-done), channel_id=1, source_target_pairs={{0,16},{8,24},{16,0},{24,8},{1,17},{9,25},{17,1},{25,9},{2,18},{10... | collective-permute-start | bytes 196616 | tf_op jit(solution)/shard_map/ppermute | solution.py:198
  18.7 6.0 %collective-permute-start.3 = (bf16[512,128]{1,0:T(8,128)(2,1)S(1)}, bf16[512,128]{1,0:T(8,128)(2,1)S(1)}, u32[]{:S(2)}, u32[]{:S(2)}) collective-permute-start(bf16[512,128]{1,0:T(8,128)(2,1)S(1)} %get-tuple-element.13.refs_3_), channel_id=1, source_target_pairs={{0,8},{8,0},{16,24},{24,16},{1,9},{9,1},{17,25},{25,17},{2,10},{10... | collective-permute-start | bytes 393224 | tf_op jit(solution)/shard_map/ppermute | solution.py:198
  21.6 3.1 %collective-permute-start.5 = (bf16[512,128]{1,0:T(8,128)(2,1)S(1)}, bf16[512,128]{1,0:T(8,128)(2,1)S(1)}, u32[]{:S(2)}, u32[]{:S(2)}) collective-permute-start(bf16[512,128]{1,0:T(8,128)(2,1)S(1)} %collective-permute-done.4.refs_5_), channel_id=1, source_target_pairs={{0,8},{8,0},{16,24},{24,16},{1,9},{9,1},{17,25},{25,17},{2,10},{10... | collective-permute-start | bytes 393224 | tf_op jit(solution)/shard_map/ppermute | solution.py:198
  21.6 1.4 %collective-permute-start = (bf16[64,512]{1,0:T(8,128)(2,1)S(1)}, bf16[64,512]{1,0:T(8,128)(2,1)S(1)}, u32[]{:S(2)}, u32[]{:S(2)}) collective-permute-start(bf16[64,512]{1,0:T(8,128)(2,1)S(1)} %copy-done), channel_id=1, source_target_pairs={{0,8},{8,0},{16,24},{24,16},{1,9},{9,1},{17,25},{25,17},{2,10},{10... | collective-permute-start | bytes 196616 | tf_op jit(solution)/shard_map/ppermute | solution.py:198
  22.4 1.3 %collective-permute-start.2 = (bf16[64,512]{1,0:T(8,128)(2,1)S(1)}, bf16[64,512]{1,0:T(8,128)(2,1)S(1)}, u32[]{:S(2)}, u32[]{:S(2)}) collective-permute-start(bf16[64,512]{1,0:T(8,128)(2,1)S(1)} %collective-permute-done.1.refs_5_), channel_id=1, source_target_pairs={{0,8},{8,0},{16,24},{24,16},{1,9},{9,1},{17,25},{25,17},{2,10},{10... | collective-permute-start | bytes 196616 | tf_op jit(solution)/shard_map/ppermute | solution.py:198
  23.7 0.7 %copy-start.2 = (f32[64]{0:T(128)S(1)}, f32[64]{0:T(128)}, u32[]{:S(2)}) copy-start(f32[64]{0:T(128)} %param.6) | copy-start | bytes 772
  23.7 0.7 %copy-start.3 = (f32[32]{0:T(128)S(1)}, f32[32]{0:T(128)}, u32[]{:S(2)}) copy-start(f32[32]{0:T(128)} %param.7) | copy-start | bytes 388

commit v4 on v3

--- a/solution.py
+++ b/solution.py
@@ -8,7 +8,7 @@
 from jax.sharding import PartitionSpec as P
 
 
-LANES = 128
+LANES, STORES = 128, 2
 LEAST, MOST = 8 << 20, 60 << 20
 CHOOSE_FLOPS = 10**9
 F32 = jnp.float32
@@ -20,6 +20,20 @@
     n = source.shape[1]
     pick = lax.broadcasted_iota(jnp.int32, (rows, n), 0) == source
     return jnp.where(pick, 1.0, 0.0).astype(BF16)
+
+
+def middle_out(n):
+    half, chunk = n // 2, max(1, n // 4)
+    up, down = list(range(half, n)), list(reversed(range(half)))
+    order = []
+    for at in range(0, max(len(up), len(down)), chunk):
+        order += up[at : at + chunk] + down[at : at + chunk]
+    return order
+
+
+def places(n):
+    order = middle_out(n)
+    return [order.index(k) for k in range(n)]
 
 
 def columns(n):
@@ -41,12 +55,12 @@
     moved = jnp.dot(t_ref[...], one_hot(cols, source_ref[...]), preferred_element_type=F32)
     fold = lanes // square
     high = depth // fold
-    for part in range(parts):
+    for at, part in enumerate(middle_out(parts)):
         piece = [
             moved[h * high : (h + 1) * high, part * square : (part + 1) * square]
             for h in range(fold)
         ]
-        out_ref[part, :high, :] = jnp.concatenate(piece, axis=1).astype(BF16)
+        out_ref[at, :high, :] = jnp.concatenate(piece, axis=1).astype(BF16)
     deep = v_ref.shape[0]
     for chunk in range((rows - high) // deep):
         block = v_ref[:, chunk * lanes : (chunk + 1) * lanes]
@@ -55,10 +69,13 @@
 
 
 def integral_columns(got_ref, high, deep):
-    parts, rows, lanes = got_ref.shape
+    parts, rows, _ = got_ref.shape
     return jnp.concatenate(
         [
-            got_ref[:, high + c * deep : high + (c + 1) * deep, :].reshape(parts * deep, lanes)
+            jnp.concatenate(
+                [got_ref[at, high + c * deep : high + (c + 1) * deep, :] for at in places(parts)],
+                axis=0,
+            )
             for c in range((rows - high) // deep)
         ],
         axis=1,
@@ -74,7 +91,7 @@
     packed = got_ref[:, :high, :].astype(F32)
     halves = [
         jnp.concatenate(
-            [packed[part, :, h * square : (h + 1) * square] for part in range(parts)], axis=1
+            [packed[at, :, h * square : (h + 1) * square] for at in places(parts)], axis=1
         )
         for h in range(fold)
     ]
@@ -105,7 +122,7 @@
 
 def direct_kernel(sizes, *refs):
     vir_parts, vir_own, occ_own, high, deep, width = sizes
-    got_ref, occ_ref, vir_ref, *amp_refs, lad_ref, den_ref, sel_ref, all_ref = refs
+    got_ref, occ_ref, vir_ref, *amp_refs, lad_ref, inv_ref, sel_ref, all_ref = refs
     me = lax.axis_index("vv")
     depth = amp_refs[0].shape[0]
     for rel, ref in enumerate(amp_refs):
@@ -115,7 +132,7 @@
     lad_ref[...] = lax.dot_general(
         ints, all_ref[...], (((0,), (0,)), ((), ())), preferred_element_type=F32
     ).astype(BF16)
-    rows, cols = den_ref.shape
+    rows, cols = inv_ref.shape
     vir_all, occ_all = vir_parts * vir_own, occ_ref.shape[1]
     occ = occ_ref[...]
     occ_column = pick_sum(occ, square_eye(occ_all), 1)
@@ -127,7 +144,7 @@
     vir = vir_ref[...]
     vir_mine = pick_sum(vir, lane == me * vir_own + row // vir_all, 1)
     vir_other = pick_sum(vir, lane == row % vir_all, 1)
-    den_ref[...] = occ_pair - vir_mine - vir_other
+    inv_ref[...] = 1.0 / (occ_pair - vir_mine - vir_other)
     n, area = sel_ref.shape[1], vir_own * vir_own
     rel = jnp.bitwise_xor(row % vir_all // vir_own, me)
     source = rel * width + (rel % (width // area)) * area + row // vir_all * vir_own + row % vir_own
@@ -144,9 +161,9 @@
 
 def mirror_kernel(sizes, *refs):
     depth, total, width = sizes
-    lad_ref, den_ref, sel_ref, *got_refs, out_ref, all_ref = refs
+    lad_ref, inv_ref, sel_ref, *got_refs, out_hbm, all_ref, out_ref, sems = refs
     me = lax.axis_index("vv")
-    _, cols = out_ref.shape
+    rows, cols = out_ref.shape
     chunks = cols // LANES
     for rel, ref in enumerate(got_refs):
         at = pl.multiple_of(jnp.bitwise_xor(me, rel) * depth, depth)
@@ -164,19 +181,30 @@
     rows_mirrored = lax.dot_general(
         sel_ref[...], ints, (((1,), (1,)), ((), ())), preferred_element_type=F32
     ).astype(BF16)
-    mirrored = jnp.dot(rows_mirrored, all_ref[...], preferred_element_type=F32).astype(BF16)
-    total_sum = lad_ref[...].astype(F32) + mirrored.astype(F32)
-    out_ref[...] = (total_sum / den_ref[...]).astype(BF16)
-
-
-def call(kernel, outs, args, scratch=(), flops=0, space=VMEM):
+    pieces = sems.shape[0]
+    size = rows // pieces
+    stores = []
+    for piece in range(pieces):
+        some = slice(piece * size, (piece + 1) * size)
+        mirrored = jnp.dot(rows_mirrored[some], all_ref[...], preferred_element_type=F32)
+        both = lad_ref[some, :].astype(F32) + mirrored.astype(BF16).astype(F32)
+        out_ref[some, :] = (both * inv_ref[some, :]).astype(BF16)
+        stores.append(
+            pltpu.make_async_copy(out_ref.at[some, :], out_hbm.at[some, :], sems.at[piece])
+        )
+        stores[-1].start()
+    for store in stores:
+        store.wait()
+
+
+def call(kernel, outs, args, scratch=(), flops=0, out_space=VMEM):
     outs = tuple(outs)
     moved = sum(x.size * x.dtype.itemsize for x in (*args, *outs))
     result = pl.pallas_call(
         kernel,
         out_shape=outs,
-        in_specs=[pl.BlockSpec(memory_space=space)] * len(args),
-        out_specs=tuple(pl.BlockSpec(memory_space=VMEM) for _ in outs),
+        in_specs=[pl.BlockSpec(memory_space=VMEM)] * len(args),
+        out_specs=tuple(pl.BlockSpec(memory_space=out_space) for _ in outs),
         scratch_shapes=list(scratch),
         compiler_params=pltpu.CompilerParams(vmem_limit_bytes=min(MOST, LEAST + 3 * moved)),
         cost_estimate=pl.CostEstimate(flops=flops, bytes_accessed=moved, transcendentals=0),
@@ -215,7 +243,7 @@
         (amplitudes, integrals.T, source),
         flops=2 * depth * cols * cols,
     )
-    got = lax.all_to_all(packed, "oo", 0, 0, tiled=True)
+    got = lax.all_to_all(packed, "oo", 0, 0, tiled=True, axis_index_groups=[middle_out(occ_parts)])
 
     amp_rows = cols // LANES * depth
     send_shape = jax.ShapeDtypeStruct((amp_rows + widths[0] // LANES * total, LANES), BF16)
@@ -242,7 +270,7 @@
             held = {k: (x, x) for k, x in arrived.items()}
     order = range(vir_parts)
 
-    ladder, denom, to_rows = call(
+    ladder, inverse, to_rows = call(
         functools.partial(direct_kernel, (vir_parts, vir_own, occ_own, high, deep, width)),
         [
             jax.ShapeDtypeStruct((rows, cols), BF16),
@@ -261,9 +289,14 @@
     (update,) = call(
         functools.partial(mirror_kernel, (depth, total, width)),
         [jax.ShapeDtypeStruct((rows, cols), BF16)],
-        (ladder, denom, to_rows, *(arrived[k] for k in order)),
-        scratch=[pltpu.VMEM((total, cols), BF16)],
+        (ladder, inverse, to_rows, *(arrived[k] for k in order)),
+        scratch=[
+            pltpu.VMEM((total, cols), BF16),
+            pltpu.VMEM((rows, cols), BF16),
+            pltpu.SemaphoreType.DMA((STORES,)),
+        ],
         flops=2 * rows * total * cols * 2,
+        out_space=pl.ANY,
     )
     return update
 

time: 26.2 us -> 23.9 us (0.912)
  blocking collectives: 15 us -> 12.7 us
    all_to_all x1, blocking collectives: 15 us -> 12.7 us  [on_device(): lax.all_to_all(packed, 'oo', 0, 0, tiled=True, axis_index_groups=[middle_...]
  transfers between devices with their start and end apart: 6 -> 6, of which waited for: 4 -> 4; matrix products, arithmetic and copies ran while one was open for 0% -> 0% of each run, Pallas kernels for 1% -> 2%
where the time goes in v4:
time: 23.9 us; the launch traced here: 23.6 us
  blocking collectives  12.7 us (53%)
  waiting for transfers between devices  4.5 us (19%)
  starting transfers between devices  2.61 us (11%)
  Pallas kernels  2.23 us (9%)
  local copies, waits for them, and re-layouts  1.51 us (6%)
    all_to_all x1, blocking collectives, on_device(): lax.all_to_all(packed, 'oo', 0, 0, tiled=True, axis_index_groups=[middle_...  12.7 us
    ppermute x6, waiting for transfers between devices, swap(): return lax.ppermute(x, 'vv', [(k, k ^ step) for k in range(vir_parts)])  4.5 us
    ppermute x6, starting transfers between devices, swap(): return lax.ppermute(x, 'vv', [(k, k ^ step) for k in range(vir_parts)])  2.61 us
    pallas_call x5, Pallas kernels, call(): pl.pallas_call(kernel, out_shape=outs, in_specs=[pl.BlockSpec(memory_spac...  2.23 us
    unnamed x8, local copies, waits for them, and re-layouts  1.51 us
  transfers between devices with their start and end apart: 6, of which 4 were waited for; matrix products, arithmetic and copies ran while one was open for 0% of the time, Pallas kernels for 2%

profile of v4, /device:TPU:0, one launch (start us, length us, event | category | flops | bytes accessed | tf_op | source)
XLA Modules:
  0.0 23.6 jit_solution(12034784810013596641)
XLA Ops:
  0.0 0.0 copy-start.1
  0.0 0.0 copy-start
  0.0 0.7 %copy-done.1 = bf16[256,32]{0,1:T(8,128)(2,1)S(1)} copy-done((bf16[256,32]{0,1:T(8,128)(2,1)S(1)}, bf16[256,32]{0,1:T(8,128)(2,1)}, u32[]{:S(2)}) %copy-start.1) | copy-done | bytes 16408
  0.7 0.1 copy-done
  0.9 0.3 %shard_map.47 = bf16[8,96,128]{2,1,0:T(8,128)(2,1)S(1)} custom-call(bf16[64,512]{1,0:T(8,128)(2,1)S(1)} %copy-done, bf16[32,256]{1,0:T(8,128)(2,1)S(1)} %bitcast.3, s32[1,512]{1,0:T(1,128)S(1)} %shard_map.46.source_ref), custom_call_target="tpu_custom_call" | custom-call | flops 33554432 | bytes 280576 | tf_op jit(solution)/shard_map/pallas_call | solution.py:203
  1.1 12.7 %all_to_all.5.refs_0_.got_ref = bf16[8,96,128]{2,1,0:T(8,128)(2,1)S(1)} all-to-all(bf16[8,96,128]{2,1,0:T(8,128)(2,1)S(1)} %shard_map.47), channel_id=1, replica_groups={{4,5,3,2,6,7,1,0},{12,13,11,10,14,15,9,8},{20,21,19,18,22,23,17,16},{28..., dimensions={0} | all-to-all | bytes 393216 | tf_op jit(solution)/shard_map/all_to_all | solution.py:246
  13.8 0.4 %shard_map.49 = (bf16[512,128]{1,0:T(8,128)(2,1)S(1)}, bf16[512,128]{1,0:T(8,128)(2,1)S(1)}) custom-call(bf16[8,96,128]{2,1,0:T(8,128)(2,1)S(1)} %all_to_all.5.refs_0_.got_ref), custom_call_target="tpu_custom_call" | custom-call | flops 67108864 | bytes 458752 | tf_op jit(solution)/shard_map/pallas_call | solution.py:203
  14.2 1.6 %collective-permute-start.4 = (bf16[512,128]{1,0:T(8,128)(2,1)S(1)}, bf16[512,128]{1,0:T(8,128)(2,1)S(1)}, u32[]{:S(2)}, u32[]{:S(2)}) collective-permute-start(bf16[512,128]{1,0:T(8,128)(2,1)S(1)} %get-tuple-element.14), channel_id=1, source_target_pairs={{0,16},{8,24},{16,0},{24,8},{1,17},{9,25},{17,1},{25,9},{2,18},{10... | collective-permute-start | bytes 393224 | tf_op jit(solution)/shard_map/ppermute | solution.py:226
  15.8 0.5 %collective-permute-start.1 = (bf16[64,512]{1,0:T(8,128)(2,1)S(1)}, bf16[64,512]{1,0:T(8,128)(2,1)S(1)}, u32[]{:S(2)}, u32[]{:S(2)}) collective-permute-start(bf16[64,512]{1,0:T(8,128)(2,1)S(1)} %copy-done), channel_id=1, source_target_pairs={{0,16},{8,24},{16,0},{24,8},{1,17},{9,25},{17,1},{25,9},{2,18},{10... | collective-permute-start | bytes 196616 | tf_op jit(solution)/shard_map/ppermute | solution.py:226
  16.3 0.0 collective-permute-start.3
  16.3 2.9 %collective-permute-done.4.refs_5_ = bf16[512,128]{1,0:T(8,128)(2,1)S(1)} collective-permute-done((bf16[512,128]{1,0:T(8,128)(2,1)S(1)}, bf16[512,128]{1,0:T(8,128)(2,1)S(1)}, u32[]{:S(2)}, u32[]{:S(2)}) %collective-permute-start.4) | collective-permute-done | bytes 131104 | tf_op jit(solution)/shard_map/ppermute | solution.py:226
  19.3 0.0 collective-permute-start.5
  19.3 0.5 %collective-permute-start = (bf16[64,512]{1,0:T(8,128)(2,1)S(1)}, bf16[64,512]{1,0:T(8,128)(2,1)S(1)}, u32[]{:S(2)}, u32[]{:S(2)}) collective-permute-start(bf16[64,512]{1,0:T(8,128)(2,1)S(1)} %copy-done), channel_id=1, source_target_pairs={{0,8},{8,0},{16,24},{24,16},{1,9},{9,1},{17,25},{25,17},{2,10},{10... | collective-permute-start | bytes 196616 | tf_op jit(solution)/shard_map/ppermute | solution.py:226
  19.8 0.3 %collective-permute-done.1.refs_5_ = bf16[64,512]{1,0:T(8,128)(2,1)S(1)} collective-permute-done((bf16[64,512]{1,0:T(8,128)(2,1)S(1)}, bf16[64,512]{1,0:T(8,128)(2,1)S(1)}, u32[]{:S(2)}, u32[]{:S(2)}) %collective-permute-start.1) | collective-permute-done | bytes 65568 | tf_op jit(solution)/shard_map/ppermute | solution.py:226
  20.1 0.0 collective-permute-start.2
  20.1 0.6 %collective-permute-done.refs_4_ = bf16[64,512]{1,0:T(8,128)(2,1)S(1)} collective-permute-done((bf16[64,512]{1,0:T(8,128)(2,1)S(1)}, bf16[64,512]{1,0:T(8,128)(2,1)S(1)}, u32[]{:S(2)}, u32[]{:S(2)}) %collective-permute-start) | collective-permute-done | bytes 65568 | tf_op jit(solution)/shard_map/ppermute | solution.py:226
  20.7 0.6 %collective-permute-done.2.refs_6_ = bf16[64,512]{1,0:T(8,128)(2,1)S(1)} collective-permute-done((bf16[64,512]{1,0:T(8,128)(2,1)S(1)}, bf16[64,512]{1,0:T(8,128)(2,1)S(1)}, u32[]{:S(2)}, u32[]{:S(2)}) %collective-permute-start.2) | collective-permute-done | bytes 65568 | tf_op jit(solution)/shard_map/ppermute | solution.py:226
  21.3 0.0 copy-start.2
  21.3 0.7 %copy-done.2 = f32[64]{0:T(128)S(1)} copy-done((f32[64]{0:T(128)S(1)}, f32[64]{0:T(128)}, u32[]{:S(2)}) %copy-start.2) | copy-done | bytes 280
  22.0 0.0 copy-done.3
  22.0 0.4 %shard_map.48 = (bf16[256,512]{1,0:T(8,128)(2,1)S(1)}, f32[256,512]{1,0:T(8,128)S(1)}, bf16[256,512]{1,0:T(8,128)(2,1)S(1)}) custom-call(bf16[8,96,128]{2,1,0:T(8,128)(2,1)S(1)} %all_to_all.5.refs_0_.got_ref, f32[1,64]{1,0:T(1,128)S(1)} %bitcast.4, f32[1,32]{1,0:T(1,128)S(1)} %bitcast.5, bf16[64,512]{1,0:T(8,128)(2,1)S(1)} %copy-done, ...), custom_call_target="tpu_custom_call" | custom-call | flops 67108864 | bytes 1507712 | tf_op jit(solution)/shard_map/pallas_call | solution.py:203
  22.4 0.0 collective-permute-done.3.refs_4_
  22.4 0.0 collective-permute-done.5.refs_6_
  22.4 1.2 %shard_map.50 = bf16[256,512]{1,0:T(8,128)(2,1)} custom-call(bf16[256,512]{1,0:T(8,128)(2,1)S(1)} %get-tuple-element.10.refs_0_, f32[256,512]{1,0:T(8,128)S(1)} %get-tuple-element.11.refs_1_, bf16[256,512]{1,0:T(8,128)(2,1)S(1)} %get-tuple-element.12.refs_2_, bf16[512,128]{1,0:T(8,128)(2,1)S(1)} %get-tuple-element.13.refs_3_, ...), custom_call_target="tpu_custom_call" | custom-call | flops 134217728 | bytes 1835008 | tf_op jit(solution)/shard_map/pallas_call | solution.py:203
  (2 shorter events, 0.0 us)
Async XLA Ops:
  0.0 0.7 %copy-start.1 = (bf16[256,32]{0,1:T(8,128)(2,1)S(1)}, bf16[256,32]{0,1:T(8,128)(2,1)}, u32[]{:S(2)}) copy-start(bf16[256,32]{0,1:T(8,128)(2,1)} %param.4) | copy-start | bytes 49156
  0.0 0.9 %copy-start = (bf16[64,512]{1,0:T(8,128)(2,1)S(1)}, bf16[64,512]{1,0:T(8,128)(2,1)}, u32[]{:S(2)}) copy-start(bf16[64,512]{1,0:T(8,128)(2,1)} %refs_3_.1) | copy-start | bytes 196612
  14.2 5.0 %collective-permute-start.4 = (bf16[512,128]{1,0:T(8,128)(2,1)S(1)}, bf16[512,128]{1,0:T(8,128)(2,1)S(1)}, u32[]{:S(2)}, u32[]{:S(2)}) collective-permute-start(bf16[512,128]{1,0:T(8,128)(2,1)S(1)} %get-tuple-element.14), channel_id=1, source_target_pairs={{0,16},{8,24},{16,0},{24,8},{1,17},{9,25},{17,1},{25,9},{2,18},{10... | collective-permute-start | bytes 393224 | tf_op jit(solution)/shard_map/ppermute | solution.py:226
  15.8 4.3 %collective-permute-start.1 = (bf16[64,512]{1,0:T(8,128)(2,1)S(1)}, bf16[64,512]{1,0:T(8,128)(2,1)S(1)}, u32[]{:S(2)}, u32[]{:S(2)}) collective-permute-start(bf16[64,512]{1,0:T(8,128)(2,1)S(1)} %copy-done), channel_id=1, source_target_pairs={{0,16},{8,24},{16,0},{24,8},{1,17},{9,25},{17,1},{25,9},{2,18},{10... | collective-permute-start | bytes 196616 | tf_op jit(solution)/shard_map/ppermute | solution.py:226
  16.3 6.1 %collective-permute-start.3 = (bf16[512,128]{1,0:T(8,128)(2,1)S(1)}, bf16[512,128]{1,0:T(8,128)(2,1)S(1)}, u32[]{:S(2)}, u32[]{:S(2)}) collective-permute-start(bf16[512,128]{1,0:T(8,128)(2,1)S(1)} %get-tuple-element.13.refs_3_), channel_id=1, source_target_pairs={{0,8},{8,0},{16,24},{24,16},{1,9},{9,1},{17,25},{25,17},{2,10},{10... | collective-permute-start | bytes 393224 | tf_op jit(solution)/shard_map/ppermute | solution.py:226
  19.3 3.1 %collective-permute-start.5 = (bf16[512,128]{1,0:T(8,128)(2,1)S(1)}, bf16[512,128]{1,0:T(8,128)(2,1)S(1)}, u32[]{:S(2)}, u32[]{:S(2)}) collective-permute-start(bf16[512,128]{1,0:T(8,128)(2,1)S(1)} %collective-permute-done.4.refs_5_), channel_id=1, source_target_pairs={{0,8},{8,0},{16,24},{24,16},{1,9},{9,1},{17,25},{25,17},{2,10},{10... | collective-permute-start | bytes 393224 | tf_op jit(solution)/shard_map/ppermute | solution.py:226
  19.3 1.4 %collective-permute-start = (bf16[64,512]{1,0:T(8,128)(2,1)S(1)}, bf16[64,512]{1,0:T(8,128)(2,1)S(1)}, u32[]{:S(2)}, u32[]{:S(2)}) collective-permute-start(bf16[64,512]{1,0:T(8,128)(2,1)S(1)} %copy-done), channel_id=1, source_target_pairs={{0,8},{8,0},{16,24},{24,16},{1,9},{9,1},{17,25},{25,17},{2,10},{10... | collective-permute-start | bytes 196616 | tf_op jit(solution)/shard_map/ppermute | solution.py:226
  20.1 1.3 %collective-permute-start.2 = (bf16[64,512]{1,0:T(8,128)(2,1)S(1)}, bf16[64,512]{1,0:T(8,128)(2,1)S(1)}, u32[]{:S(2)}, u32[]{:S(2)}) collective-permute-start(bf16[64,512]{1,0:T(8,128)(2,1)S(1)} %collective-permute-done.1.refs_5_), channel_id=1, source_target_pairs={{0,8},{8,0},{16,24},{24,16},{1,9},{9,1},{17,25},{25,17},{2,10},{10... | collective-permute-start | bytes 196616 | tf_op jit(solution)/shard_map/ppermute | solution.py:226
  21.3 0.7 %copy-start.2 = (f32[64]{0:T(128)S(1)}, f32[64]{0:T(128)}, u32[]{:S(2)}) copy-start(f32[64]{0:T(128)} %param.6) | copy-start | bytes 772
  21.3 0.7 %copy-start.3 = (f32[32]{0:T(128)S(1)}, f32[32]{0:T(128)}, u32[]{:S(2)}) copy-start(f32[32]{0:T(128)} %param.7) | copy-start | bytes 388

commit v5 on v4

--- a/solution.py
+++ b/solution.py
@@ -27,7 +27,7 @@
     up, down = list(range(half, n)), list(reversed(range(half)))
     order = []
     for at in range(0, max(len(up), len(down)), chunk):
-        order += up[at : at + chunk] + down[at : at + chunk]
+        order += sorted(up[at : at + chunk], reverse=at > 0) + down[at : at + chunk]
     return order
 
 
@@ -82,47 +82,65 @@
     )
 
 
-def split_kernel(sizes, got_ref, send_ref, keep_ref):
-    vir_parts, vir_own, occ_own, high, deep, kept = sizes
+def split_kernel(occ_own, high, deep, got_ref, amp_ref, int_ref, send_ref, keep_ref):
     parts, _, lanes = got_ref.shape
     square = occ_own * occ_own
-    fold = lanes // square
     cols = parts * square
     packed = got_ref[:, :high, :].astype(F32)
     halves = [
         jnp.concatenate(
             [packed[at, :, h * square : (h + 1) * square] for at in places(parts)], axis=1
         )
-        for h in range(fold)
+        for h in range(lanes // square)
     ]
     amps = jnp.concatenate(halves, axis=0).astype(BF16)
-    col, occ_all = columns(cols), parts * occ_own
-    source = (col % occ_all // occ_own) * square + (col % occ_own) * occ_own + col // occ_all
-    amps = jnp.dot(amps, one_hot(cols, source), preferred_element_type=F32).astype(BF16)
-    depth = amps.shape[0]
-    chunks = cols // lanes
-    for c in range(chunks):
-        block = amps[:, c * lanes : (c + 1) * lanes]
-        send_ref[c * depth : (c + 1) * depth, :] = block
-        keep_ref[c * depth : (c + 1) * depth, :] = block
+    amps = jnp.dot(amps, amp_ref[...], preferred_element_type=F32).astype(BF16)
     ints = integral_columns(got_ref, high, deep)
     total, rows = ints.shape
-    col, area = columns(rows), vir_own * vir_own
-    owner = jnp.bitwise_xor(col // area, lax.axis_index("vv"))
-    source = (col % vir_own) * (vir_parts * vir_own) + owner * vir_own + col % area // vir_own
-    ints = jnp.dot(ints, one_hot(rows, source), preferred_element_type=F32).astype(BF16)
-    base = chunks * depth
-    for c in range(kept):
-        keep_ref[base + c * total : base + (c + 1) * total, :] = ints[:, c * lanes : (c + 1) * lanes]
-    first = rows // lanes - (send_ref.shape[0] - base) // total
-    for c in range(first, rows // lanes):
-        at = base + (c - first) * total
-        send_ref[at : at + total, :] = ints[:, c * lanes : (c + 1) * lanes]
-
-
-def direct_kernel(sizes, *refs):
-    vir_parts, vir_own, occ_own, high, deep, width = sizes
-    got_ref, occ_ref, vir_ref, *amp_refs, lad_ref, inv_ref, sel_ref, all_ref = refs
+    ints = jnp.dot(ints, int_ref[...], preferred_element_type=F32).astype(BF16)
+    depth = amps.shape[0]
+    base = cols // lanes * depth
+    kept = (send_ref.shape[0] - base) // total
+    for ref, first in ((send_ref, rows // lanes - kept), (keep_ref, 0)):
+        for c in range(cols // lanes):
+            ref[c * depth : (c + 1) * depth, :] = amps[:, c * lanes : (c + 1) * lanes]
+        for c in range(kept):
+            at = (first + c) * lanes
+            ref[base + c * total : base + (c + 1) * total, :] = ints[:, at : at + lanes]
+
+
+def prepare_kernel(sizes, occ_ref, vir_ref, amp_ref, int_ref, sel_ref, inv_ref):
+    vir_parts, vir_own, occ_own, width = sizes
+    rows, cols = inv_ref.shape
+    vir_all, occ_all = vir_parts * vir_own, occ_ref.shape[1]
+    square, area = occ_own * occ_own, vir_own * vir_own
+    me = lax.axis_index("vv")
+    col = columns(cols)
+    source = (col % occ_all // occ_own) * square + (col % occ_own) * occ_own + col // occ_all
+    amp_ref[...] = one_hot(cols, source)
+    col = columns(rows)
+    owner = jnp.bitwise_xor(col // area, me)
+    source = (col % vir_own) * vir_all + owner * vir_own + col % area // vir_own
+    int_ref[...] = one_hot(rows, source)
+    row = lax.broadcasted_iota(jnp.int32, (rows, 1), 0)
+    rel = jnp.bitwise_xor(row % vir_all // vir_own, me)
+    source = rel * width + (rel % (width // area)) * area + row // vir_all * vir_own + row % vir_own
+    pick = lax.broadcasted_iota(jnp.int32, sel_ref.shape, 1) == source
+    sel_ref[...] = jnp.where(pick, 1.0, 0.0).astype(BF16)
+    occ = occ_ref[...]
+    occ_column = pick_sum(occ, square_eye(occ_all), 1)
+    mine = lax.axis_index("oo") * occ_own + columns(cols) // occ_all
+    occ_mine = pick_sum(occ_column, lax.broadcasted_iota(jnp.int32, (occ_all, cols), 0) == mine, 0)
+    occ_pair = occ_mine + jnp.concatenate([occ] * occ_own, axis=1)
+    lane = lax.broadcasted_iota(jnp.int32, (rows, vir_all), 1)
+    vir = vir_ref[...]
+    vir_mine = pick_sum(vir, lane == me * vir_own + row // vir_all, 1)
+    vir_other = pick_sum(vir, lane == row % vir_all, 1)
+    inv_ref[...] = 1.0 / (occ_pair - vir_mine - vir_other)
+
+
+def direct_kernel(high, deep, got_ref, *refs):
+    *amp_refs, lad_ref, all_ref = refs
     me = lax.axis_index("vv")
     depth = amp_refs[0].shape[0]
     for rel, ref in enumerate(amp_refs):
@@ -132,24 +150,6 @@
     lad_ref[...] = lax.dot_general(
         ints, all_ref[...], (((0,), (0,)), ((), ())), preferred_element_type=F32
     ).astype(BF16)
-    rows, cols = inv_ref.shape
-    vir_all, occ_all = vir_parts * vir_own, occ_ref.shape[1]
-    occ = occ_ref[...]
-    occ_column = pick_sum(occ, square_eye(occ_all), 1)
-    mine = lax.axis_index("oo") * occ_own + columns(cols) // occ_all
-    occ_mine = pick_sum(occ_column, lax.broadcasted_iota(jnp.int32, (occ_all, cols), 0) == mine, 0)
-    occ_pair = occ_mine + jnp.concatenate([occ] * occ_own, axis=1)
-    lane = lax.broadcasted_iota(jnp.int32, (rows, vir_all), 1)
-    row = lax.broadcasted_iota(jnp.int32, (rows, 1), 0)
-    vir = vir_ref[...]
-    vir_mine = pick_sum(vir, lane == me * vir_own + row // vir_all, 1)
-    vir_other = pick_sum(vir, lane == row % vir_all, 1)
-    inv_ref[...] = 1.0 / (occ_pair - vir_mine - vir_other)
-    n, area = sel_ref.shape[1], vir_own * vir_own
-    rel = jnp.bitwise_xor(row % vir_all // vir_own, me)
-    source = rel * width + (rel % (width // area)) * area + row // vir_all * vir_own + row % vir_own
-    pick = lax.broadcasted_iota(jnp.int32, (rows, n), 1) == source
-    sel_ref[...] = jnp.where(pick, 1.0, 0.0).astype(BF16)
 
 
 def choose_kernel(own, source_ref):
@@ -159,11 +159,11 @@
     source_ref[...] = (col % square // own) * occ_all + (col // square) * own + col % own
 
 
-def mirror_kernel(sizes, *refs):
-    depth, total, width = sizes
+def mirror_kernel(depth, *refs):
     lad_ref, inv_ref, sel_ref, *got_refs, out_hbm, all_ref, out_ref, sems = refs
     me = lax.axis_index("vv")
     rows, cols = out_ref.shape
+    total = all_ref.shape[0]
     chunks = cols // LANES
     for rel, ref in enumerate(got_refs):
         at = pl.multiple_of(jnp.bitwise_xor(me, rel) * depth, depth)
@@ -172,9 +172,9 @@
     base = chunks * depth
     ints = jnp.concatenate(
         [
-            ref[base + c * total : base + (c + 1) * total, :]
+            ref[at : at + total, :]
             for ref in got_refs
-            for c in range(width // LANES)
+            for at in range(base, ref.shape[0], total)
         ],
         axis=1,
     )
@@ -222,6 +222,9 @@
     high = depth * occ_own * occ_own // LANES
     area = vir_own * vir_own
 
+    def struct(*shape, dtype=BF16):
+        return jax.ShapeDtypeStruct(shape, dtype)
+
     def swap(x, step):
         return lax.ppermute(x, "vv", [(k, k ^ step) for k in range(vir_parts)])
 
@@ -231,28 +234,34 @@
 
     (source,) = call(
         functools.partial(choose_kernel, occ_own),
-        [jax.ShapeDtypeStruct((1, cols), jnp.int32)],
+        [struct(1, cols, dtype=jnp.int32)],
         (),
         flops=CHOOSE_FLOPS,
     )
 
-    shape = (occ_parts, high + rows // LANES * deep, LANES)
     (packed,) = call(
         functools.partial(pack_kernel, occ_own),
-        [jax.ShapeDtypeStruct(shape, BF16)],
+        [struct(occ_parts, high + rows // LANES * deep, LANES)],
         (amplitudes, integrals.T, source),
         flops=2 * depth * cols * cols,
     )
     got = lax.all_to_all(packed, "oo", 0, 0, tiled=True, axis_index_groups=[middle_out(occ_parts)])
+    to_amps, to_ints, to_rows, inverse = call(
+        functools.partial(prepare_kernel, (vir_parts, vir_own, occ_own, width)),
+        [
+            struct(cols, cols),
+            struct(rows, rows),
+            struct(rows, vir_parts * width),
+            struct(rows, cols, dtype=F32),
+        ],
+        (occ_energy.reshape(1, occ_all), vir_energy.reshape(1, vir_all)),
+    )
 
     amp_rows = cols // LANES * depth
-    send_shape = jax.ShapeDtypeStruct((amp_rows + widths[0] // LANES * total, LANES), BF16)
     send, keep = call(
-        functools.partial(
-            split_kernel, (vir_parts, vir_own, occ_own, high, deep, widths[0] // LANES)
-        ),
-        [send_shape] * 2,
-        (got,),
+        functools.partial(split_kernel, occ_own, high, deep),
+        [struct(amp_rows + widths[0] // LANES * total, LANES)] * 2,
+        (got, to_amps, to_ints),
         flops=2 * depth * cols * cols + 2 * total * rows * rows,
     )
     held = {0: (send, keep)}
@@ -270,25 +279,16 @@
             held = {k: (x, x) for k, x in arrived.items()}
     order = range(vir_parts)
 
-    ladder, inverse, to_rows = call(
-        functools.partial(direct_kernel, (vir_parts, vir_own, occ_own, high, deep, width)),
-        [
-            jax.ShapeDtypeStruct((rows, cols), BF16),
-            jax.ShapeDtypeStruct((rows, cols), F32),
-            jax.ShapeDtypeStruct((rows, vir_parts * width), BF16),
-        ],
-        (
-            got,
-            occ_energy.reshape(1, occ_all),
-            vir_energy.reshape(1, vir_all),
-            *(direct[k] for k in order),
-        ),
+    (ladder,) = call(
+        functools.partial(direct_kernel, high, deep),
+        [struct(rows, cols)],
+        (got, *(direct[k] for k in order)),
         scratch=[pltpu.VMEM((total, cols), BF16)],
         flops=2 * rows * total * cols,
     )
     (update,) = call(
-        functools.partial(mirror_kernel, (depth, total, width)),
-        [jax.ShapeDtypeStruct((rows, cols), BF16)],
+        functools.partial(mirror_kernel, depth),
+        [struct(rows, cols)],
         (ladder, inverse, to_rows, *(arrived[k] for k in order)),
         scratch=[
             pltpu.VMEM((total, cols), BF16),

time: 23.9 us -> 23.7 us (level)
  blocking collectives: 12.7 us -> 0 us
  starting transfers between devices: 2.61 us -> 10.4 us
  waiting for transfers between devices: 4.5 us -> 8.17 us
  Pallas kernels: 2.23 us -> 3.22 us
    all_to_all x1 -> x0, blocking collectives: 12.7 us -> none  [on_device(): lax.all_to_all(packed, 'oo', 0, 0, tiled=True, axis_index_groups=[middle_...]
    all_to_all x0 -> x1, starting transfers between devices: none -> 7.84 us  [on_device(): lax.all_to_all(packed, 'oo', 0, 0, tiled=True, axis_index_groups=[middle_...]
    all_to_all x0 -> x1, waiting for transfers between devices: none -> 3.67 us  [on_device(): lax.all_to_all(packed, 'oo', 0, 0, tiled=True, axis_index_groups=[middle_...]
    pallas_call x5 -> x6, Pallas kernels: 2.23 us -> 3.22 us  [call(): pl.pallas_call(kernel, out_shape=outs, in_specs=[pl.BlockSpec(memory_spac...]
  transfers between devices with their start and end apart: 6 -> 7, of which waited for: 4 -> 5; matrix products, arithmetic and copies ran while one was open for 0% -> 0% of each run, Pallas kernels for 2% -> 3%
where the time goes in v5:
time: 23.7 us; the launch traced here: 23.4 us
  starting transfers between devices  10.4 us (44%)
  waiting for transfers between devices  8.17 us (34%)
  Pallas kernels  3.22 us (14%)
  local copies, waits for them, and re-layouts  1.51 us (6%)
    all_to_all x1, starting transfers between devices, on_device(): lax.all_to_all(packed, 'oo', 0, 0, tiled=True, axis_index_groups=[middle_...  7.84 us
    ppermute x6, waiting for transfers between devices, swap(): return lax.ppermute(x, 'vv', [(k, k ^ step) for k in range(vir_parts)])  4.5 us
    all_to_all x1, waiting for transfers between devices, on_device(): lax.all_to_all(packed, 'oo', 0, 0, tiled=True, axis_index_groups=[middle_...  3.67 us
    pallas_call x6, Pallas kernels, call(): pl.pallas_call(kernel, out_shape=outs, in_specs=[pl.BlockSpec(memory_spac...  3.22 us
    ppermute x6, starting transfers between devices, swap(): return lax.ppermute(x, 'vv', [(k, k ^ step) for k in range(vir_parts)])  2.61 us
    unnamed x8, local copies, waits for them, and re-layouts  1.51 us
  transfers between devices with their start and end apart: 7, of which 5 were waited for; matrix products, arithmetic and copies ran while one was open for 0% of the time, Pallas kernels for 3%

profile of v5, /device:TPU:0, one launch (start us, length us, event | category | flops | bytes accessed | tf_op | source)
XLA Modules:
  0.0 23.4 jit_solution(7453493397625641031)
XLA Ops:
  0.0 0.0 copy-start.1
  0.0 0.7 %copy-done.1 = bf16[256,32]{0,1:T(8,128)(2,1)S(1)} copy-done((bf16[256,32]{0,1:T(8,128)(2,1)S(1)}, bf16[256,32]{0,1:T(8,128)(2,1)}, u32[]{:S(2)}) %copy-start.1) | copy-done | bytes 16408
  0.7 0.1 copy-done
  0.9 1.0 %shard_map.47 = bf16[8,96,128]{2,1,0:T(8,128)(2,1)} custom-call(bf16[64,512]{1,0:T(8,128)(2,1)S(1)} %copy-done, bf16[32,256]{1,0:T(8,128)(2,1)S(1)} %bitcast.3, s32[1,512]{1,0:T(1,128)S(1)} %shard_map.46.source_ref), custom_call_target="tpu_custom_call" | custom-call | flops 33554432 | bytes 280576 | tf_op jit(solution)/shard_map/pallas_call | solution.py:203
  1.8 7.8 %all-to-all-start = ((bf16[8,96,128]{2,1,0:T(8,128)(2,1)}), bf16[8,96,128]{2,1,0:T(8,128)(2,1)S(1)}, u32[]{:S(2)}, u32[]{:S(2)}) async-start(bf16[8,96,128]{2,1,0:T(8,128)(2,1)} %shard_map.47), calls=%async_computation | async-start | bytes 393216 | tf_op jit(solution)/shard_map/all_to_all | solution.py:248
  9.7 0.7 %copy-done.2 = f32[64]{0:T(128)S(1)} copy-done((f32[64]{0:T(128)S(1)}, f32[64]{0:T(128)}, u32[]{:S(2)}) %copy-start.2) | copy-done | bytes 280
  10.3 0.0 copy-done.3
  10.3 0.5 %shard_map.49 = (bf16[512,512]{1,0:T(8,128)(2,1)S(1)}, bf16[256,256]{1,0:T(8,128)(2,1)S(1)}, bf16[256,512]{1,0:T(8,128)(2,1)S(1)}, f32[256,512]{1,0:T(8,128)S(1)}) custom-call(f32[1,64]{1,0:T(1,128)S(1)} %bitcast.4, f32[1,32]{1,0:T(1,128)S(1)} %bitcast.5), custom_call_target="tpu_custom_call" | custom-call | bytes 1442176 | tf_op jit(solution)/shard_map/pallas_call | solution.py:203
  10.8 3.7 %all-to-all-done.got_ref = bf16[8,96,128]{2,1,0:T(8,128)(2,1)S(1)} async-done(((bf16[8,96,128]{2,1,0:T(8,128)(2,1)}), bf16[8,96,128]{2,1,0:T(8,128)(2,1)S(1)}, u32[]{:S(2)}, u32[]{:S(2)}) %all-to-all-start) | async-done | bytes 196640 | tf_op jit(solution)/shard_map/all_to_all | solution.py:248
  14.5 0.3 %shard_map.50 = (bf16[512,128]{1,0:T(8,128)(2,1)S(1)}, bf16[512,128]{1,0:T(8,128)(2,1)S(1)}) custom-call(bf16[8,96,128]{2,1,0:T(8,128)(2,1)S(1)} %all-to-all-done.got_ref, bf16[512,512]{1,0:T(8,128)(2,1)S(1)} %get-tuple-element.13.amp_ref, bf16[256,256]{1,0:T(8,128)(2,1)S(1)} %get-tuple-element.14.int_ref), custom_call_target="tpu_custom_call" | custom-call | flops 67108864 | bytes 1114112 | tf_op jit(solution)/shard_map/pallas_call | solution.py:203
  14.8 1.6 %collective-permute-start.4 = (bf16[512,128]{1,0:T(8,128)(2,1)S(1)}, bf16[512,128]{1,0:T(8,128)(2,1)S(1)}, u32[]{:S(2)}, u32[]{:S(2)}) collective-permute-start(bf16[512,128]{1,0:T(8,128)(2,1)S(1)} %get-tuple-element.16), channel_id=1, source_target_pairs={{0,16},{8,24},{16,0},{24,8},{1,17},{9,25},{17,1},{25,9},{2,18},{10... | collective-permute-start | bytes 393224 | tf_op jit(solution)/shard_map/ppermute | solution.py:229
  16.4 0.5 %collective-permute-start.1 = (bf16[64,512]{1,0:T(8,128)(2,1)S(1)}, bf16[64,512]{1,0:T(8,128)(2,1)S(1)}, u32[]{:S(2)}, u32[]{:S(2)}) collective-permute-start(bf16[64,512]{1,0:T(8,128)(2,1)S(1)} %copy-done), channel_id=1, source_target_pairs={{0,16},{8,24},{16,0},{24,8},{1,17},{9,25},{17,1},{25,9},{2,18},{10... | collective-permute-start | bytes 196616 | tf_op jit(solution)/shard_map/ppermute | solution.py:229
  16.9 0.0 collective-permute-start.3
  16.9 2.9 %collective-permute-done.4.refs_5_ = bf16[512,128]{1,0:T(8,128)(2,1)S(1)} collective-permute-done((bf16[512,128]{1,0:T(8,128)(2,1)S(1)}, bf16[512,128]{1,0:T(8,128)(2,1)S(1)}, u32[]{:S(2)}, u32[]{:S(2)}) %collective-permute-start.4) | collective-permute-done | bytes 131104 | tf_op jit(solution)/shard_map/ppermute | solution.py:229
  19.9 0.0 collective-permute-start.5
  19.9 0.5 %collective-permute-start = (bf16[64,512]{1,0:T(8,128)(2,1)S(1)}, bf16[64,512]{1,0:T(8,128)(2,1)S(1)}, u32[]{:S(2)}, u32[]{:S(2)}) collective-permute-start(bf16[64,512]{1,0:T(8,128)(2,1)S(1)} %copy-done), channel_id=1, source_target_pairs={{0,8},{8,0},{16,24},{24,16},{1,9},{9,1},{17,25},{25,17},{2,10},{10... | collective-permute-start | bytes 196616 | tf_op jit(solution)/shard_map/ppermute | solution.py:229
  20.4 0.3 %collective-permute-done.1.refs_2_ = bf16[64,512]{1,0:T(8,128)(2,1)S(1)} collective-permute-done((bf16[64,512]{1,0:T(8,128)(2,1)S(1)}, bf16[64,512]{1,0:T(8,128)(2,1)S(1)}, u32[]{:S(2)}, u32[]{:S(2)}) %collective-permute-start.1) | collective-permute-done | bytes 65568 | tf_op jit(solution)/shard_map/ppermute | solution.py:229
  20.7 0.0 collective-permute-start.2
  20.7 0.6 %collective-permute-done.refs_1_ = bf16[64,512]{1,0:T(8,128)(2,1)S(1)} collective-permute-done((bf16[64,512]{1,0:T(8,128)(2,1)S(1)}, bf16[64,512]{1,0:T(8,128)(2,1)S(1)}, u32[]{:S(2)}, u32[]{:S(2)}) %collective-permute-start) | collective-permute-done | bytes 65568 | tf_op jit(solution)/shard_map/ppermute | solution.py:229
  21.3 0.6 %collective-permute-done.2.refs_3_ = bf16[64,512]{1,0:T(8,128)(2,1)S(1)} collective-permute-done((bf16[64,512]{1,0:T(8,128)(2,1)S(1)}, bf16[64,512]{1,0:T(8,128)(2,1)S(1)}, u32[]{:S(2)}, u32[]{:S(2)}) %collective-permute-start.2) | collective-permute-done | bytes 65568 | tf_op jit(solution)/shard_map/ppermute | solution.py:229
  21.9 0.2 %shard_map.48.refs_0_ = bf16[256,512]{1,0:T(8,128)(2,1)S(1)} custom-call(bf16[8,96,128]{2,1,0:T(8,128)(2,1)S(1)} %all-to-all-done.got_ref, bf16[64,512]{1,0:T(8,128)(2,1)S(1)} %copy-done, bf16[64,512]{1,0:T(8,128)(2,1)S(1)} %collective-permute-done.refs_1_, bf16[64,512]{1,0:T(8,128)(2,1)S(1)} %collective-permute-done.1.refs_2_, ...), custom_call_target="tpu_custom_call" | custom-call | flops 67108864 | bytes 720896 | tf_op jit(solution)/shard_map/pallas_call | solution.py:203
  22.2 0.0 collective-permute-done.3.refs_4_
  22.2 0.0 collective-permute-done.5.refs_6_
  22.2 1.2 %shard_map.51 = bf16[256,512]{1,0:T(8,128)(2,1)} custom-call(bf16[256,512]{1,0:T(8,128)(2,1)S(1)} %shard_map.48.refs_0_, f32[256,512]{1,0:T(8,128)S(1)} %get-tuple-element.11.refs_1_, bf16[256,512]{1,0:T(8,128)(2,1)S(1)} %get-tuple-element.12.refs_2_, bf16[512,128]{1,0:T(8,128)(2,1)S(1)} %get-tuple-element.15.refs_3_, ...), custom_call_target="tpu_custom_call" | custom-call | flops 134217728 | bytes 1835008 | tf_op jit(solution)/shard_map/pallas_call | solution.py:203
  (4 shorter events, 0.0 us)
Async XLA Ops:
  0.0 0.7 %copy-start.1 = (bf16[256,32]{0,1:T(8,128)(2,1)S(1)}, bf16[256,32]{0,1:T(8,128)(2,1)}, u32[]{:S(2)}) copy-start(bf16[256,32]{0,1:T(8,128)(2,1)} %param.4) | copy-start | bytes 49156
  0.0 0.9 %copy-start = (bf16[64,512]{1,0:T(8,128)(2,1)S(1)}, bf16[64,512]{1,0:T(8,128)(2,1)}, u32[]{:S(2)}) copy-start(bf16[64,512]{1,0:T(8,128)(2,1)} %refs_0_.1) | copy-start | bytes 196612
  1.8 12.7 %all-to-all-start = ((bf16[8,96,128]{2,1,0:T(8,128)(2,1)}), bf16[8,96,128]{2,1,0:T(8,128)(2,1)S(1)}, u32[]{:S(2)}, u32[]{:S(2)}) async-start(bf16[8,96,128]{2,1,0:T(8,128)(2,1)} %shard_map.47), calls=%async_computation | async-start | bytes 393216 | tf_op jit(solution)/shard_map/all_to_all | solution.py:248
  9.7 0.7 %copy-start.2 = (f32[64]{0:T(128)S(1)}, f32[64]{0:T(128)}, u32[]{:S(2)}) copy-start(f32[64]{0:T(128)} %param.6) | copy-start | bytes 772
  9.7 0.7 %copy-start.3 = (f32[32]{0:T(128)S(1)}, f32[32]{0:T(128)}, u32[]{:S(2)}) copy-start(f32[32]{0:T(128)} %param.7) | copy-start | bytes 388
  14.8 5.0 %collective-permute-start.4 = (bf16[512,128]{1,0:T(8,128)(2,1)S(1)}, bf16[512,128]{1,0:T(8,128)(2,1)S(1)}, u32[]{:S(2)}, u32[]{:S(2)}) collective-permute-start(bf16[512,128]{1,0:T(8,128)(2,1)S(1)} %get-tuple-element.16), channel_id=1, source_target_pairs={{0,16},{8,24},{16,0},{24,8},{1,17},{9,25},{17,1},{25,9},{2,18},{10... | collective-permute-start | bytes 393224 | tf_op jit(solution)/shard_map/ppermute | solution.py:229
  16.4 4.3 %collective-permute-start.1 = (bf16[64,512]{1,0:T(8,128)(2,1)S(1)}, bf16[64,512]{1,0:T(8,128)(2,1)S(1)}, u32[]{:S(2)}, u32[]{:S(2)}) collective-permute-start(bf16[64,512]{1,0:T(8,128)(2,1)S(1)} %copy-done), channel_id=1, source_target_pairs={{0,16},{8,24},{16,0},{24,8},{1,17},{9,25},{17,1},{25,9},{2,18},{10... | collective-permute-start | bytes 196616 | tf_op jit(solution)/shard_map/ppermute | solution.py:229
  16.9 5.3 %collective-permute-start.3 = (bf16[512,128]{1,0:T(8,128)(2,1)S(1)}, bf16[512,128]{1,0:T(8,128)(2,1)S(1)}, u32[]{:S(2)}, u32[]{:S(2)}) collective-permute-start(bf16[512,128]{1,0:T(8,128)(2,1)S(1)} %get-tuple-element.15.refs_3_), channel_id=1, source_target_pairs={{0,8},{8,0},{16,24},{24,16},{1,9},{9,1},{17,25},{25,17},{2,10},{10... | collective-permute-start | bytes 393224 | tf_op jit(solution)/shard_map/ppermute | solution.py:229
  19.9 2.3 %collective-permute-start.5 = (bf16[512,128]{1,0:T(8,128)(2,1)S(1)}, bf16[512,128]{1,0:T(8,128)(2,1)S(1)}, u32[]{:S(2)}, u32[]{:S(2)}) collective-permute-start(bf16[512,128]{1,0:T(8,128)(2,1)S(1)} %collective-permute-done.4.refs_5_), channel_id=1, source_target_pairs={{0,8},{8,0},{16,24},{24,16},{1,9},{9,1},{17,25},{25,17},{2,10},{10... | collective-permute-start | bytes 393224 | tf_op jit(solution)/shard_map/ppermute | solution.py:229
  19.9 1.4 %collective-permute-start = (bf16[64,512]{1,0:T(8,128)(2,1)S(1)}, bf16[64,512]{1,0:T(8,128)(2,1)S(1)}, u32[]{:S(2)}, u32[]{:S(2)}) collective-permute-start(bf16[64,512]{1,0:T(8,128)(2,1)S(1)} %copy-done), channel_id=1, source_target_pairs={{0,8},{8,0},{16,24},{24,16},{1,9},{9,1},{17,25},{25,17},{2,10},{10... | collective-permute-start | bytes 196616 | tf_op jit(solution)/shard_map/ppermute | solution.py:229
  20.7 1.3 %collective-permute-start.2 = (bf16[64,512]{1,0:T(8,128)(2,1)S(1)}, bf16[64,512]{1,0:T(8,128)(2,1)S(1)}, u32[]{:S(2)}, u32[]{:S(2)}) collective-permute-start(bf16[64,512]{1,0:T(8,128)(2,1)S(1)} %collective-permute-done.1.refs_2_), channel_id=1, source_target_pairs={{0,8},{8,0},{16,24},{24,16},{1,9},{9,1},{17,25},{25,17},{2,10},{10... | collective-permute-start | bytes 196616 | tf_op jit(solution)/shard_map/ppermute | solution.py:229

commit v6 on v5

--- a/solution.py
+++ b/solution.py
@@ -8,7 +8,7 @@
 from jax.sharding import PartitionSpec as P
 
 
-LANES, STORES = 128, 2
+LANES = 128
 LEAST, MOST = 8 << 20, 60 << 20
 CHOOSE_FLOPS = 10**9
 F32 = jnp.float32
@@ -20,6 +20,17 @@
     n = source.shape[1]
     pick = lax.broadcasted_iota(jnp.int32, (rows, n), 0) == source
     return jnp.where(pick, 1.0, 0.0).astype(BF16)
+
+
+def one_hot_rows(source, n):
+    pick = lax.broadcasted_iota(jnp.int32, (source.shape[0], n), 1) == source
+    return jnp.where(pick, 1.0, 0.0).astype(BF16)
+
+
+def choose_rows(order, columns_first):
+    return lax.dot_general(
+        order, columns_first, (((1,), (1,)), ((), ())), preferred_element_type=F32
+    ).astype(BF16)
 
 
 def middle_out(n):
@@ -82,7 +93,7 @@
     )
 
 
-def split_kernel(occ_own, high, deep, got_ref, amp_ref, int_ref, send_ref, keep_ref):
+def split_kernel(vir_parts, occ_own, high, deep, got_ref, amp_ref, int_ref, send_ref, keep_ref):
     parts, _, lanes = got_ref.shape
     square = occ_own * occ_own
     cols = parts * square
@@ -95,22 +106,26 @@
     ]
     amps = jnp.concatenate(halves, axis=0).astype(BF16)
     amps = jnp.dot(amps, amp_ref[...], preferred_element_type=F32).astype(BF16)
-    ints = integral_columns(got_ref, high, deep)
-    total, rows = ints.shape
-    ints = jnp.dot(ints, int_ref[...], preferred_element_type=F32).astype(BF16)
+    ints = choose_rows(int_ref[...], integral_columns(got_ref, high, deep))
     depth = amps.shape[0]
     base = cols // lanes * depth
-    kept = (send_ref.shape[0] - base) // total
-    for ref, first in ((send_ref, rows // lanes - kept), (keep_ref, 0)):
+    rows, total = ints.shape
+    area = rows // vir_parts
+    kept = (send_ref.shape[0] - base) // (area * (total // lanes))
+    for ref, first in ((send_ref, vir_parts - kept), (keep_ref, 0)):
         for c in range(cols // lanes):
             ref[c * depth : (c + 1) * depth, :] = amps[:, c * lanes : (c + 1) * lanes]
-        for c in range(kept):
-            at = (first + c) * lanes
-            ref[base + c * total : base + (c + 1) * total, :] = ints[:, at : at + lanes]
-
-
-def prepare_kernel(sizes, occ_ref, vir_ref, amp_ref, int_ref, sel_ref, inv_ref):
-    vir_parts, vir_own, occ_own, width = sizes
+        at = base
+        for rel in range(first, first + kept):
+            for c in range(total // lanes):
+                ref[at : at + area, :] = ints[
+                    rel * area : (rel + 1) * area, c * lanes : (c + 1) * lanes
+                ]
+                at += area
+
+
+def prepare_kernel(sizes, occ_ref, vir_ref, amp_ref, int_ref, row_ref, inv_ref):
+    vir_parts, vir_own, occ_own = sizes
     rows, cols = inv_ref.shape
     vir_all, occ_all = vir_parts * vir_own, occ_ref.shape[1]
     square, area = occ_own * occ_own, vir_own * vir_own
@@ -118,15 +133,11 @@
     col = columns(cols)
     source = (col % occ_all // occ_own) * square + (col % occ_own) * occ_own + col // occ_all
     amp_ref[...] = one_hot(cols, source)
-    col = columns(rows)
-    owner = jnp.bitwise_xor(col // area, me)
-    source = (col % vir_own) * vir_all + owner * vir_own + col % area // vir_own
-    int_ref[...] = one_hot(rows, source)
     row = lax.broadcasted_iota(jnp.int32, (rows, 1), 0)
-    rel = jnp.bitwise_xor(row % vir_all // vir_own, me)
-    source = rel * width + (rel % (width // area)) * area + row // vir_all * vir_own + row % vir_own
-    pick = lax.broadcasted_iota(jnp.int32, sel_ref.shape, 1) == source
-    sel_ref[...] = jnp.where(pick, 1.0, 0.0).astype(BF16)
+    other = jnp.bitwise_xor(row // area, me) * vir_own
+    outer, inner = row % area // vir_own, row % vir_own
+    int_ref[...] = one_hot_rows(inner * vir_all + other + outer, rows)
+    row_ref[...] = one_hot_rows(outer * vir_all + other + inner, rows)
     occ = occ_ref[...]
     occ_column = pick_sum(occ, square_eye(occ_all), 1)
     mine = lax.axis_index("oo") * occ_own + columns(cols) // occ_all
@@ -134,22 +145,21 @@
     occ_pair = occ_mine + jnp.concatenate([occ] * occ_own, axis=1)
     lane = lax.broadcasted_iota(jnp.int32, (rows, vir_all), 1)
     vir = vir_ref[...]
-    vir_mine = pick_sum(vir, lane == me * vir_own + row // vir_all, 1)
-    vir_other = pick_sum(vir, lane == row % vir_all, 1)
+    vir_mine = pick_sum(vir, lane == me * vir_own + outer, 1)
+    vir_other = pick_sum(vir, lane == other + inner, 1)
     inv_ref[...] = 1.0 / (occ_pair - vir_mine - vir_other)
 
 
-def direct_kernel(high, deep, got_ref, *refs):
+def direct_kernel(high, deep, got_ref, row_ref, *refs):
     *amp_refs, lad_ref, all_ref = refs
     me = lax.axis_index("vv")
     depth = amp_refs[0].shape[0]
     for rel, ref in enumerate(amp_refs):
         at = pl.multiple_of(jnp.bitwise_xor(me, rel) * depth, depth)
         all_ref[pl.ds(at, depth), :] = ref[...]
-    ints = integral_columns(got_ref, high, deep)
-    lad_ref[...] = lax.dot_general(
-        ints, all_ref[...], (((0,), (0,)), ((), ())), preferred_element_type=F32
-    ).astype(BF16)
+    ints = choose_rows(row_ref[...], integral_columns(got_ref, high, deep))
+    ladder = jnp.dot(ints, all_ref[...], preferred_element_type=F32)
+    lad_ref[...] = ladder.astype(BF16)
 
 
 def choose_kernel(own, source_ref):
@@ -160,37 +170,35 @@
 
 
 def mirror_kernel(depth, *refs):
-    lad_ref, inv_ref, sel_ref, *got_refs, out_hbm, all_ref, out_ref, sems = refs
+    lad_ref, inv_ref, *got_refs, out_hbm, all_ref, out_ref, sems = refs
     me = lax.axis_index("vv")
-    rows, cols = out_ref.shape
+    _, own, _, cols = out_ref.shape
     total = all_ref.shape[0]
+    area = own * own
     chunks = cols // LANES
     for rel, ref in enumerate(got_refs):
         at = pl.multiple_of(jnp.bitwise_xor(me, rel) * depth, depth)
         for c in range(chunks):
             all_ref[pl.ds(at, depth), c * LANES : (c + 1) * LANES] = ref[c * depth : (c + 1) * depth, :]
     base = chunks * depth
-    ints = jnp.concatenate(
-        [
-            ref[at : at + total, :]
-            for ref in got_refs
-            for at in range(base, ref.shape[0], total)
-        ],
-        axis=1,
-    )
-    rows_mirrored = lax.dot_general(
-        sel_ref[...], ints, (((1,), (1,)), ((), ())), preferred_element_type=F32
-    ).astype(BF16)
-    pieces = sems.shape[0]
-    size = rows // pieces
     stores = []
-    for piece in range(pieces):
-        some = slice(piece * size, (piece + 1) * size)
-        mirrored = jnp.dot(rows_mirrored[some], all_ref[...], preferred_element_type=F32)
+    for rel, ref in enumerate(got_refs):
+        first = base + (rel % 2) * area * (total // LANES)
+        ints = jnp.concatenate(
+            [
+                ref[first + c * area : first + (c + 1) * area, :]
+                for c in range(total // LANES)
+            ],
+            axis=1,
+        )
+        mirrored = jnp.dot(ints, all_ref[...], preferred_element_type=F32)
+        some = slice(rel * area, (rel + 1) * area)
         both = lad_ref[some, :].astype(F32) + mirrored.astype(BF16).astype(F32)
-        out_ref[some, :] = (both * inv_ref[some, :]).astype(BF16)
+        both = both * inv_ref[some, :]
+        out_ref[rel] = both.reshape(own, own, cols).astype(BF16)
+        other = jnp.bitwise_xor(me, rel)
         stores.append(
-            pltpu.make_async_copy(out_ref.at[some, :], out_hbm.at[some, :], sems.at[piece])
+            pltpu.make_async_copy(out_ref.at[rel], out_hbm.at[:, other], sems.at[rel])
         )
         stores[-1].start()
     for store in stores:
@@ -229,8 +237,6 @@
         return lax.ppermute(x, "vv", [(k, k ^ step) for k in range(vir_parts)])
 
     steps = [1 << bit for bit in reversed(range((vir_parts - 1).bit_length()))]
-    widths = [s * area for s in steps if s * area % LANES == 0] or [rows]
-    width = widths[-1]
 
     (source,) = call(
         functools.partial(choose_kernel, occ_own),
@@ -247,31 +253,26 @@
     )
     got = lax.all_to_all(packed, "oo", 0, 0, tiled=True, axis_index_groups=[middle_out(occ_parts)])
     to_amps, to_ints, to_rows, inverse = call(
-        functools.partial(prepare_kernel, (vir_parts, vir_own, occ_own, width)),
-        [
-            struct(cols, cols),
-            struct(rows, rows),
-            struct(rows, vir_parts * width),
-            struct(rows, cols, dtype=F32),
-        ],
+        functools.partial(prepare_kernel, (vir_parts, vir_own, occ_own)),
+        [struct(cols, cols), struct(rows, rows), struct(rows, rows), struct(rows, cols, dtype=F32)],
         (occ_energy.reshape(1, occ_all), vir_energy.reshape(1, vir_all)),
     )
 
-    amp_rows = cols // LANES * depth
+    amp_rows, int_rows = cols // LANES * depth, total // LANES * area
     send, keep = call(
-        functools.partial(split_kernel, occ_own, high, deep),
-        [struct(amp_rows + widths[0] // LANES * total, LANES)] * 2,
+        functools.partial(split_kernel, vir_parts, occ_own, high, deep),
+        [struct(amp_rows + vir_parts // 2 * int_rows, LANES)] * 2,
         (got, to_amps, to_ints),
         flops=2 * depth * cols * cols + 2 * total * rows * rows,
     )
     held = {0: (send, keep)}
     direct = {0: amplitudes}
-    for at, step in enumerate(steps):
+    for step in steps:
         direct |= {k ^ step: swap(x, step) for k, x in direct.items()}
         arrived = {k: x for k, (_, x) in held.items()}
         arrived |= {k ^ step: swap(x, step) for k, (x, _) in held.items()}
-        if at + 1 < len(widths):
-            cut = amp_rows + widths[at + 1] // LANES * total
+        if step > 2:
+            cut = amp_rows + step // 2 * int_rows
             held = {
                 k: (jnp.concatenate([x[:amp_rows], x[cut:]]), x[:cut]) for k, x in arrived.items()
             }
@@ -282,23 +283,23 @@
     (ladder,) = call(
         functools.partial(direct_kernel, high, deep),
         [struct(rows, cols)],
-        (got, *(direct[k] for k in order)),
+        (got, to_rows, *(direct[k] for k in order)),
         scratch=[pltpu.VMEM((total, cols), BF16)],
         flops=2 * rows * total * cols,
     )
     (update,) = call(
         functools.partial(mirror_kernel, depth),
-        [struct(rows, cols)],
-        (ladder, inverse, to_rows, *(arrived[k] for k in order)),
+        [struct(vir_own, vir_parts, vir_own, cols)],
+        (ladder, inverse, *(arrived[k] for k in order)),
         scratch=[
             pltpu.VMEM((total, cols), BF16),
-            pltpu.VMEM((rows, cols), BF16),
-            pltpu.SemaphoreType.DMA((STORES,)),
+            pltpu.VMEM((vir_parts, vir_own, vir_own, cols), BF16),
+            pltpu.SemaphoreType.DMA((vir_parts,)),
         ],
         flops=2 * rows * total * cols * 2,
         out_space=pl.ANY,
     )
-    return update
+    return update.reshape(rows, cols)
 
 
 def solution(mesh):

time: 23.7 us -> 23.7 us (level)
  transfers between devices with their start and end apart: 7 -> 7, of which waited for: 5 -> 5; matrix products, arithmetic and copies ran while one was open for 0% -> 0% of each run, Pallas kernels for 3% -> 4%
where the time goes in v6:
time: 23.7 us; the launch traced here: 23.4 us
  starting transfers between devices  10.4 us (44%)
  waiting for transfers between devices  8.24 us (35%)
  Pallas kernels  3.18 us (13%)
  local copies, waits for them, and re-layouts  1.51 us (6%)
    all_to_all x1, starting transfers between devices, on_device(): lax.all_to_all(packed, 'oo', 0, 0, tiled=True, axis_index_groups=[middle_...  7.84 us
    ppermute x6, waiting for transfers between devices, swap(): return lax.ppermute(x, 'vv', [(k, k ^ step) for k in range(vir_parts)])  4.5 us
    all_to_all x1, waiting for transfers between devices, on_device(): lax.all_to_all(packed, 'oo', 0, 0, tiled=True, axis_index_groups=[middle_...  3.74 us
    pallas_call x6, Pallas kernels, call(): pl.pallas_call(kernel, out_shape=outs, in_specs=[pl.BlockSpec(memory_spac...  3.18 us
    ppermute x6, starting transfers between devices, swap(): return lax.ppermute(x, 'vv', [(k, k ^ step) for k in range(vir_parts)])  2.61 us
    unnamed x8, local copies, waits for them, and re-layouts  1.51 us
  transfers between devices with their start and end apart: 7, of which 5 were waited for; matrix products, arithmetic and copies ran while one was open for 0% of the time, Pallas kernels for 4%

profile of v6, /device:TPU:0, one launch (start us, length us, event | category | flops | bytes accessed | tf_op | source)
XLA Modules:
  0.0 23.4 jit_solution(9360375691699368353)
XLA Ops:
  0.0 0.0 copy-start.1
  0.0 0.7 %copy-done.1 = bf16[256,32]{0,1:T(8,128)(2,1)S(1)} copy-done((bf16[256,32]{0,1:T(8,128)(2,1)S(1)}, bf16[256,32]{0,1:T(8,128)(2,1)}, u32[]{:S(2)}) %copy-start.1) | copy-done | bytes 16408
  0.7 0.1 copy-done
  0.9 1.0 %shard_map.47 = bf16[8,96,128]{2,1,0:T(8,128)(2,1)} custom-call(bf16[64,512]{1,0:T(8,128)(2,1)S(1)} %copy-done, bf16[32,256]{1,0:T(8,128)(2,1)S(1)} %bitcast.4, s32[1,512]{1,0:T(1,128)S(1)} %shard_map.46.source_ref), custom_call_target="tpu_custom_call" | custom-call | flops 33554432 | bytes 280576 | tf_op jit(solution)/shard_map/pallas_call | solution.py:211
  1.8 7.8 %all-to-all-start = ((bf16[8,96,128]{2,1,0:T(8,128)(2,1)}), bf16[8,96,128]{2,1,0:T(8,128)(2,1)S(1)}, u32[]{:S(2)}, u32[]{:S(2)}) async-start(bf16[8,96,128]{2,1,0:T(8,128)(2,1)} %shard_map.47), calls=%async_computation | async-start | bytes 393216 | tf_op jit(solution)/shard_map/all_to_all | solution.py:254
  9.7 0.7 %copy-done.2 = f32[64]{0:T(128)S(1)} copy-done((f32[64]{0:T(128)S(1)}, f32[64]{0:T(128)}, u32[]{:S(2)}) %copy-start.2) | copy-done | bytes 280
  10.3 0.0 copy-done.3
  10.3 0.4 %shard_map.48 = (bf16[512,512]{1,0:T(8,128)(2,1)S(1)}, bf16[256,256]{1,0:T(8,128)(2,1)S(1)}, bf16[256,256]{1,0:T(8,128)(2,1)S(1)}, f32[256,512]{1,0:T(8,128)S(1)}) custom-call(f32[1,64]{1,0:T(1,128)S(1)} %bitcast.5, f32[1,32]{1,0:T(1,128)S(1)} %bitcast.6), custom_call_target="tpu_custom_call" | custom-call | bytes 1311104 | tf_op jit(solution)/shard_map/pallas_call | solution.py:211
  10.8 3.7 %all-to-all-done.got_ref = bf16[8,96,128]{2,1,0:T(8,128)(2,1)S(1)} async-done(((bf16[8,96,128]{2,1,0:T(8,128)(2,1)}), bf16[8,96,128]{2,1,0:T(8,128)(2,1)S(1)}, u32[]{:S(2)}, u32[]{:S(2)}) %all-to-all-start) | async-done | bytes 196640 | tf_op jit(solution)/shard_map/all_to_all | solution.py:254
  14.5 0.3 %shard_map.50 = (bf16[512,128]{1,0:T(8,128)(2,1)S(1)}, bf16[512,128]{1,0:T(8,128)(2,1)S(1)}) custom-call(bf16[8,96,128]{2,1,0:T(8,128)(2,1)S(1)} %all-to-all-done.got_ref, bf16[512,512]{1,0:T(8,128)(2,1)S(1)} %get-tuple-element.13.amp_ref, bf16[256,256]{1,0:T(8,128)(2,1)S(1)} %get-tuple-element.14.int_ref), custom_call_target="tpu_custom_call" | custom-call | flops 67108864 | bytes 1114112 | tf_op jit(solution)/shard_map/pallas_call | solution.py:211
  14.8 1.6 %collective-permute-start.4 = (bf16[512,128]{1,0:T(8,128)(2,1)S(1)}, bf16[512,128]{1,0:T(8,128)(2,1)S(1)}, u32[]{:S(2)}, u32[]{:S(2)}) collective-permute-start(bf16[512,128]{1,0:T(8,128)(2,1)S(1)} %get-tuple-element.16), channel_id=1, source_target_pairs={{0,16},{8,24},{16,0},{24,8},{1,17},{9,25},{17,1},{25,9},{2,18},{10... | collective-permute-start | bytes 393224 | tf_op jit(solution)/shard_map/ppermute | solution.py:237
  16.4 0.5 %collective-permute-start.1 = (bf16[64,512]{1,0:T(8,128)(2,1)S(1)}, bf16[64,512]{1,0:T(8,128)(2,1)S(1)}, u32[]{:S(2)}, u32[]{:S(2)}) collective-permute-start(bf16[64,512]{1,0:T(8,128)(2,1)S(1)} %copy-done), channel_id=1, source_target_pairs={{0,16},{8,24},{16,0},{24,8},{1,17},{9,25},{17,1},{25,9},{2,18},{10... | collective-permute-start | bytes 196616 | tf_op jit(solution)/shard_map/ppermute | solution.py:237
  16.9 0.0 collective-permute-start.3
  16.9 2.9 %collective-permute-done.4.refs_4_ = bf16[512,128]{1,0:T(8,128)(2,1)S(1)} collective-permute-done((bf16[512,128]{1,0:T(8,128)(2,1)S(1)}, bf16[512,128]{1,0:T(8,128)(2,1)S(1)}, u32[]{:S(2)}, u32[]{:S(2)}) %collective-permute-start.4) | collective-permute-done | bytes 131104 | tf_op jit(solution)/shard_map/ppermute | solution.py:237
  19.9 0.0 collective-permute-start.5
  19.9 0.5 %collective-permute-start = (bf16[64,512]{1,0:T(8,128)(2,1)S(1)}, bf16[64,512]{1,0:T(8,128)(2,1)S(1)}, u32[]{:S(2)}, u32[]{:S(2)}) collective-permute-start(bf16[64,512]{1,0:T(8,128)(2,1)S(1)} %copy-done), channel_id=1, source_target_pairs={{0,8},{8,0},{16,24},{24,16},{1,9},{9,1},{17,25},{25,17},{2,10},{10... | collective-permute-start | bytes 196616 | tf_op jit(solution)/shard_map/ppermute | solution.py:237
  20.4 0.3 %collective-permute-done.1.refs_2_ = bf16[64,512]{1,0:T(8,128)(2,1)S(1)} collective-permute-done((bf16[64,512]{1,0:T(8,128)(2,1)S(1)}, bf16[64,512]{1,0:T(8,128)(2,1)S(1)}, u32[]{:S(2)}, u32[]{:S(2)}) %collective-permute-start.1) | collective-permute-done | bytes 65568 | tf_op jit(solution)/shard_map/ppermute | solution.py:237
  20.7 0.0 collective-permute-start.2
  20.7 0.6 %collective-permute-done.refs_1_ = bf16[64,512]{1,0:T(8,128)(2,1)S(1)} collective-permute-done((bf16[64,512]{1,0:T(8,128)(2,1)S(1)}, bf16[64,512]{1,0:T(8,128)(2,1)S(1)}, u32[]{:S(2)}, u32[]{:S(2)}) %collective-permute-start) | collective-permute-done | bytes 65568 | tf_op jit(solution)/shard_map/ppermute | solution.py:237
  21.3 0.6 %collective-permute-done.2.refs_3_ = bf16[64,512]{1,0:T(8,128)(2,1)S(1)} collective-permute-done((bf16[64,512]{1,0:T(8,128)(2,1)S(1)}, bf16[64,512]{1,0:T(8,128)(2,1)S(1)}, u32[]{:S(2)}, u32[]{:S(2)}) %collective-permute-start.2) | collective-permute-done | bytes 65568 | tf_op jit(solution)/shard_map/ppermute | solution.py:237
  21.9 0.4 %shard_map.49.refs_0_ = bf16[256,512]{1,0:T(8,128)(2,1)S(1)} custom-call(bf16[8,96,128]{2,1,0:T(8,128)(2,1)S(1)} %all-to-all-done.got_ref, bf16[256,256]{1,0:T(8,128)(2,1)S(1)} %get-tuple-element.11.row_ref, bf16[64,512]{1,0:T(8,128)(2,1)S(1)} %copy-done, bf16[64,512]{1,0:T(8,128)(2,1)S(1)} %collective-permute-done.refs_1_, ...), custom_call_target="tpu_custom_call" | custom-call | flops 67108864 | bytes 851968 | tf_op jit(solution)/shard_map/pallas_call | solution.py:211
  22.4 0.0 collective-permute-done.3.refs_3_
  22.4 0.0 collective-permute-done.5.refs_5_
  22.4 1.0 %shard_map.51 = bf16[8,4,8,512]{3,2,1,0:T(8,128)(2,1)} custom-call(bf16[256,512]{1,0:T(8,128)(2,1)S(1)} %shard_map.49.refs_0_, f32[256,512]{1,0:T(8,128)S(1)} %get-tuple-element.12.refs_1_, bf16[512,128]{1,0:T(8,128)(2,1)S(1)} %get-tuple-element.15.refs_2_, bf16[512,128]{1,0:T(8,128)(2,1)S(1)} %collective-permute-done.3.refs_3_, ...), custom_call_target="tpu_custom_call" | custom-call | flops 134217728 | bytes 1572864 | tf_op jit(solution)/shard_map/pallas_call | solution.py:211
  (4 shorter events, 0.0 us)
Async XLA Ops:
  0.0 0.7 %copy-start.1 = (bf16[256,32]{0,1:T(8,128)(2,1)S(1)}, bf16[256,32]{0,1:T(8,128)(2,1)}, u32[]{:S(2)}) copy-start(bf16[256,32]{0,1:T(8,128)(2,1)} %param.4) | copy-start | bytes 49156
  0.0 0.9 %copy-start = (bf16[64,512]{1,0:T(8,128)(2,1)S(1)}, bf16[64,512]{1,0:T(8,128)(2,1)}, u32[]{:S(2)}) copy-start(bf16[64,512]{1,0:T(8,128)(2,1)} %refs_0_.1) | copy-start | bytes 196612
  1.8 12.7 %all-to-all-start = ((bf16[8,96,128]{2,1,0:T(8,128)(2,1)}), bf16[8,96,128]{2,1,0:T(8,128)(2,1)S(1)}, u32[]{:S(2)}, u32[]{:S(2)}) async-start(bf16[8,96,128]{2,1,0:T(8,128)(2,1)} %shard_map.47), calls=%async_computation | async-start | bytes 393216 | tf_op jit(solution)/shard_map/all_to_all | solution.py:254
  9.7 0.7 %copy-start.2 = (f32[64]{0:T(128)S(1)}, f32[64]{0:T(128)}, u32[]{:S(2)}) copy-start(f32[64]{0:T(128)} %param.6) | copy-start | bytes 772
  9.7 0.7 %copy-start.3 = (f32[32]{0:T(128)S(1)}, f32[32]{0:T(128)}, u32[]{:S(2)}) copy-start(f32[32]{0:T(128)} %param.7) | copy-start | bytes 388
  14.8 5.0 %collective-permute-start.4 = (bf16[512,128]{1,0:T(8,128)(2,1)S(1)}, bf16[512,128]{1,0:T(8,128)(2,1)S(1)}, u32[]{:S(2)}, u32[]{:S(2)}) collective-permute-start(bf16[512,128]{1,0:T(8,128)(2,1)S(1)} %get-tuple-element.16), channel_id=1, source_target_pairs={{0,16},{8,24},{16,0},{24,8},{1,17},{9,25},{17,1},{25,9},{2,18},{10... | collective-permute-start | bytes 393224 | tf_op jit(solution)/shard_map/ppermute | solution.py:237
  16.4 4.3 %collective-permute-start.1 = (bf16[64,512]{1,0:T(8,128)(2,1)S(1)}, bf16[64,512]{1,0:T(8,128)(2,1)S(1)}, u32[]{:S(2)}, u32[]{:S(2)}) collective-permute-start(bf16[64,512]{1,0:T(8,128)(2,1)S(1)} %copy-done), channel_id=1, source_target_pairs={{0,16},{8,24},{16,0},{24,8},{1,17},{9,25},{17,1},{25,9},{2,18},{10... | collective-permute-start | bytes 196616 | tf_op jit(solution)/shard_map/ppermute | solution.py:237
  16.9 5.5 %collective-permute-start.3 = (bf16[512,128]{1,0:T(8,128)(2,1)S(1)}, bf16[512,128]{1,0:T(8,128)(2,1)S(1)}, u32[]{:S(2)}, u32[]{:S(2)}) collective-permute-start(bf16[512,128]{1,0:T(8,128)(2,1)S(1)} %get-tuple-element.15.refs_2_), channel_id=1, source_target_pairs={{0,8},{8,0},{16,24},{24,16},{1,9},{9,1},{17,25},{25,17},{2,10},{10... | collective-permute-start | bytes 393224 | tf_op jit(solution)/shard_map/ppermute | solution.py:237
  19.9 2.5 %collective-permute-start.5 = (bf16[512,128]{1,0:T(8,128)(2,1)S(1)}, bf16[512,128]{1,0:T(8,128)(2,1)S(1)}, u32[]{:S(2)}, u32[]{:S(2)}) collective-permute-start(bf16[512,128]{1,0:T(8,128)(2,1)S(1)} %collective-permute-done.4.refs_4_), channel_id=1, source_target_pairs={{0,8},{8,0},{16,24},{24,16},{1,9},{9,1},{17,25},{25,17},{2,10},{10... | collective-permute-start | bytes 393224 | tf_op jit(solution)/shard_map/ppermute | solution.py:237
  19.9 1.4 %collective-permute-start = (bf16[64,512]{1,0:T(8,128)(2,1)S(1)}, bf16[64,512]{1,0:T(8,128)(2,1)S(1)}, u32[]{:S(2)}, u32[]{:S(2)}) collective-permute-start(bf16[64,512]{1,0:T(8,128)(2,1)S(1)} %copy-done), channel_id=1, source_target_pairs={{0,8},{8,0},{16,24},{24,16},{1,9},{9,1},{17,25},{25,17},{2,10},{10... | collective-permute-start | bytes 196616 | tf_op jit(solution)/shard_map/ppermute | solution.py:237
  20.7 1.3 %collective-permute-start.2 = (bf16[64,512]{1,0:T(8,128)(2,1)S(1)}, bf16[64,512]{1,0:T(8,128)(2,1)S(1)}, u32[]{:S(2)}, u32[]{:S(2)}) collective-permute-start(bf16[64,512]{1,0:T(8,128)(2,1)S(1)} %collective-permute-done.1.refs_2_), channel_id=1, source_target_pairs={{0,8},{8,0},{16,24},{24,16},{1,9},{9,1},{17,25},{25,17},{2,10},{10... | collective-permute-start | bytes 196616 | tf_op jit(solution)/shard_map/ppermute | solution.py:237

commit v7 on v6

--- a/solution.py
+++ b/solution.py
@@ -1,4 +1,5 @@
 import functools
+import math
 
 import jax
 import jax.numpy as jnp
@@ -38,7 +39,7 @@
     up, down = list(range(half, n)), list(reversed(range(half)))
     order = []
     for at in range(0, max(len(up), len(down)), chunk):
-        order += sorted(up[at : at + chunk], reverse=at > 0) + down[at : at + chunk]
+        order += list(reversed(up[at : at + chunk])) + down[at : at + chunk]
     return order
 
 
@@ -93,7 +94,7 @@
     )
 
 
-def split_kernel(vir_parts, occ_own, high, deep, got_ref, amp_ref, int_ref, send_ref, keep_ref):
+def split_kernel(vir_parts, occ_own, high, deep, got_ref, send_ref, keep_ref):
     parts, _, lanes = got_ref.shape
     square = occ_own * occ_own
     cols = parts * square
@@ -105,12 +106,18 @@
         for h in range(lanes // square)
     ]
     amps = jnp.concatenate(halves, axis=0).astype(BF16)
-    amps = jnp.dot(amps, amp_ref[...], preferred_element_type=F32).astype(BF16)
-    ints = choose_rows(int_ref[...], integral_columns(got_ref, high, deep))
+    col, occ_all = columns(cols), parts * occ_own
+    source = (col % occ_all // occ_own) * square + (col % occ_own) * occ_own + col // occ_all
+    amps = jnp.dot(amps, one_hot(cols, source), preferred_element_type=F32).astype(BF16)
+    ints = integral_columns(got_ref, high, deep)
+    total, rows = ints.shape
+    area = rows // vir_parts
+    outer, other, inner = row_parts(rows, vir_parts)
+    vir_own = math.isqrt(area)
+    source = inner * (vir_parts * vir_own) + other + outer
+    ints = choose_rows(one_hot_rows(source, rows), ints)
     depth = amps.shape[0]
     base = cols // lanes * depth
-    rows, total = ints.shape
-    area = rows // vir_parts
     kept = (send_ref.shape[0] - base) // (area * (total // lanes))
     for ref, first in ((send_ref, vir_parts - kept), (keep_ref, 0)):
         for c in range(cols // lanes):
@@ -124,19 +131,18 @@
                 at += area
 
 
-def prepare_kernel(sizes, occ_ref, vir_ref, amp_ref, int_ref, row_ref, inv_ref):
-    vir_parts, vir_own, occ_own = sizes
+def row_parts(rows, vir_parts):
+    area = rows // vir_parts
+    own = math.isqrt(area)
+    row = lax.broadcasted_iota(jnp.int32, (rows, 1), 0)
+    other = jnp.bitwise_xor(row // area, lax.axis_index("vv")) * own
+    return row % area // own, other, row % own
+
+
+def prepare_kernel(vir_parts, occ_own, occ_ref, vir_ref, row_ref, inv_ref):
     rows, cols = inv_ref.shape
-    vir_all, occ_all = vir_parts * vir_own, occ_ref.shape[1]
-    square, area = occ_own * occ_own, vir_own * vir_own
-    me = lax.axis_index("vv")
-    col = columns(cols)
-    source = (col % occ_all // occ_own) * square + (col % occ_own) * occ_own + col // occ_all
-    amp_ref[...] = one_hot(cols, source)
-    row = lax.broadcasted_iota(jnp.int32, (rows, 1), 0)
-    other = jnp.bitwise_xor(row // area, me) * vir_own
-    outer, inner = row % area // vir_own, row % vir_own
-    int_ref[...] = one_hot_rows(inner * vir_all + other + outer, rows)
+    vir_all, occ_all = vir_ref.shape[1], occ_ref.shape[1]
+    outer, other, inner = row_parts(rows, vir_parts)
     row_ref[...] = one_hot_rows(outer * vir_all + other + inner, rows)
     occ = occ_ref[...]
     occ_column = pick_sum(occ, square_eye(occ_all), 1)
@@ -145,7 +151,8 @@
     occ_pair = occ_mine + jnp.concatenate([occ] * occ_own, axis=1)
     lane = lax.broadcasted_iota(jnp.int32, (rows, vir_all), 1)
     vir = vir_ref[...]
-    vir_mine = pick_sum(vir, lane == me * vir_own + outer, 1)
+    mine = lax.axis_index("vv") * (vir_all // vir_parts) + outer
+    vir_mine = pick_sum(vir, lane == mine, 1)
     vir_other = pick_sum(vir, lane == other + inner, 1)
     inv_ref[...] = 1.0 / (occ_pair - vir_mine - vir_other)
 
@@ -252,17 +259,18 @@
         flops=2 * depth * cols * cols,
     )
     got = lax.all_to_all(packed, "oo", 0, 0, tiled=True, axis_index_groups=[middle_out(occ_parts)])
-    to_amps, to_ints, to_rows, inverse = call(
-        functools.partial(prepare_kernel, (vir_parts, vir_own, occ_own)),
-        [struct(cols, cols), struct(rows, rows), struct(rows, rows), struct(rows, cols, dtype=F32)],
+    to_rows, inverse = call(
+        functools.partial(prepare_kernel, vir_parts, occ_own),
+        [struct(rows, rows), struct(rows, cols, dtype=F32)],
         (occ_energy.reshape(1, occ_all), vir_energy.reshape(1, vir_all)),
+        flops=10 * rows * cols,
     )
 
     amp_rows, int_rows = cols // LANES * depth, total // LANES * area
     send, keep = call(
         functools.partial(split_kernel, vir_parts, occ_own, high, deep),
         [struct(amp_rows + vir_parts // 2 * int_rows, LANES)] * 2,
-        (got, to_amps, to_ints),
+        (got,),
         flops=2 * depth * cols * cols + 2 * total * rows * rows,
     )
     held = {0: (send, keep)}

time: 23.7 us -> 22.2 us (0.937)
  blocking collectives: 0 us -> 11.8 us
  starting transfers between devices: 10.4 us -> 2.61 us
  waiting for transfers between devices: 8.24 us -> 3.59 us
  Pallas kernels: 3.18 us -> 2.34 us
    all_to_all x0 -> x1, blocking collectives: none -> 11.8 us  [on_device(): lax.all_to_all(packed, 'oo', 0, 0, tiled=True, axis_index_groups=[middle_...]
    all_to_all x1 -> x0, starting transfers between devices: 7.84 us -> none  [on_device(): lax.all_to_all(packed, 'oo', 0, 0, tiled=True, axis_index_groups=[middle_...]
    all_to_all x1 -> x0, waiting for transfers between devices: 3.74 us -> none  [on_device(): lax.all_to_all(packed, 'oo', 0, 0, tiled=True, axis_index_groups=[middle_...]
    ppermute x6, waiting for transfers between devices: 4.5 us -> 3.59 us  [swap(): return lax.ppermute(x, 'vv', [(k, k ^ step) for k in range(vir_parts)])]
    pallas_call x6, Pallas kernels: 3.18 us -> 2.34 us  [call(): pl.pallas_call(kernel, out_shape=outs, in_specs=[pl.BlockSpec(memory_spac...]
  transfers between devices with their start and end apart: 7 -> 6, of which waited for: 5 -> 3; matrix products, arithmetic and copies ran while one was open for 0% -> 0% of each run, Pallas kernels for 4% -> 3%
where the time goes in v7:
time: 22.2 us; the launch traced here: 21.9 us
  blocking collectives  11.8 us (53%)
  waiting for transfers between devices  3.59 us (16%)
  starting transfers between devices  2.61 us (12%)
  Pallas kernels  2.34 us (11%)
  local copies, waits for them, and re-layouts  1.51 us (7%)
    all_to_all x1, blocking collectives, on_device(): lax.all_to_all(packed, 'oo', 0, 0, tiled=True, axis_index_groups=[middle_...  11.8 us
    ppermute x6, waiting for transfers between devices, swap(): return lax.ppermute(x, 'vv', [(k, k ^ step) for k in range(vir_parts)])  3.59 us
    ppermute x6, starting transfers between devices, swap(): return lax.ppermute(x, 'vv', [(k, k ^ step) for k in range(vir_parts)])  2.61 us
    pallas_call x6, Pallas kernels, call(): pl.pallas_call(kernel, out_shape=outs, in_specs=[pl.BlockSpec(memory_spac...  2.34 us
    unnamed x8, local copies, waits for them, and re-layouts  1.51 us
  transfers between devices with their start and end apart: 6, of which 3 were waited for; matrix products, arithmetic and copies ran while one was open for 0% of the time, Pallas kernels for 3%

profile of v7, /device:TPU:0, one launch (start us, length us, event | category | flops | bytes accessed | tf_op | source)
XLA Modules:
  0.0 21.9 jit_solution(11964690851934762725)
XLA Ops:
  0.0 0.0 copy-start.1
  0.0 0.0 copy-start
  0.0 0.7 %copy-done.1 = bf16[256,32]{0,1:T(8,128)(2,1)S(1)} copy-done((bf16[256,32]{0,1:T(8,128)(2,1)S(1)}, bf16[256,32]{0,1:T(8,128)(2,1)}, u32[]{:S(2)}) %copy-start.1) | copy-done | bytes 16408
  0.7 0.1 copy-done
  0.9 0.3 %shard_map.47 = bf16[8,96,128]{2,1,0:T(8,128)(2,1)S(1)} custom-call(bf16[64,512]{1,0:T(8,128)(2,1)S(1)} %copy-done, bf16[32,256]{1,0:T(8,128)(2,1)S(1)} %bitcast.4, s32[1,512]{1,0:T(1,128)S(1)} %shard_map.46.source_ref), custom_call_target="tpu_custom_call" | custom-call | flops 33554432 | bytes 280576 | tf_op jit(solution)/shard_map/pallas_call | solution.py:218
  1.1 11.8 %all_to_all.5.got_ref = bf16[8,96,128]{2,1,0:T(8,128)(2,1)S(1)} all-to-all(bf16[8,96,128]{2,1,0:T(8,128)(2,1)S(1)} %shard_map.47), channel_id=1, replica_groups={{5,4,3,2,7,6,1,0},{13,12,11,10,15,14,9,8},{21,20,19,18,23,22,17,16},{29..., dimensions={0} | all-to-all | bytes 393216 | tf_op jit(solution)/shard_map/all_to_all | solution.py:261
  13.0 0.4 %shard_map.50 = (bf16[512,128]{1,0:T(8,128)(2,1)S(1)}, bf16[512,128]{1,0:T(8,128)(2,1)S(1)}) custom-call(bf16[8,96,128]{2,1,0:T(8,128)(2,1)S(1)} %all_to_all.5.got_ref), custom_call_target="tpu_custom_call" | custom-call | flops 67108864 | bytes 458752 | tf_op jit(solution)/shard_map/pallas_call | solution.py:218
  13.3 1.6 %collective-permute-start.4 = (bf16[512,128]{1,0:T(8,128)(2,1)S(1)}, bf16[512,128]{1,0:T(8,128)(2,1)S(1)}, u32[]{:S(2)}, u32[]{:S(2)}) collective-permute-start(bf16[512,128]{1,0:T(8,128)(2,1)S(1)} %get-tuple-element.12), channel_id=1, source_target_pairs={{0,16},{8,24},{16,0},{24,8},{1,17},{9,25},{17,1},{25,9},{2,18},{10... | collective-permute-start | bytes 393224 | tf_op jit(solution)/shard_map/ppermute | solution.py:244
  14.9 0.5 %collective-permute-start.1 = (bf16[64,512]{1,0:T(8,128)(2,1)S(1)}, bf16[64,512]{1,0:T(8,128)(2,1)S(1)}, u32[]{:S(2)}, u32[]{:S(2)}) collective-permute-start(bf16[64,512]{1,0:T(8,128)(2,1)S(1)} %copy-done), channel_id=1, source_target_pairs={{0,16},{8,24},{16,0},{24,8},{1,17},{9,25},{17,1},{25,9},{2,18},{10... | collective-permute-start | bytes 196616 | tf_op jit(solution)/shard_map/ppermute | solution.py:244
  15.4 0.0 collective-permute-start.3
  15.4 2.9 %collective-permute-done.4.refs_4_ = bf16[512,128]{1,0:T(8,128)(2,1)S(1)} collective-permute-done((bf16[512,128]{1,0:T(8,128)(2,1)S(1)}, bf16[512,128]{1,0:T(8,128)(2,1)S(1)}, u32[]{:S(2)}, u32[]{:S(2)}) %collective-permute-start.4) | collective-permute-done | bytes 131104 | tf_op jit(solution)/shard_map/ppermute | solution.py:244
  18.4 0.0 collective-permute-start.5
  18.4 0.5 %collective-permute-start = (bf16[64,512]{1,0:T(8,128)(2,1)S(1)}, bf16[64,512]{1,0:T(8,128)(2,1)S(1)}, u32[]{:S(2)}, u32[]{:S(2)}) collective-permute-start(bf16[64,512]{1,0:T(8,128)(2,1)S(1)} %copy-done), channel_id=1, source_target_pairs={{0,8},{8,0},{16,24},{24,16},{1,9},{9,1},{17,25},{25,17},{2,10},{10... | collective-permute-start | bytes 196616 | tf_op jit(solution)/shard_map/ppermute | solution.py:244
  18.9 0.3 %collective-permute-done.1.refs_2_ = bf16[64,512]{1,0:T(8,128)(2,1)S(1)} collective-permute-done((bf16[64,512]{1,0:T(8,128)(2,1)S(1)}, bf16[64,512]{1,0:T(8,128)(2,1)S(1)}, u32[]{:S(2)}, u32[]{:S(2)}) %collective-permute-start.1) | collective-permute-done | bytes 65568 | tf_op jit(solution)/shard_map/ppermute | solution.py:244
  19.2 0.0 collective-permute-start.2
  19.2 0.7 %copy-done.2 = f32[64]{0:T(128)S(1)} copy-done((f32[64]{0:T(128)S(1)}, f32[64]{0:T(128)}, u32[]{:S(2)}) %copy-start.2) | copy-done | bytes 280
  19.9 0.0 copy-done.3
  19.9 0.2 %shard_map.48 = (bf16[256,256]{1,0:T(8,128)(2,1)S(1)}, f32[256,512]{1,0:T(8,128)S(1)}) custom-call(f32[1,64]{1,0:T(1,128)S(1)} %bitcast.5, f32[1,32]{1,0:T(1,128)S(1)} %bitcast.6), custom_call_target="tpu_custom_call" | custom-call | flops 1310720 | bytes 655744 | tf_op jit(solution)/shard_map/pallas_call | solution.py:218
  20.1 0.0 collective-permute-done.refs_1_
  20.1 0.3 %collective-permute-done.2.refs_3_ = bf16[64,512]{1,0:T(8,128)(2,1)S(1)} collective-permute-done((bf16[64,512]{1,0:T(8,128)(2,1)S(1)}, bf16[64,512]{1,0:T(8,128)(2,1)S(1)}, u32[]{:S(2)}, u32[]{:S(2)}) %collective-permute-start.2) | collective-permute-done | bytes 65568 | tf_op jit(solution)/shard_map/ppermute | solution.py:244
  20.5 0.4 %shard_map.49.refs_0_ = bf16[256,512]{1,0:T(8,128)(2,1)S(1)} custom-call(bf16[8,96,128]{2,1,0:T(8,128)(2,1)S(1)} %all_to_all.5.got_ref, bf16[256,256]{1,0:T(8,128)(2,1)S(1)} %get-tuple-element.9.row_ref, bf16[64,512]{1,0:T(8,128)(2,1)S(1)} %copy-done, bf16[64,512]{1,0:T(8,128)(2,1)S(1)} %collective-permute-done.refs_1_, ...), custom_call_target="tpu_custom_call" | custom-call | flops 67108864 | bytes 851968 | tf_op jit(solution)/shard_map/pallas_call | solution.py:218
  20.9 0.0 collective-permute-done.3.refs_3_
  20.9 0.0 collective-permute-done.5.refs_5_
  20.9 1.0 %shard_map.51 = bf16[8,4,8,512]{3,2,1,0:T(8,128)(2,1)} custom-call(bf16[256,512]{1,0:T(8,128)(2,1)S(1)} %shard_map.49.refs_0_, f32[256,512]{1,0:T(8,128)S(1)} %get-tuple-element.10.refs_1_, bf16[512,128]{1,0:T(8,128)(2,1)S(1)} %get-tuple-element.11.refs_2_, bf16[512,128]{1,0:T(8,128)(2,1)S(1)} %collective-permute-done.3.refs_3_, ...), custom_call_target="tpu_custom_call" | custom-call | flops 134217728 | bytes 1572864 | tf_op jit(solution)/shard_map/pallas_call | solution.py:218
  (3 shorter events, 0.0 us)
Async XLA Ops:
  0.0 0.7 %copy-start.1 = (bf16[256,32]{0,1:T(8,128)(2,1)S(1)}, bf16[256,32]{0,1:T(8,128)(2,1)}, u32[]{:S(2)}) copy-start(bf16[256,32]{0,1:T(8,128)(2,1)} %param.4) | copy-start | bytes 49156
  0.0 0.9 %copy-start = (bf16[64,512]{1,0:T(8,128)(2,1)S(1)}, bf16[64,512]{1,0:T(8,128)(2,1)}, u32[]{:S(2)}) copy-start(bf16[64,512]{1,0:T(8,128)(2,1)} %refs_0_.1) | copy-start | bytes 196612
  13.3 5.0 %collective-permute-start.4 = (bf16[512,128]{1,0:T(8,128)(2,1)S(1)}, bf16[512,128]{1,0:T(8,128)(2,1)S(1)}, u32[]{:S(2)}, u32[]{:S(2)}) collective-permute-start(bf16[512,128]{1,0:T(8,128)(2,1)S(1)} %get-tuple-element.12), channel_id=1, source_target_pairs={{0,16},{8,24},{16,0},{24,8},{1,17},{9,25},{17,1},{25,9},{2,18},{10... | collective-permute-start | bytes 393224 | tf_op jit(solution)/shard_map/ppermute | solution.py:244
  14.9 4.3 %collective-permute-start.1 = (bf16[64,512]{1,0:T(8,128)(2,1)S(1)}, bf16[64,512]{1,0:T(8,128)(2,1)S(1)}, u32[]{:S(2)}, u32[]{:S(2)}) collective-permute-start(bf16[64,512]{1,0:T(8,128)(2,1)S(1)} %copy-done), channel_id=1, source_target_pairs={{0,16},{8,24},{16,0},{24,8},{1,17},{9,25},{17,1},{25,9},{2,18},{10... | collective-permute-start | bytes 196616 | tf_op jit(solution)/shard_map/ppermute | solution.py:244
  15.4 5.5 %collective-permute-start.3 = (bf16[512,128]{1,0:T(8,128)(2,1)S(1)}, bf16[512,128]{1,0:T(8,128)(2,1)S(1)}, u32[]{:S(2)}, u32[]{:S(2)}) collective-permute-start(bf16[512,128]{1,0:T(8,128)(2,1)S(1)} %get-tuple-element.11.refs_2_), channel_id=1, source_target_pairs={{0,8},{8,0},{16,24},{24,16},{1,9},{9,1},{17,25},{25,17},{2,10},{10... | collective-permute-start | bytes 393224 | tf_op jit(solution)/shard_map/ppermute | solution.py:244
  18.4 2.5 %collective-permute-start.5 = (bf16[512,128]{1,0:T(8,128)(2,1)S(1)}, bf16[512,128]{1,0:T(8,128)(2,1)S(1)}, u32[]{:S(2)}, u32[]{:S(2)}) collective-permute-start(bf16[512,128]{1,0:T(8,128)(2,1)S(1)} %collective-permute-done.4.refs_4_), channel_id=1, source_target_pairs={{0,8},{8,0},{16,24},{24,16},{1,9},{9,1},{17,25},{25,17},{2,10},{10... | collective-permute-start | bytes 393224 | tf_op jit(solution)/shard_map/ppermute | solution.py:244
  18.4 1.7 %collective-permute-start = (bf16[64,512]{1,0:T(8,128)(2,1)S(1)}, bf16[64,512]{1,0:T(8,128)(2,1)S(1)}, u32[]{:S(2)}, u32[]{:S(2)}) collective-permute-start(bf16[64,512]{1,0:T(8,128)(2,1)S(1)} %copy-done), channel_id=1, source_target_pairs={{0,8},{8,0},{16,24},{24,16},{1,9},{9,1},{17,25},{25,17},{2,10},{10... | collective-permute-start | bytes 196616 | tf_op jit(solution)/shard_map/ppermute | solution.py:244
  19.2 1.3 %collective-permute-start.2 = (bf16[64,512]{1,0:T(8,128)(2,1)S(1)}, bf16[64,512]{1,0:T(8,128)(2,1)S(1)}, u32[]{:S(2)}, u32[]{:S(2)}) collective-permute-start(bf16[64,512]{1,0:T(8,128)(2,1)S(1)} %collective-permute-done.1.refs_2_), channel_id=1, source_target_pairs={{0,8},{8,0},{16,24},{24,16},{1,9},{9,1},{17,25},{25,17},{2,10},{10... | collective-permute-start | bytes 196616 | tf_op jit(solution)/shard_map/ppermute | solution.py:244
  19.2 0.7 %copy-start.2 = (f32[64]{0:T(128)S(1)}, f32[64]{0:T(128)}, u32[]{:S(2)}) copy-start(f32[64]{0:T(128)} %param.6) | copy-start | bytes 772
  19.2 0.7 %copy-start.3 = (f32[32]{0:T(128)S(1)}, f32[32]{0:T(128)}, u32[]{:S(2)}) copy-start(f32[32]{0:T(128)} %param.7) | copy-start | bytes 388

commit v8 on v7

--- a/solution.py
+++ b/solution.py
@@ -98,14 +98,14 @@
     parts, _, lanes = got_ref.shape
     square = occ_own * occ_own
     cols = parts * square
-    packed = got_ref[:, :high, :].astype(F32)
+    packed = got_ref[:, :high, :]
     halves = [
         jnp.concatenate(
             [packed[at, :, h * square : (h + 1) * square] for at in places(parts)], axis=1
         )
         for h in range(lanes // square)
     ]
-    amps = jnp.concatenate(halves, axis=0).astype(BF16)
+    amps = jnp.concatenate(halves, axis=0)
     col, occ_all = columns(cols), parts * occ_own
     source = (col % occ_all // occ_own) * square + (col % occ_own) * occ_own + col // occ_all
     amps = jnp.dot(amps, one_hot(cols, source), preferred_element_type=F32).astype(BF16)
@@ -179,7 +179,7 @@
 def mirror_kernel(depth, *refs):
     lad_ref, inv_ref, *got_refs, out_hbm, all_ref, out_ref, sems = refs
     me = lax.axis_index("vv")
-    _, own, _, cols = out_ref.shape
+    vir_parts, own, _, cols = out_ref.shape
     total = all_ref.shape[0]
     area = own * own
     chunks = cols // LANES
@@ -189,18 +189,23 @@
             all_ref[pl.ds(at, depth), c * LANES : (c + 1) * LANES] = ref[c * depth : (c + 1) * depth, :]
     base = chunks * depth
     stores = []
+    ints = []
     for rel, ref in enumerate(got_refs):
         first = base + (rel % 2) * area * (total // LANES)
-        ints = jnp.concatenate(
-            [
-                ref[first + c * area : first + (c + 1) * area, :]
-                for c in range(total // LANES)
-            ],
-            axis=1,
+        ints.append(
+            jnp.concatenate(
+                [
+                    ref[first + c * area : first + (c + 1) * area, :]
+                    for c in range(total // LANES)
+                ],
+                axis=1,
+            )
         )
-        mirrored = jnp.dot(ints, all_ref[...], preferred_element_type=F32)
+    ints = jnp.concatenate(ints, axis=0)
+    product = jnp.dot(ints, all_ref[...], preferred_element_type=F32)
+    for rel in range(vir_parts):
         some = slice(rel * area, (rel + 1) * area)
-        both = lad_ref[some, :].astype(F32) + mirrored.astype(BF16).astype(F32)
+        both = lad_ref[some, :].astype(F32) + product[some].astype(BF16).astype(F32)
         both = both * inv_ref[some, :]
         out_ref[rel] = both.reshape(own, own, cols).astype(BF16)
         other = jnp.bitwise_xor(me, rel)

time: 22.2 us -> 22.1 us (level)
  no operation moved by 1% of the time
where the time goes in v8:
time: 22.1 us; the launch traced here: 21.9 us
  blocking collectives  11.8 us (53%)
  waiting for transfers between devices  3.59 us (16%)
  starting transfers between devices  2.61 us (12%)
  Pallas kernels  2.27 us (10%)
  local copies, waits for them, and re-layouts  1.51 us (7%)
    all_to_all x1, blocking collectives, on_device(): lax.all_to_all(packed, 'oo', 0, 0, tiled=True, axis_index_groups=[middle_...  11.8 us
    ppermute x6, waiting for transfers between devices, swap(): return lax.ppermute(x, 'vv', [(k, k ^ step) for k in range(vir_parts)])  3.59 us
    ppermute x6, starting transfers between devices, swap(): return lax.ppermute(x, 'vv', [(k, k ^ step) for k in range(vir_parts)])  2.61 us
    pallas_call x6, Pallas kernels, call(): pl.pallas_call(kernel, out_shape=outs, in_specs=[pl.BlockSpec(memory_spac...  2.27 us
    unnamed x8, local copies, waits for them, and re-layouts  1.51 us
  transfers between devices with their start and end apart: 6, of which 3 were waited for; matrix products, arithmetic and copies ran while one was open for 0% of the time, Pallas kernels for 3%

profile of v8, /device:TPU:0, one launch (start us, length us, event | category | flops | bytes accessed | tf_op | source)
XLA Modules:
  0.0 21.9 jit_solution(5187529805006453158)
XLA Ops:
  0.0 0.0 copy-start.1
  0.0 0.0 copy-start
  0.0 0.7 %copy-done.1 = bf16[256,32]{0,1:T(8,128)(2,1)S(1)} copy-done((bf16[256,32]{0,1:T(8,128)(2,1)S(1)}, bf16[256,32]{0,1:T(8,128)(2,1)}, u32[]{:S(2)}) %copy-start.1) | copy-done | bytes 16408
  0.7 0.1 copy-done
  0.9 0.3 %shard_map.47 = bf16[8,96,128]{2,1,0:T(8,128)(2,1)S(1)} custom-call(bf16[64,512]{1,0:T(8,128)(2,1)S(1)} %copy-done, bf16[32,256]{1,0:T(8,128)(2,1)S(1)} %bitcast.4, s32[1,512]{1,0:T(1,128)S(1)} %shard_map.46.source_ref), custom_call_target="tpu_custom_call" | custom-call | flops 33554432 | bytes 280576 | tf_op jit(solution)/shard_map/pallas_call | solution.py:223
  1.1 11.8 %all_to_all.5.got_ref = bf16[8,96,128]{2,1,0:T(8,128)(2,1)S(1)} all-to-all(bf16[8,96,128]{2,1,0:T(8,128)(2,1)S(1)} %shard_map.47), channel_id=1, replica_groups={{5,4,3,2,7,6,1,0},{13,12,11,10,15,14,9,8},{21,20,19,18,23,22,17,16},{29..., dimensions={0} | all-to-all | bytes 393216 | tf_op jit(solution)/shard_map/all_to_all | solution.py:266
  13.0 0.3 %shard_map.50 = (bf16[512,128]{1,0:T(8,128)(2,1)S(1)}, bf16[512,128]{1,0:T(8,128)(2,1)S(1)}) custom-call(bf16[8,96,128]{2,1,0:T(8,128)(2,1)S(1)} %all_to_all.5.got_ref), custom_call_target="tpu_custom_call" | custom-call | flops 67108864 | bytes 458752 | tf_op jit(solution)/shard_map/pallas_call | solution.py:223
  13.3 1.6 %collective-permute-start.4 = (bf16[512,128]{1,0:T(8,128)(2,1)S(1)}, bf16[512,128]{1,0:T(8,128)(2,1)S(1)}, u32[]{:S(2)}, u32[]{:S(2)}) collective-permute-start(bf16[512,128]{1,0:T(8,128)(2,1)S(1)} %get-tuple-element.12), channel_id=1, source_target_pairs={{0,16},{8,24},{16,0},{24,8},{1,17},{9,25},{17,1},{25,9},{2,18},{10... | collective-permute-start | bytes 393224 | tf_op jit(solution)/shard_map/ppermute | solution.py:249
  14.9 0.5 %collective-permute-start.1 = (bf16[64,512]{1,0:T(8,128)(2,1)S(1)}, bf16[64,512]{1,0:T(8,128)(2,1)S(1)}, u32[]{:S(2)}, u32[]{:S(2)}) collective-permute-start(bf16[64,512]{1,0:T(8,128)(2,1)S(1)} %copy-done), channel_id=1, source_target_pairs={{0,16},{8,24},{16,0},{24,8},{1,17},{9,25},{17,1},{25,9},{2,18},{10... | collective-permute-start | bytes 196616 | tf_op jit(solution)/shard_map/ppermute | solution.py:249
  15.4 0.0 collective-permute-start.3
  15.4 2.9 %collective-permute-done.4.refs_4_ = bf16[512,128]{1,0:T(8,128)(2,1)S(1)} collective-permute-done((bf16[512,128]{1,0:T(8,128)(2,1)S(1)}, bf16[512,128]{1,0:T(8,128)(2,1)S(1)}, u32[]{:S(2)}, u32[]{:S(2)}) %collective-permute-start.4) | collective-permute-done | bytes 131104 | tf_op jit(solution)/shard_map/ppermute | solution.py:249
  18.4 0.0 collective-permute-start.5
  18.4 0.5 %collective-permute-start = (bf16[64,512]{1,0:T(8,128)(2,1)S(1)}, bf16[64,512]{1,0:T(8,128)(2,1)S(1)}, u32[]{:S(2)}, u32[]{:S(2)}) collective-permute-start(bf16[64,512]{1,0:T(8,128)(2,1)S(1)} %copy-done), channel_id=1, source_target_pairs={{0,8},{8,0},{16,24},{24,16},{1,9},{9,1},{17,25},{25,17},{2,10},{10... | collective-permute-start | bytes 196616 | tf_op jit(solution)/shard_map/ppermute | solution.py:249
  18.9 0.3 %collective-permute-done.1.refs_2_ = bf16[64,512]{1,0:T(8,128)(2,1)S(1)} collective-permute-done((bf16[64,512]{1,0:T(8,128)(2,1)S(1)}, bf16[64,512]{1,0:T(8,128)(2,1)S(1)}, u32[]{:S(2)}, u32[]{:S(2)}) %collective-permute-start.1) | collective-permute-done | bytes 65568 | tf_op jit(solution)/shard_map/ppermute | solution.py:249
  19.2 0.0 collective-permute-start.2
  19.2 0.7 %copy-done.2 = f32[64]{0:T(128)S(1)} copy-done((f32[64]{0:T(128)S(1)}, f32[64]{0:T(128)}, u32[]{:S(2)}) %copy-start.2) | copy-done | bytes 280
  19.8 0.0 copy-done.3
  19.9 0.2 %shard_map.48 = (bf16[256,256]{1,0:T(8,128)(2,1)S(1)}, f32[256,512]{1,0:T(8,128)S(1)}) custom-call(f32[1,64]{1,0:T(1,128)S(1)} %bitcast.5, f32[1,32]{1,0:T(1,128)S(1)} %bitcast.6), custom_call_target="tpu_custom_call" | custom-call | flops 1310720 | bytes 655744 | tf_op jit(solution)/shard_map/pallas_call | solution.py:223
  20.1 0.0 collective-permute-done.refs_1_
  20.1 0.3 %collective-permute-done.2.refs_3_ = bf16[64,512]{1,0:T(8,128)(2,1)S(1)} collective-permute-done((bf16[64,512]{1,0:T(8,128)(2,1)S(1)}, bf16[64,512]{1,0:T(8,128)(2,1)S(1)}, u32[]{:S(2)}, u32[]{:S(2)}) %collective-permute-start.2) | collective-permute-done | bytes 65568 | tf_op jit(solution)/shard_map/ppermute | solution.py:249
  20.4 0.4 %shard_map.49.refs_0_ = bf16[256,512]{1,0:T(8,128)(2,1)S(1)} custom-call(bf16[8,96,128]{2,1,0:T(8,128)(2,1)S(1)} %all_to_all.5.got_ref, bf16[256,256]{1,0:T(8,128)(2,1)S(1)} %get-tuple-element.9.row_ref, bf16[64,512]{1,0:T(8,128)(2,1)S(1)} %copy-done, bf16[64,512]{1,0:T(8,128)(2,1)S(1)} %collective-permute-done.refs_1_, ...), custom_call_target="tpu_custom_call" | custom-call | flops 67108864 | bytes 851968 | tf_op jit(solution)/shard_map/pallas_call | solution.py:223
  20.9 0.0 collective-permute-done.3.refs_3_
  20.9 0.0 collective-permute-done.5.refs_5_
  20.9 1.0 %shard_map.51 = bf16[8,4,8,512]{3,2,1,0:T(8,128)(2,1)} custom-call(bf16[256,512]{1,0:T(8,128)(2,1)S(1)} %shard_map.49.refs_0_, f32[256,512]{1,0:T(8,128)S(1)} %get-tuple-element.10.refs_1_, bf16[512,128]{1,0:T(8,128)(2,1)S(1)} %get-tuple-element.11.refs_2_, bf16[512,128]{1,0:T(8,128)(2,1)S(1)} %collective-permute-done.3.refs_3_, ...), custom_call_target="tpu_custom_call" | custom-call | flops 134217728 | bytes 1572864 | tf_op jit(solution)/shard_map/pallas_call | solution.py:223
  (3 shorter events, 0.0 us)
Async XLA Ops:
  0.0 0.7 %copy-start.1 = (bf16[256,32]{0,1:T(8,128)(2,1)S(1)}, bf16[256,32]{0,1:T(8,128)(2,1)}, u32[]{:S(2)}) copy-start(bf16[256,32]{0,1:T(8,128)(2,1)} %param.4) | copy-start | bytes 49156
  0.0 0.9 %copy-start = (bf16[64,512]{1,0:T(8,128)(2,1)S(1)}, bf16[64,512]{1,0:T(8,128)(2,1)}, u32[]{:S(2)}) copy-start(bf16[64,512]{1,0:T(8,128)(2,1)} %refs_0_.1) | copy-start | bytes 196612
  13.3 5.0 %collective-permute-start.4 = (bf16[512,128]{1,0:T(8,128)(2,1)S(1)}, bf16[512,128]{1,0:T(8,128)(2,1)S(1)}, u32[]{:S(2)}, u32[]{:S(2)}) collective-permute-start(bf16[512,128]{1,0:T(8,128)(2,1)S(1)} %get-tuple-element.12), channel_id=1, source_target_pairs={{0,16},{8,24},{16,0},{24,8},{1,17},{9,25},{17,1},{25,9},{2,18},{10... | collective-permute-start | bytes 393224 | tf_op jit(solution)/shard_map/ppermute | solution.py:249
  14.9 4.3 %collective-permute-start.1 = (bf16[64,512]{1,0:T(8,128)(2,1)S(1)}, bf16[64,512]{1,0:T(8,128)(2,1)S(1)}, u32[]{:S(2)}, u32[]{:S(2)}) collective-permute-start(bf16[64,512]{1,0:T(8,128)(2,1)S(1)} %copy-done), channel_id=1, source_target_pairs={{0,16},{8,24},{16,0},{24,8},{1,17},{9,25},{17,1},{25,9},{2,18},{10... | collective-permute-start | bytes 196616 | tf_op jit(solution)/shard_map/ppermute | solution.py:249
  15.4 5.5 %collective-permute-start.3 = (bf16[512,128]{1,0:T(8,128)(2,1)S(1)}, bf16[512,128]{1,0:T(8,128)(2,1)S(1)}, u32[]{:S(2)}, u32[]{:S(2)}) collective-permute-start(bf16[512,128]{1,0:T(8,128)(2,1)S(1)} %get-tuple-element.11.refs_2_), channel_id=1, source_target_pairs={{0,8},{8,0},{16,24},{24,16},{1,9},{9,1},{17,25},{25,17},{2,10},{10... | collective-permute-start | bytes 393224 | tf_op jit(solution)/shard_map/ppermute | solution.py:249
  18.4 2.5 %collective-permute-start.5 = (bf16[512,128]{1,0:T(8,128)(2,1)S(1)}, bf16[512,128]{1,0:T(8,128)(2,1)S(1)}, u32[]{:S(2)}, u32[]{:S(2)}) collective-permute-start(bf16[512,128]{1,0:T(8,128)(2,1)S(1)} %collective-permute-done.4.refs_4_), channel_id=1, source_target_pairs={{0,8},{8,0},{16,24},{24,16},{1,9},{9,1},{17,25},{25,17},{2,10},{10... | collective-permute-start | bytes 393224 | tf_op jit(solution)/shard_map/ppermute | solution.py:249
  18.4 1.7 %collective-permute-start = (bf16[64,512]{1,0:T(8,128)(2,1)S(1)}, bf16[64,512]{1,0:T(8,128)(2,1)S(1)}, u32[]{:S(2)}, u32[]{:S(2)}) collective-permute-start(bf16[64,512]{1,0:T(8,128)(2,1)S(1)} %copy-done), channel_id=1, source_target_pairs={{0,8},{8,0},{16,24},{24,16},{1,9},{9,1},{17,25},{25,17},{2,10},{10... | collective-permute-start | bytes 196616 | tf_op jit(solution)/shard_map/ppermute | solution.py:249
  19.2 1.3 %collective-permute-start.2 = (bf16[64,512]{1,0:T(8,128)(2,1)S(1)}, bf16[64,512]{1,0:T(8,128)(2,1)S(1)}, u32[]{:S(2)}, u32[]{:S(2)}) collective-permute-start(bf16[64,512]{1,0:T(8,128)(2,1)S(1)} %collective-permute-done.1.refs_2_), channel_id=1, source_target_pairs={{0,8},{8,0},{16,24},{24,16},{1,9},{9,1},{17,25},{25,17},{2,10},{10... | collective-permute-start | bytes 196616 | tf_op jit(solution)/shard_map/ppermute | solution.py:249
  19.2 0.7 %copy-start.2 = (f32[64]{0:T(128)S(1)}, f32[64]{0:T(128)}, u32[]{:S(2)}) copy-start(f32[64]{0:T(128)} %param.6) | copy-start | bytes 772
  19.2 0.7 %copy-start.3 = (f32[32]{0:T(128)S(1)}, f32[32]{0:T(128)}, u32[]{:S(2)}) copy-start(f32[32]{0:T(128)} %param.7) | copy-start | bytes 388
